TPU v7x, 256 devices: a whole 4x4x8 slice. The times are simulated.
256 devices in a mesh: gx: 16 (over x_hi, z), gz: 16 (over x_lo, y, core).
Axes of the slice: x: 4 (x_hi: 2, x_lo: 2; x = x_hi * 2 + x_lo), y: 4, z: 8, core: 2. Of those that a mesh axis runs over, the one named last changes fastest.
Arguments:
- direct_modes: bfloat16 [3, 256, 1024, 128], P(None, 'gx', 'gz'), may hold values from -6 to 6
- adjoint_modes: bfloat16 [3, 256, 1024, 128], P(None, 'gx', 'gz'), may hold values from -0.0048828125 to 0.0048828125
- stencil_taps: float32 [36, 256, 1024], P(None, 'gx', 'gz'), may hold values from -0.72 to 0.72
- coupling: float32 [18, 256, 1024], P(None, 'gx', 'gz'), may hold values from -1.2 to 1.2
Outputs:
- evolved: bfloat16 [3, 256, 1024, 128], P(None, 'gx', 'gz')
- reduced: float32 [64, 64], P('gx')
All inputs are finite; a program needn't handle non-finite values.
Results may differ from a plain program's by a relative error of at most 0.0031.
Values sent between devices are 32-bit elements; how exact they have to be, the bound alone decides.
A program may use at most 64 MiB of HBM per device.

v0:
```python
import jax
import jax.numpy as jnp
from jax import lax
from jax.sharding import PartitionSpec as P

STEPS = 4


def with_halo(x, sides, width):
    for axis, dim in sides:
        peers, length = (lax.axis_size(axis), x.shape[dim])
        up = [(i, (i + 1) % peers) for i in range(peers)]
        down = [(j, i) for i, j in up]
        last = lax.slice_in_dim(x, length - width, length, axis=dim)
        leading = lax.slice_in_dim(x, 0, width, axis=dim)
        before = lax.ppermute(last, axis, up)
        after = lax.ppermute(leading, axis, down)
        x = jnp.concatenate([before, x, after], axis=dim)
    return x


def lane_weight(lower, first, second):
    return jnp.where(lower, first[:, :, None], second[:, :, None])


def advance(padded, tap_block, mix_block):
    width_x = padded.shape[1] - 2
    width_z = padded.shape[2] - 2
    lanes_all = padded.shape[3]
    half = lanes_all // 2
    lower = lax.broadcasted_iota(jnp.int32, (1, 1, lanes_all), 2) < half
    swapped = jnp.concatenate((padded[:, :, :, half:], padded[:, :, :, :half]), axis=3)
    own = padded[:, 1 : 1 + width_x, 1 : 1 + width_z, :]
    total = jnp.zeros((3, width_x, width_z, lanes_all), jnp.float32)
    for side_at in range(2):
        source = padded if side_at == 0 else swapped
        for tap_at in range(9):
            shift_x = tap_at // 3
            shift_z = tap_at % 3
            shifted = source[:, shift_x : shift_x + width_x, shift_z : shift_z + width_z, :]
            weight = lane_weight(
                lower, tap_block[side_at * 9 + tap_at], tap_block[18 + side_at * 9 + tap_at]
            )
            total = total + weight[None] * shifted
    mixed = []
    for comp_at in range(3):
        term = jnp.zeros((width_x, width_z, lanes_all), jnp.float32)
        for other_at in range(3):
            weight = lane_weight(
                lower, mix_block[comp_at * 3 + other_at], mix_block[9 + comp_at * 3 + other_at]
            )
            term = term + weight * own[other_at]
        mixed.append(term)
    return own + total + jnp.stack(mixed, axis=0)


def plane_product(adjoint_flat, evolved_flat):
    result = jnp.zeros((adjoint_flat.shape[2], evolved_flat.shape[2]), jnp.float32)
    for plane_at in range(2):
        result = result + lax.dot_general(
            adjoint_flat[:, plane_at, :],
            evolved_flat[:, plane_at, :],
            (((0,), (0,)), ((), ())),
            preferred_element_type=jnp.float32,
        )
    return result


def body(direct_modes, adjoint_modes, stencil_taps, coupling):
    state = direct_modes.astype(jnp.float32)
    modes = state.shape[3] // 2
    for step in range(STEPS):
        padded = with_halo(state, (("gx", 1), ("gz", 2)), 1)
        state = advance(padded, stencil_taps, coupling)
    evolved = state.astype(jnp.bfloat16)
    adjoint_flat = adjoint_modes.reshape(-1, 2, modes)
    evolved_flat = evolved.reshape(-1, 2, modes)
    partial_sum = plane_product(adjoint_flat, evolved_flat)
    spanned = lax.psum(partial_sum, "gz")
    reduced = lax.psum_scatter(spanned, "gx", scatter_dimension=0, tiled=True)
    return (evolved, reduced)


def solution(mesh):
    placed = (
        P(None, "gx", "gz", None),
        P(None, "gx", "gz", None),
        P(None, "gx", "gz"),
        P(None, "gx", "gz"),
    )
    return jax.shard_map(
        body,
        mesh=mesh,
        in_specs=placed,
        out_specs=(P(None, "gx", "gz", None), P("gx", None)),
        check_vma=False,
    )
```

profile of v0, /device:TPU:1, one launch (start us, length us, event | category | flops | bytes accessed | tf_op | source)
XLA Modules:
  0.0 265.6 jit_solution(13567518144057242414)
XLA Ops:
  0.6 1.6 fusion.176
  2.2 8.9 %collective-permute-start.1 = (f32[3,1,64,128]{3,2,1,0:T(8,128)}, f32[3,1,64,128]{3,2,1,0:T(8,128)S(1)}, u32[]{:S(2)}, u32[]{:S(2)}) collective-permute-start(f32[3,1,64,128]{3,2,1,0:T(8,128)} %get-tuple-element.51), channel_id=1, source_target_pairs={{16,0},{32,16},{48,32},{64,48},{80,64},{96,80},{112,96},{128,112},... | collective-permute-start | bytes 294920 | tf_op jit(solution)/shard_map/ppermute | solution.py:17
  11.1 1.3 convert_element_type.6
  13.8 3.2 %reshape.117 = bf16[3072,2,64]{2,1,0:T(2,128)(2,1)S(1)} reshape(bf16[3,16,64,128]{3,2,1,0:T(8,128)(2,1)} %param.5) | data formatting | bytes 1572864 | tf_op jit(solution)/shard_map/reshape | solution.py:76
  17.2 3.5 %fusion.172 = (bf16[3072,1,64]{2,1,0:T(2,128)(2,1)}, bf16[3072,1,64]{2,1,0:T(2,128)(2,1)}) fusion(bf16[3072,2,64]{2,1,0:T(2,128)(2,1)S(1)} %reshape.117), kind=kLoop, calls=%fused_computation.399 | loop fusion | bytes 1572864 | tf_op jit(solution)/shard_map/slice | solution.py:61
  20.9 3.9 %broadcast_select_fusion.8 = (f32[16,64,128]{2,1,0:T(8,128)S(1)}, f32[16,64,128]{2,1,0:T(8,128)S(1)}, f32[16,64,128]{2,1,0:T(8,128)S(1)}, f32[16,64,128]{2,1,0:T...) fusion(f32[16,64]{1,0:T(8,128)S(1)} %copy-done.47, ...), kind=kLoop, calls=%fused_computation.316 | loop fusion | flops 1179648 | bytes 4792448 | tf_op jit(solution)/shard_map/jit(_where)/select_n | solution.py:23
  24.9 4.1 %broadcast_select_fusion.17 = (f32[16,64,128]{2,1,0:T(8,128)}, f32[16,64,128]{2,1,0:T(8,128)}, f32[16,64,128]{2,1,0:T(8,128)}, f32[16,64,128]{2,1,0:T(8,128)}, f...) fusion(f32[16,64]{1,0:T(8,128)S(1)} %get-tuple-element.71, ...), kind=kLoop, calls=%fused_computation.325 | loop fusion | flops 1179648 | bytes 4792448 | tf_op jit(solution)/shard_map/jit(_where)/select_n | solution.py:23
  29.0 2.9 %fusion.139 = (f32[1,16,64,128]{3,2,1,0:T(8,128)}, f32[1,16,64,128]{3,2,1,0:T(8,128)}) fusion(f32[3,16,64,128]{3,2,1,0:T(8,128)S(1)} %convert_element_type.6, f32[16,64]{1,0:T(8,128)S(1)} %get-tuple-element.99, f32[16,64]{1,0:T(8,128)S(1)} %get-tuple-element.100, f32[16,64]{1,0:T(8,128)S(1)} %get-tuple-element.101, f32[16,64]{1,0:T(8,128)S(1)} %get-tuple-element.102, ...), kind=kLoop, calls=%fused_computation.280 | loop fusion | flops 2097152 | bytes 2670720 | tf_op jit(solution)/shard_map/add | solution.py:52
  34.7 1.7 fusion.155
  36.3 4.1 %copy.18 = bf16[3072,1,64]{0,2,1:T(8,128)(2,1)} copy(bf16[3072,1,64]{2,1,0:T(2,128)(2,1)} %get-tuple-element.43) | data formatting | bytes 786432
  40.5 4.1 %copy.20 = bf16[3072,1,64]{0,2,1:T(8,128)(2,1)} copy(bf16[3072,1,64]{2,1,0:T(2,128)(2,1)} %get-tuple-element.42) | data formatting | bytes 786432
  49.9 6.4 %fusion.106 = f32[3,16,64,128]{3,2,1,0:T(8,128)S(1)} fusion(f32[3,16,64,128]{3,2,1,0:T(8,128)S(1)} %convert_element_type.6, f32[3,18,66,64]{3,2,1,0:T(8,128)S(1)} %get-tuple-element.15, f32[3,18,66,64]{3,2,1,0:T(8,128)S(1)} %get-tuple-element.14, f32[3,18,65,128]{3,2,1,0:T(8,128)S(1)} %get-tuple-element.29, ...), kind=kLoop, calls=%fused_computation.188 | loop fusion | flops 19660800 | bytes 25614336 | tf_op jit(solution)/shard_map/add | solution.py:54
  56.4 5.6 %collective-permute-start.5 = (f32[3,1,64,128]{3,2,1,0:T(8,128)S(1)}, f32[3,1,64,128]{3,2,1,0:T(8,128)S(1)}, u32[]{:S(2)}, u32[]{:S(2)}) collective-permute-start(f32[3,1,64,128]{3,2,1,0:T(8,128)S(1)} %get-tuple-element.49), channel_id=1, source_target_pairs={{16,0},{32,16},{48,32},{64,48},{80,64},{96,80},{112,96},{128,112},... | collective-permute-start | bytes 294920 | tf_op jit(solution)/shard_map/ppermute | solution.py:17
  62.0 2.0 fusion.141
  64.0 5.1 %collective-permute-done.4 = f32[3,1,64,128]{3,2,1,0:T(8,128)S(1)} collective-permute-done((f32[3,1,64,128]{3,2,1,0:T(8,128)S(1)}, f32[3,1,64,128]{3,2,1,0:T(8,128)S(1)}, u32[]{:S(2)}, u32[]{:S(2)}) %collective-permute-start.4) | collective-permute-done | bytes 98336 | tf_op jit(solution)/shard_map/ppermute | solution.py:16
  69.1 2.9 %collective-permute-start.7 = (f32[3,18,1,128]{3,2,1,0:T(1,128)S(1)}, f32[3,18,1,128]{3,2,1,0:T(1,128)S(1)}, u32[]{:S(2)}, u32[]{:S(2)}) collective-permute-start(f32[3,18,1,128]{3,2,1,0:T(1,128)S(1)} %get-tuple-element.27), channel_id=1, source_target_pairs={{1,0},{2,1},{3,2},{4,3},{5,4},{6,5},{7,6},{8,7},{9,8},{10,9},{11,1... | collective-permute-start | bytes 82952 | tf_op jit(solution)/shard_map/ppermute | solution.py:17
  75.8 6.5 %fusion.72 = f32[3,16,64,128]{3,2,1,0:T(8,128)S(1)} fusion(f32[3,16,64,128]{3,2,1,0:T(8,128)S(1)} %fusion.106, f32[3,18,66,64]{3,2,1,0:T(8,128)S(1)} %get-tuple-element.13, f32[3,18,66,64]{3,2,1,0:T(8,128)S(1)} %get-tuple-element.12, f32[3,18,65,128]{3,2,1,0:T(8,128)S(1)} %get-tuple-element.25, f32[3,1,64,128]{3,2,1,0:T(8,128)S(1)} %collective-permute-done.5, ...), kind=kLoop, calls=%fused_computation.131 | loop fusion | flops 19660800 | bytes 25614336 | tf_op jit(solution)/shard_map/add | solution.py:54
  83.8 2.0 fusion.143
  85.8 4.2 %collective-permute-done.8 = f32[3,1,64,128]{3,2,1,0:T(8,128)S(1)} collective-permute-done((f32[3,1,64,128]{3,2,1,0:T(8,128)S(1)}, f32[3,1,64,128]{3,2,1,0:T(8,128)S(1)}, u32[]{:S(2)}, u32[]{:S(2)}) %collective-permute-start.8) | collective-permute-done | bytes 98336 | tf_op jit(solution)/shard_map/ppermute | solution.py:16
  90.1 6.2 %collective-permute-start.11 = (f32[3,18,1,128]{3,2,1,0:T(1,128)S(1)}, f32[3,18,1,128]{3,2,1,0:T(1,128)S(1)}, u32[]{:S(2)}, u32[]{:S(2)}) collective-permute-start(f32[3,18,1,128]{3,2,1,0:T(1,128)S(1)} %get-tuple-element.23), channel_id=1, source_target_pairs={{1,0},{2,1},{3,2},{4,3},{5,4},{6,5},{7,6},{8,7},{9,8},{10,9},{11,1... | collective-permute-start | bytes 82952 | tf_op jit(solution)/shard_map/ppermute | solution.py:17
  98.8 6.5 %fusion.38 = f32[3,16,64,128]{3,2,1,0:T(8,128)S(1)} fusion(f32[3,16,64,128]{3,2,1,0:T(8,128)S(1)} %fusion.72, f32[3,18,66,64]{3,2,1,0:T(8,128)S(1)} %get-tuple-element.11, f32[3,18,66,64]{3,2,1,0:T(8,128)S(1)} %get-tuple-element.10, f32[3,18,65,128]{3,2,1,0:T(8,128)S(1)} %get-tuple-element.21, f32[3,1,64,128]{3,2,1,0:T(8,128)S(1)} %collective-permute-done.9, ...), kind=kLoop, calls=%fused_computation.74 | loop fusion | flops 19660800 | bytes 25614336 | tf_op jit(solution)/shard_map/add | solution.py:54
  105.4 1.5 collective-permute-start.12
  106.9 2.0 fusion.145
  108.9 3.7 %collective-permute-done.12 = f32[3,1,64,128]{3,2,1,0:T(8,128)S(1)} collective-permute-done((f32[3,1,64,128]{3,2,1,0:T(8,128)S(1)}, f32[3,1,64,128]{3,2,1,0:T(8,128)S(1)}, u32[]{:S(2)}, u32[]{:S(2)}) %collective-permute-start.12) | collective-permute-done | bytes 98336 | tf_op jit(solution)/shard_map/ppermute | solution.py:16
  112.6 5.7 %collective-permute-start.15 = (f32[3,18,1,128]{3,2,1,0:T(1,128)S(1)}, f32[3,18,1,128]{3,2,1,0:T(1,128)S(1)}, u32[]{:S(2)}, u32[]{:S(2)}) collective-permute-start(f32[3,18,1,128]{3,2,1,0:T(1,128)S(1)} %get-tuple-element.19), channel_id=1, source_target_pairs={{1,0},{2,1},{3,2},{4,3},{5,4},{6,5},{7,6},{8,7},{9,8},{10,9},{11,1... | collective-permute-start | bytes 82952 | tf_op jit(solution)/shard_map/ppermute | solution.py:17
  120.8 7.3 %fusion.4 = bf16[3,16,64,128]{3,2,1,0:T(8,128)(2,1)} fusion(f32[3,16,64,128]{3,2,1,0:T(8,128)S(1)} %fusion.38, f32[3,18,66,64]{3,2,1,0:T(8,128)S(1)} %get-tuple-element.9, f32[3,18,66,64]{3,2,1,0:T(8,128)S(1)} %get-tuple-element.8, f32[3,18,65,128]{3,2,1,0:T(8,128)S(1)} %get-tuple-element.17, f32[3,1,64,128]{3,2,1,0:T(8,128)S(1)} %collective-permute-done.13, ...), kind=kLoop, calls=%fused_computation.17 | loop fusion | flops 20054016 | bytes 24827904 | tf_op jit(solution)/shard_map/convert_element_type | solution.py:75
  128.1 3.2 %reshape.116 = bf16[3072,2,64]{2,1,0:T(2,128)(2,1)S(1)} reshape(bf16[3,16,64,128]{3,2,1,0:T(8,128)(2,1)} %fusion.4) | data formatting | bytes 1572864 | tf_op jit(solution)/shard_map/reshape | solution.py:77
  131.3 3.1 %fusion.171 = (bf16[3072,1,64]{2,1,0:T(2,128)(2,1)S(1)}, bf16[3072,1,64]{2,1,0:T(2,128)(2,1)}) fusion(bf16[3072,2,64]{2,1,0:T(2,128)(2,1)S(1)} %reshape.116), kind=kLoop, calls=%fused_computation.398 | loop fusion | bytes 1572864 | tf_op jit(solution)/shard_map/slice | solution.py:62
  134.4 3.5 %copy.17 = bf16[3072,1,64]{0,2,1:T(8,128)(2,1)S(1)} copy(bf16[3072,1,64]{2,1,0:T(2,128)(2,1)} %get-tuple-element.41) | data formatting | bytes 786432
  137.9 1.5 copy.19
  140.0 58.0 %all-reduce = f32[64,64]{0,1:T(8,128)S(1)} all-reduce(f32[64,64]{0,1:T(8,128)S(1)} %fusion.137), channel_id=2, replica_groups=mesh['gx'=16,'gz'=16] {'gx'}, use_global_device_ids=true, to_apply=%region_1.2.clone | all-reduce | flops 4096 | bytes 32768
  198.0 66.9 %psum.8 = f32[4,64]{0,1:T(8,128)S(1)} all-reduce(f32[4,64]{0,1:T(8,128)S(1)} %constant_dynamic-slice_fusion), channel_id=1, replica_groups=mesh['gx'=16,'gz'=16] {'gz'}, use_global_device_ids=true, to_apply=%region_0.1 | all-reduce | flops 256 | bytes 2048 | tf_op jit(solution)/shard_map/psum | solution.py:79
  (158 shorter events, 20.7 us)
Async XLA Ops:
  0.6 11.7 %copy-start.20 = (f32[36,16,64]{2,1,0:T(8,128)S(1)}, f32[36,16,64]{2,1,0:T(8,128)}, u32[]{:S(2)}) copy-start(f32[36,16,64]{2,1,0:T(8,128)} %param.6) | copy-start | bytes 442372
  2.2 11.5 %copy-start.21 = (f32[18,16,64]{2,1,0:T(8,128)S(1)}, f32[18,16,64]{2,1,0:T(8,128)}, u32[]{:S(2)}) copy-start(f32[18,16,64]{2,1,0:T(8,128)} %param.7) | copy-start | bytes 221188
  2.2 29.7 %collective-permute-start.1 = (f32[3,1,64,128]{3,2,1,0:T(8,128)}, f32[3,1,64,128]{3,2,1,0:T(8,128)S(1)}, u32[]{:S(2)}, u32[]{:S(2)}) collective-permute-start(f32[3,1,64,128]{3,2,1,0:T(8,128)} %get-tuple-element.51), channel_id=1, source_target_pairs={{16,0},{32,16},{48,32},{64,48},{80,64},{96,80},{112,96},{128,112},... | collective-permute-start | bytes 294920 | tf_op jit(solution)/shard_map/ppermute | solution.py:17
  11.1 20.8 %collective-permute-start = (f32[3,1,64,128]{3,2,1,0:T(8,128)}, f32[3,1,64,128]{3,2,1,0:T(8,128)S(1)}, u32[]{:S(2)}, u32[]{:S(2)}) collective-permute-start(f32[3,1,64,128]{3,2,1,0:T(8,128)} %get-tuple-element.50), channel_id=1, source_target_pairs={{0,16},{16,32},{32,48},{48,64},{64,80},{80,96},{96,112},{112,128},... | collective-permute-start | bytes 294920 | tf_op jit(solution)/shard_map/ppermute | solution.py:16
  17.0 3.6 %copy-start.33 = (f32[16,64]{1,0:T(8,128)S(1)}, f32[16,64]{1,0:T(8,128)}, u32[]{:S(2)}) copy-start(f32[16,64]{1,0:T(8,128)} %get-tuple-element.53) | copy-start | bytes 12292
  20.8 4.0 %copy-start.22 = (f32[16,64]{1,0:T(8,128)S(1)}, f32[16,64]{1,0:T(8,128)}, u32[]{:S(2)}) copy-start(f32[16,64]{1,0:T(8,128)} %get-tuple-element.75) | copy-start | bytes 12292
  20.8 4.0 %copy-start.23 = (f32[16,64]{1,0:T(8,128)S(1)}, f32[16,64]{1,0:T(8,128)}, u32[]{:S(2)}) copy-start(f32[16,64]{1,0:T(8,128)} %get-tuple-element.76) | copy-start | bytes 12292
  20.8 4.0 %copy-start.24 = (f32[16,64]{1,0:T(8,128)S(1)}, f32[16,64]{1,0:T(8,128)}, u32[]{:S(2)}) copy-start(f32[16,64]{1,0:T(8,128)} %get-tuple-element.77) | copy-start | bytes 12292
  20.8 4.0 %copy-start.25 = (f32[16,64]{1,0:T(8,128)S(1)}, f32[16,64]{1,0:T(8,128)}, u32[]{:S(2)}) copy-start(f32[16,64]{1,0:T(8,128)} %get-tuple-element.78) | copy-start | bytes 12292
  20.8 4.0 %copy-start.26 = (f32[16,64]{1,0:T(8,128)S(1)}, f32[16,64]{1,0:T(8,128)}, u32[]{:S(2)}) copy-start(f32[16,64]{1,0:T(8,128)} %get-tuple-element.79) | copy-start | bytes 12292
  20.8 4.0 %copy-start.27 = (f32[16,64]{1,0:T(8,128)S(1)}, f32[16,64]{1,0:T(8,128)}, u32[]{:S(2)}) copy-start(f32[16,64]{1,0:T(8,128)} %get-tuple-element.80) | copy-start | bytes 12292
  20.9 4.0 %copy-start.28 = (f32[16,64]{1,0:T(8,128)S(1)}, f32[16,64]{1,0:T(8,128)}, u32[]{:S(2)}) copy-start(f32[16,64]{1,0:T(8,128)} %get-tuple-element.81) | copy-start | bytes 12292
  20.9 4.0 %copy-start.29 = (f32[16,64]{1,0:T(8,128)S(1)}, f32[16,64]{1,0:T(8,128)}, u32[]{:S(2)}) copy-start(f32[16,64]{1,0:T(8,128)} %get-tuple-element.82) | copy-start | bytes 12292
  20.9 4.0 %copy-start.30 = (f32[16,64]{1,0:T(8,128)S(1)}, f32[16,64]{1,0:T(8,128)}, u32[]{:S(2)}) copy-start(f32[16,64]{1,0:T(8,128)} %get-tuple-element.83) | copy-start | bytes 12292
  20.9 4.0 %copy-start.31 = (f32[16,64]{1,0:T(8,128)S(1)}, f32[16,64]{1,0:T(8,128)}, u32[]{:S(2)}) copy-start(f32[16,64]{1,0:T(8,128)} %get-tuple-element.84) | copy-start | bytes 12292
  20.9 4.0 %copy-start.32 = (f32[16,64]{1,0:T(8,128)S(1)}, f32[16,64]{1,0:T(8,128)}, u32[]{:S(2)}) copy-start(f32[16,64]{1,0:T(8,128)} %get-tuple-element.85) | copy-start | bytes 12292
  32.5 13.2 %collective-permute-start.3 = (f32[3,18,1,128]{3,2,1,0:T(1,128)}, f32[3,18,1,128]{3,2,1,0:T(1,128)S(1)}, u32[]{:S(2)}, u32[]{:S(2)}) collective-permute-start(f32[3,18,1,128]{3,2,1,0:T(1,128)} %get-tuple-element.31), channel_id=1, source_target_pairs={{1,0},{2,1},{3,2},{4,3},{5,4},{6,5},{7,6},{8,7},{9,8},{10,9},{11,1... | collective-permute-start | bytes 82952 | tf_op jit(solution)/shard_map/ppermute | solution.py:17
  33.5 12.3 %collective-permute-start.2 = (f32[3,18,1,128]{3,2,1,0:T(1,128)}, f32[3,18,1,128]{3,2,1,0:T(1,128)S(1)}, u32[]{:S(2)}, u32[]{:S(2)}) collective-permute-start(f32[3,18,1,128]{3,2,1,0:T(1,128)} %get-tuple-element.30), channel_id=1, source_target_pairs={{0,1},{1,2},{2,3},{3,4},{4,5},{5,6},{6,7},{7,8},{8,9},{9,10},{10,1... | collective-permute-start | bytes 82952 | tf_op jit(solution)/shard_map/ppermute | solution.py:16
  36.3 8.2 %copy-start.51 = (u32[256]{0:T(256)S(1)}, u32[256]{0:T(256)}, u32[]{:S(2)}) copy-start(u32[256]{0:T(256)} %constant.4) | copy-start | bytes 3076
  56.4 7.6 %collective-permute-start.5 = (f32[3,1,64,128]{3,2,1,0:T(8,128)S(1)}, f32[3,1,64,128]{3,2,1,0:T(8,128)S(1)}, u32[]{:S(2)}, u32[]{:S(2)}) collective-permute-start(f32[3,1,64,128]{3,2,1,0:T(8,128)S(1)} %get-tuple-element.49), channel_id=1, source_target_pairs={{16,0},{32,16},{48,32},{64,48},{80,64},{96,80},{112,96},{128,112},... | collective-permute-start | bytes 294920 | tf_op jit(solution)/shard_map/ppermute | solution.py:17
  62.0 7.1 %collective-permute-start.4 = (f32[3,1,64,128]{3,2,1,0:T(8,128)S(1)}, f32[3,1,64,128]{3,2,1,0:T(8,128)S(1)}, u32[]{:S(2)}, u32[]{:S(2)}) collective-permute-start(f32[3,1,64,128]{3,2,1,0:T(8,128)S(1)} %get-tuple-element.48), channel_id=1, source_target_pairs={{0,16},{16,32},{32,48},{48,64},{64,80},{80,96},{96,112},{112,128},... | collective-permute-start | bytes 294920 | tf_op jit(solution)/shard_map/ppermute | solution.py:16
  69.1 4.5 %collective-permute-start.7 = (f32[3,18,1,128]{3,2,1,0:T(1,128)S(1)}, f32[3,18,1,128]{3,2,1,0:T(1,128)S(1)}, u32[]{:S(2)}, u32[]{:S(2)}) collective-permute-start(f32[3,18,1,128]{3,2,1,0:T(1,128)S(1)} %get-tuple-element.27), channel_id=1, source_target_pairs={{1,0},{2,1},{3,2},{4,3},{5,4},{6,5},{7,6},{8,7},{9,8},{10,9},{11,1... | collective-permute-start | bytes 82952 | tf_op jit(solution)/shard_map/ppermute | solution.py:17
  72.0 2.5 collective-permute-start.6
  82.3 3.5 %collective-permute-start.9 = (f32[3,1,64,128]{3,2,1,0:T(8,128)S(1)}, f32[3,1,64,128]{3,2,1,0:T(8,128)S(1)}, u32[]{:S(2)}, u32[]{:S(2)}) collective-permute-start(f32[3,1,64,128]{3,2,1,0:T(8,128)S(1)} %get-tuple-element.47), channel_id=1, source_target_pairs={{16,0},{32,16},{48,32},{64,48},{80,64},{96,80},{112,96},{128,112},... | collective-permute-start | bytes 294920 | tf_op jit(solution)/shard_map/ppermute | solution.py:17
  83.0 7.1 %collective-permute-start.8 = (f32[3,1,64,128]{3,2,1,0:T(8,128)S(1)}, f32[3,1,64,128]{3,2,1,0:T(8,128)S(1)}, u32[]{:S(2)}, u32[]{:S(2)}) collective-permute-start(f32[3,1,64,128]{3,2,1,0:T(8,128)S(1)} %get-tuple-element.46), channel_id=1, source_target_pairs={{0,16},{16,32},{32,48},{48,64},{64,80},{80,96},{96,112},{112,128},... | collective-permute-start | bytes 294920 | tf_op jit(solution)/shard_map/ppermute | solution.py:16
  90.1 7.2 %collective-permute-start.11 = (f32[3,18,1,128]{3,2,1,0:T(1,128)S(1)}, f32[3,18,1,128]{3,2,1,0:T(1,128)S(1)}, u32[]{:S(2)}, u32[]{:S(2)}) collective-permute-start(f32[3,18,1,128]{3,2,1,0:T(1,128)S(1)} %get-tuple-element.23), channel_id=1, source_target_pairs={{1,0},{2,1},{3,2},{4,3},{5,4},{6,5},{7,6},{8,7},{9,8},{10,9},{11,1... | collective-permute-start | bytes 82952 | tf_op jit(solution)/shard_map/ppermute | solution.py:17
  96.3 1.2 collective-permute-start.10
  105.3 3.5 %collective-permute-start.13 = (f32[3,1,64,128]{3,2,1,0:T(8,128)S(1)}, f32[3,1,64,128]{3,2,1,0:T(8,128)S(1)}, u32[]{:S(2)}, u32[]{:S(2)}) collective-permute-start(f32[3,1,64,128]{3,2,1,0:T(8,128)S(1)} %get-tuple-element.45), channel_id=1, source_target_pairs={{16,0},{32,16},{48,32},{64,48},{80,64},{96,80},{112,96},{128,112},... | collective-permute-start | bytes 294920 | tf_op jit(solution)/shard_map/ppermute | solution.py:17
  105.4 7.2 %collective-permute-start.12 = (f32[3,1,64,128]{3,2,1,0:T(8,128)S(1)}, f32[3,1,64,128]{3,2,1,0:T(8,128)S(1)}, u32[]{:S(2)}, u32[]{:S(2)}) collective-permute-start(f32[3,1,64,128]{3,2,1,0:T(8,128)S(1)} %get-tuple-element.44), channel_id=1, source_target_pairs={{0,16},{16,32},{32,48},{48,64},{64,80},{80,96},{96,112},{112,128},... | collective-permute-start | bytes 294920 | tf_op jit(solution)/shard_map/ppermute | solution.py:16
  112.6 6.7 %collective-permute-start.15 = (f32[3,18,1,128]{3,2,1,0:T(1,128)S(1)}, f32[3,18,1,128]{3,2,1,0:T(1,128)S(1)}, u32[]{:S(2)}, u32[]{:S(2)}) collective-permute-start(f32[3,18,1,128]{3,2,1,0:T(1,128)S(1)} %get-tuple-element.19), channel_id=1, source_target_pairs={{1,0},{2,1},{3,2},{4,3},{5,4},{6,5},{7,6},{8,7},{9,8},{10,9},{11,1... | collective-permute-start | bytes 82952 | tf_op jit(solution)/shard_map/ppermute | solution.py:17
  118.3 1.2 collective-permute-start.14
  134.4 5.1 %copy-start.18 = (bf16[3072,1,64]{0,2,1:T(8,128)(2,1)S(1)}, bf16[3072,1,64]{0,2,1:T(8,128)(2,1)}, u32[]{:S(2)}) copy-start(bf16[3072,1,64]{0,2,1:T(8,128)(2,1)} %copy.18) | copy-start | bytes 1179652
  (36 other events, 99.7 us)
where the time goes:
time: 268 us; the launch traced here: 266 us
  blocking collectives  125 us (47%)
  other arithmetic  52.6 us (20%)
  local copies, waits for them, and re-layouts  35.8 us (13%)
  starting transfers between devices  34.7 us (13%)
  waiting for transfers between devices  14.8 us (6%)
    psum x1, blocking collectives, body(): spanned = lax.psum(partial_sum, 'gz')  66.9 us
    unnamed x1, blocking collectives  58 us
    ppermute x8, starting transfers between devices, with_halo(): after = lax.ppermute(leading, axis, down)  31 us
    add x3, other arithmetic, advance(): return own + total + jnp.stack(mixed, axis=0)  19.4 us
    unnamed x111, local copies, waits for them, and re-layouts  17.3 us
    ppermute x8, waiting for transfers between devices, with_halo(): before = lax.ppermute(last, axis, up)  14.3 us
    add x8, other arithmetic, advance(): term = term + weight * own[other_at]  13.3 us
    select_n x2, other arithmetic, lane_weight(): return jnp.where(lower, first[:, :, None], second[:, :, None])  7.98 us
  transfers between devices with their start and end apart: 16, of which 7 were waited for; matrix products, arithmetic and copies ran while one was open for 15% of the time, Pallas kernels for 0%

commit v1 on v0

--- a/solution.py
+++ b/solution.py
@@ -76,8 +76,9 @@
     adjoint_flat = adjoint_modes.reshape(-1, 2, modes)
     evolved_flat = evolved.reshape(-1, 2, modes)
     partial_sum = plane_product(adjoint_flat, evolved_flat)
-    spanned = lax.psum(partial_sum, "gz")
-    reduced = lax.psum_scatter(spanned, "gx", scatter_dimension=0, tiled=True)
+    total = lax.psum(partial_sum, ("gx", "gz"))
+    rows = total.shape[0] // lax.axis_size("gx")
+    reduced = lax.dynamic_slice_in_dim(total, lax.axis_index("gx") * rows, rows, axis=0)
     return (evolved, reduced)
 
 

time: 268 us -> 215 us (0.80)
  blocking collectives: 125 us -> 75.4 us
    unnamed x1 -> x0, blocking collectives: 58 us -> none
    psum x1, blocking collectives: 66.9 us -> 75.4 us  [body(): total = lax.psum(partial_sum, ('gx', 'gz'))]
    unnamed x111 -> x107, local copies, waits for them, and re-layouts: 17.3 us -> 16.7 us
  transfers between devices with their start and end apart: 16 -> 16, of which waited for: 7 -> 7; matrix products, arithmetic and copies ran while one was open for 15% -> 18% of each run, Pallas kernels for 0% -> 0%
where the time goes in v1:
time: 215 us
  blocking collectives  75.4 us (35%)
  other arithmetic  52.6 us (24%)
  local copies, waits for them, and re-layouts  35.2 us (16%)
  starting transfers between devices  34.7 us (16%)
  waiting for transfers between devices  14.8 us (7%)
    psum x1, blocking collectives, body(): total = lax.psum(partial_sum, ('gx', 'gz'))  75.4 us
    ppermute x8, starting transfers between devices, with_halo(): after = lax.ppermute(leading, axis, down)  31 us
    add x3, other arithmetic, advance(): return own + total + jnp.stack(mixed, axis=0)  19.4 us
    unnamed x107, local copies, waits for them, and re-layouts  16.7 us
    ppermute x8, waiting for transfers between devices, with_halo(): before = lax.ppermute(last, axis, up)  14.3 us
    add x8, other arithmetic, advance(): term = term + weight * own[other_at]  13.3 us
    select_n x2, other arithmetic, lane_weight(): return jnp.where(lower, first[:, :, None], second[:, :, None])  8.01 us
    convert_element_type x1, other arithmetic, body(): evolved = state.astype(jnp.bfloat16)  7.25 us
  transfers between devices with their start and end apart: 16, of which 7 were waited for; matrix products, arithmetic and copies ran while one was open for 18% of the time, Pallas kernels for 0%

profile of v1, /device:TPU:1, one launch (start us, length us, event | category | flops | bytes accessed | tf_op | source)
XLA Modules:
  0.0 214.8 jit_solution(7010674692382622125)
XLA Ops:
  0.6 1.6 fusion.176
  2.2 8.9 %collective-permute-start.1 = (f32[3,1,64,128]{3,2,1,0:T(8,128)}, f32[3,1,64,128]{3,2,1,0:T(8,128)S(1)}, u32[]{:S(2)}, u32[]{:S(2)}) collective-permute-start(f32[3,1,64,128]{3,2,1,0:T(8,128)} %get-tuple-element.49), channel_id=1, source_target_pairs={{16,0},{32,16},{48,32},{64,48},{80,64},{96,80},{112,96},{128,112},... | collective-permute-start | bytes 294920 | tf_op jit(solution)/shard_map/ppermute | solution.py:17
  11.1 1.3 convert_element_type.6
  13.8 3.2 %reshape.117 = bf16[3072,2,64]{2,1,0:T(2,128)(2,1)S(1)} reshape(bf16[3,16,64,128]{3,2,1,0:T(8,128)(2,1)} %param.5) | data formatting | bytes 1572864 | tf_op jit(solution)/shard_map/reshape | solution.py:76
  17.2 3.5 %fusion.172 = (bf16[3072,1,64]{2,1,0:T(2,128)(2,1)}, bf16[3072,1,64]{2,1,0:T(2,128)(2,1)}) fusion(bf16[3072,2,64]{2,1,0:T(2,128)(2,1)S(1)} %reshape.117), kind=kLoop, calls=%fused_computation.399 | loop fusion | bytes 1572864 | tf_op jit(solution)/shard_map/slice | solution.py:61
  20.9 3.9 %broadcast_select_fusion.8 = (f32[16,64,128]{2,1,0:T(8,128)S(1)}, f32[16,64,128]{2,1,0:T(8,128)S(1)}, f32[16,64,128]{2,1,0:T(8,128)S(1)}, f32[16,64,128]{2,1,0:T...) fusion(f32[16,64]{1,0:T(8,128)S(1)} %copy-done.47, ...), kind=kLoop, calls=%fused_computation.316 | loop fusion | flops 1179648 | bytes 4792448 | tf_op jit(solution)/shard_map/jit(_where)/select_n | solution.py:23
  24.9 4.1 %broadcast_select_fusion.17 = (f32[16,64,128]{2,1,0:T(8,128)}, f32[16,64,128]{2,1,0:T(8,128)}, f32[16,64,128]{2,1,0:T(8,128)}, f32[16,64,128]{2,1,0:T(8,128)}, f...) fusion(f32[16,64]{1,0:T(8,128)S(1)} %get-tuple-element.69, ...), kind=kLoop, calls=%fused_computation.325 | loop fusion | flops 1179648 | bytes 4792448 | tf_op jit(solution)/shard_map/jit(_where)/select_n | solution.py:23
  29.0 2.9 %fusion.139 = (f32[1,16,64,128]{3,2,1,0:T(8,128)}, f32[1,16,64,128]{3,2,1,0:T(8,128)}) fusion(f32[3,16,64,128]{3,2,1,0:T(8,128)S(1)} %convert_element_type.6, f32[16,64]{1,0:T(8,128)S(1)} %get-tuple-element.97, f32[16,64]{1,0:T(8,128)S(1)} %get-tuple-element.98, f32[16,64]{1,0:T(8,128)S(1)} %get-tuple-element.99, f32[16,64]{1,0:T(8,128)S(1)} %get-tuple-element.100, ...), kind=kLoop, calls=%fused_computation.280 | loop fusion | flops 2097152 | bytes 2670720 | tf_op jit(solution)/shard_map/add | solution.py:52
  33.5 1.2 collective-permute-start.2
  34.7 1.7 fusion.155
  36.3 4.1 %copy.13 = bf16[3072,1,64]{0,2,1:T(8,128)(2,1)} copy(bf16[3072,1,64]{2,1,0:T(2,128)(2,1)} %get-tuple-element.41) | data formatting | bytes 786432
  40.4 4.1 %copy.15 = bf16[3072,1,64]{0,2,1:T(8,128)(2,1)} copy(bf16[3072,1,64]{2,1,0:T(2,128)(2,1)} %get-tuple-element.40) | data formatting | bytes 786432
  48.7 6.4 %fusion.106 = f32[3,16,64,128]{3,2,1,0:T(8,128)S(1)} fusion(f32[3,16,64,128]{3,2,1,0:T(8,128)S(1)} %convert_element_type.6, f32[3,18,66,64]{3,2,1,0:T(8,128)S(1)} %get-tuple-element.13, f32[3,18,66,64]{3,2,1,0:T(8,128)S(1)} %get-tuple-element.12, f32[3,18,65,128]{3,2,1,0:T(8,128)S(1)} %get-tuple-element.27, ...), kind=kLoop, calls=%fused_computation.188 | loop fusion | flops 19660800 | bytes 25614336 | tf_op jit(solution)/shard_map/add | solution.py:54
  55.1 5.6 %collective-permute-start.5 = (f32[3,1,64,128]{3,2,1,0:T(8,128)S(1)}, f32[3,1,64,128]{3,2,1,0:T(8,128)S(1)}, u32[]{:S(2)}, u32[]{:S(2)}) collective-permute-start(f32[3,1,64,128]{3,2,1,0:T(8,128)S(1)} %get-tuple-element.47), channel_id=1, source_target_pairs={{16,0},{32,16},{48,32},{64,48},{80,64},{96,80},{112,96},{128,112},... | collective-permute-start | bytes 294920 | tf_op jit(solution)/shard_map/ppermute | solution.py:17
  60.7 2.0 fusion.141
  62.7 5.1 %collective-permute-done.4 = f32[3,1,64,128]{3,2,1,0:T(8,128)S(1)} collective-permute-done((f32[3,1,64,128]{3,2,1,0:T(8,128)S(1)}, f32[3,1,64,128]{3,2,1,0:T(8,128)S(1)}, u32[]{:S(2)}, u32[]{:S(2)}) %collective-permute-start.4) | collective-permute-done | bytes 98336 | tf_op jit(solution)/shard_map/ppermute | solution.py:16
  67.8 2.9 %collective-permute-start.7 = (f32[3,18,1,128]{3,2,1,0:T(1,128)S(1)}, f32[3,18,1,128]{3,2,1,0:T(1,128)S(1)}, u32[]{:S(2)}, u32[]{:S(2)}) collective-permute-start(f32[3,18,1,128]{3,2,1,0:T(1,128)S(1)} %get-tuple-element.25), channel_id=1, source_target_pairs={{1,0},{2,1},{3,2},{4,3},{5,4},{6,5},{7,6},{8,7},{9,8},{10,9},{11,1... | collective-permute-start | bytes 82952 | tf_op jit(solution)/shard_map/ppermute | solution.py:17
  74.5 6.5 %fusion.72 = f32[3,16,64,128]{3,2,1,0:T(8,128)S(1)} fusion(f32[3,16,64,128]{3,2,1,0:T(8,128)S(1)} %fusion.106, f32[3,18,66,64]{3,2,1,0:T(8,128)S(1)} %get-tuple-element.11, f32[3,18,66,64]{3,2,1,0:T(8,128)S(1)} %get-tuple-element.10, f32[3,18,65,128]{3,2,1,0:T(8,128)S(1)} %get-tuple-element.23, f32[3,1,64,128]{3,2,1,0:T(8,128)S(1)} %collective-permute-done.5, ...), kind=kLoop, calls=%fused_computation.131 | loop fusion | flops 19660800 | bytes 25614336 | tf_op jit(solution)/shard_map/add | solution.py:54
  82.6 2.0 fusion.143
  84.6 4.2 %collective-permute-done.8 = f32[3,1,64,128]{3,2,1,0:T(8,128)S(1)} collective-permute-done((f32[3,1,64,128]{3,2,1,0:T(8,128)S(1)}, f32[3,1,64,128]{3,2,1,0:T(8,128)S(1)}, u32[]{:S(2)}, u32[]{:S(2)}) %collective-permute-start.8) | collective-permute-done | bytes 98336 | tf_op jit(solution)/shard_map/ppermute | solution.py:16
  88.8 6.2 %collective-permute-start.11 = (f32[3,18,1,128]{3,2,1,0:T(1,128)S(1)}, f32[3,18,1,128]{3,2,1,0:T(1,128)S(1)}, u32[]{:S(2)}, u32[]{:S(2)}) collective-permute-start(f32[3,18,1,128]{3,2,1,0:T(1,128)S(1)} %get-tuple-element.21), channel_id=1, source_target_pairs={{1,0},{2,1},{3,2},{4,3},{5,4},{6,5},{7,6},{8,7},{9,8},{10,9},{11,1... | collective-permute-start | bytes 82952 | tf_op jit(solution)/shard_map/ppermute | solution.py:17
  97.5 6.5 %fusion.38 = f32[3,16,64,128]{3,2,1,0:T(8,128)S(1)} fusion(f32[3,16,64,128]{3,2,1,0:T(8,128)S(1)} %fusion.72, f32[3,18,66,64]{3,2,1,0:T(8,128)S(1)} %get-tuple-element.9, f32[3,18,66,64]{3,2,1,0:T(8,128)S(1)} %get-tuple-element.8, f32[3,18,65,128]{3,2,1,0:T(8,128)S(1)} %get-tuple-element.19, f32[3,1,64,128]{3,2,1,0:T(8,128)S(1)} %collective-permute-done.9, ...), kind=kLoop, calls=%fused_computation.74 | loop fusion | flops 19660800 | bytes 25614336 | tf_op jit(solution)/shard_map/add | solution.py:54
  104.1 1.5 collective-permute-start.12
  105.6 2.0 fusion.145
  107.6 3.7 %collective-permute-done.12 = f32[3,1,64,128]{3,2,1,0:T(8,128)S(1)} collective-permute-done((f32[3,1,64,128]{3,2,1,0:T(8,128)S(1)}, f32[3,1,64,128]{3,2,1,0:T(8,128)S(1)}, u32[]{:S(2)}, u32[]{:S(2)}) %collective-permute-start.12) | collective-permute-done | bytes 98336 | tf_op jit(solution)/shard_map/ppermute | solution.py:16
  111.3 5.7 %collective-permute-start.15 = (f32[3,18,1,128]{3,2,1,0:T(1,128)S(1)}, f32[3,18,1,128]{3,2,1,0:T(1,128)S(1)}, u32[]{:S(2)}, u32[]{:S(2)}) collective-permute-start(f32[3,18,1,128]{3,2,1,0:T(1,128)S(1)} %get-tuple-element.17), channel_id=1, source_target_pairs={{1,0},{2,1},{3,2},{4,3},{5,4},{6,5},{7,6},{8,7},{9,8},{10,9},{11,1... | collective-permute-start | bytes 82952 | tf_op jit(solution)/shard_map/ppermute | solution.py:17
  119.6 7.3 %fusion.4 = bf16[3,16,64,128]{3,2,1,0:T(8,128)(2,1)} fusion(f32[3,16,64,128]{3,2,1,0:T(8,128)S(1)} %fusion.38, f32[3,18,66,64]{3,2,1,0:T(8,128)S(1)} %get-tuple-element.7, f32[3,18,66,64]{3,2,1,0:T(8,128)S(1)} %get-tuple-element.6, f32[3,18,65,128]{3,2,1,0:T(8,128)S(1)} %get-tuple-element.15, f32[3,1,64,128]{3,2,1,0:T(8,128)S(1)} %collective-permute-done.13, ...), kind=kLoop, calls=%fused_computation.17 | loop fusion | flops 20054016 | bytes 24827904 | tf_op jit(solution)/shard_map/convert_element_type | solution.py:75
  126.8 3.2 %reshape.116 = bf16[3072,2,64]{2,1,0:T(2,128)(2,1)S(1)} reshape(bf16[3,16,64,128]{3,2,1,0:T(8,128)(2,1)} %fusion.4) | data formatting | bytes 1572864 | tf_op jit(solution)/shard_map/reshape | solution.py:77
  130.0 3.1 %fusion.171 = (bf16[3072,1,64]{2,1,0:T(2,128)(2,1)S(1)}, bf16[3072,1,64]{2,1,0:T(2,128)(2,1)}) fusion(bf16[3072,2,64]{2,1,0:T(2,128)(2,1)S(1)} %reshape.116), kind=kLoop, calls=%fused_computation.398 | loop fusion | bytes 1572864 | tf_op jit(solution)/shard_map/slice | solution.py:62
  133.1 3.5 %copy.12 = bf16[3072,1,64]{0,2,1:T(8,128)(2,1)S(1)} copy(bf16[3072,1,64]{2,1,0:T(2,128)(2,1)} %get-tuple-element.39) | data formatting | bytes 786432
  136.6 1.5 copy.14
  138.7 75.4 %psum.7 = f32[64,64]{0,1:T(8,128)S(1)} all-reduce(f32[64,64]{0,1:T(8,128)S(1)} %fusion.137), channel_id=1, replica_groups=mesh['gx'=16,'gz'=16] {'gx','gz'}, use_global_device_ids=true, to_apply=%region_0.1 | all-reduce | flops 4096 | bytes 32768 | tf_op jit(solution)/shard_map/psum | solution.py:79
  (154 shorter events, 18.9 us)
Async XLA Ops:
  0.6 11.7 %copy-start.20 = (f32[36,16,64]{2,1,0:T(8,128)S(1)}, f32[36,16,64]{2,1,0:T(8,128)}, u32[]{:S(2)}) copy-start(f32[36,16,64]{2,1,0:T(8,128)} %param.6) | copy-start | bytes 442372
  2.2 11.5 %copy-start.21 = (f32[18,16,64]{2,1,0:T(8,128)S(1)}, f32[18,16,64]{2,1,0:T(8,128)}, u32[]{:S(2)}) copy-start(f32[18,16,64]{2,1,0:T(8,128)} %param.7) | copy-start | bytes 221188
  2.2 29.7 %collective-permute-start.1 = (f32[3,1,64,128]{3,2,1,0:T(8,128)}, f32[3,1,64,128]{3,2,1,0:T(8,128)S(1)}, u32[]{:S(2)}, u32[]{:S(2)}) collective-permute-start(f32[3,1,64,128]{3,2,1,0:T(8,128)} %get-tuple-element.49), channel_id=1, source_target_pairs={{16,0},{32,16},{48,32},{64,48},{80,64},{96,80},{112,96},{128,112},... | collective-permute-start | bytes 294920 | tf_op jit(solution)/shard_map/ppermute | solution.py:17
  11.1 20.8 %collective-permute-start = (f32[3,1,64,128]{3,2,1,0:T(8,128)}, f32[3,1,64,128]{3,2,1,0:T(8,128)S(1)}, u32[]{:S(2)}, u32[]{:S(2)}) collective-permute-start(f32[3,1,64,128]{3,2,1,0:T(8,128)} %get-tuple-element.48), channel_id=1, source_target_pairs={{0,16},{16,32},{32,48},{48,64},{64,80},{80,96},{96,112},{112,128},... | collective-permute-start | bytes 294920 | tf_op jit(solution)/shard_map/ppermute | solution.py:16
  17.0 3.7 %copy-start.33 = (f32[16,64]{1,0:T(8,128)S(1)}, f32[16,64]{1,0:T(8,128)}, u32[]{:S(2)}) copy-start(f32[16,64]{1,0:T(8,128)} %get-tuple-element.51) | copy-start | bytes 12292
  17.0 3.6 %copy-start.34 = (f32[16,64]{1,0:T(8,128)S(1)}, f32[16,64]{1,0:T(8,128)}, u32[]{:S(2)}) copy-start(f32[16,64]{1,0:T(8,128)} %get-tuple-element.52) | copy-start | bytes 12292
  20.8 4.0 %copy-start.22 = (f32[16,64]{1,0:T(8,128)S(1)}, f32[16,64]{1,0:T(8,128)}, u32[]{:S(2)}) copy-start(f32[16,64]{1,0:T(8,128)} %get-tuple-element.73) | copy-start | bytes 12292
  20.8 4.0 %copy-start.23 = (f32[16,64]{1,0:T(8,128)S(1)}, f32[16,64]{1,0:T(8,128)}, u32[]{:S(2)}) copy-start(f32[16,64]{1,0:T(8,128)} %get-tuple-element.74) | copy-start | bytes 12292
  20.8 4.0 %copy-start.24 = (f32[16,64]{1,0:T(8,128)S(1)}, f32[16,64]{1,0:T(8,128)}, u32[]{:S(2)}) copy-start(f32[16,64]{1,0:T(8,128)} %get-tuple-element.75) | copy-start | bytes 12292
  20.8 4.0 %copy-start.25 = (f32[16,64]{1,0:T(8,128)S(1)}, f32[16,64]{1,0:T(8,128)}, u32[]{:S(2)}) copy-start(f32[16,64]{1,0:T(8,128)} %get-tuple-element.76) | copy-start | bytes 12292
  20.8 4.0 %copy-start.26 = (f32[16,64]{1,0:T(8,128)S(1)}, f32[16,64]{1,0:T(8,128)}, u32[]{:S(2)}) copy-start(f32[16,64]{1,0:T(8,128)} %get-tuple-element.77) | copy-start | bytes 12292
  20.8 4.0 %copy-start.27 = (f32[16,64]{1,0:T(8,128)S(1)}, f32[16,64]{1,0:T(8,128)}, u32[]{:S(2)}) copy-start(f32[16,64]{1,0:T(8,128)} %get-tuple-element.78) | copy-start | bytes 12292
  20.9 4.0 %copy-start.28 = (f32[16,64]{1,0:T(8,128)S(1)}, f32[16,64]{1,0:T(8,128)}, u32[]{:S(2)}) copy-start(f32[16,64]{1,0:T(8,128)} %get-tuple-element.79) | copy-start | bytes 12292
  20.9 4.0 %copy-start.29 = (f32[16,64]{1,0:T(8,128)S(1)}, f32[16,64]{1,0:T(8,128)}, u32[]{:S(2)}) copy-start(f32[16,64]{1,0:T(8,128)} %get-tuple-element.80) | copy-start | bytes 12292
  20.9 4.0 %copy-start.30 = (f32[16,64]{1,0:T(8,128)S(1)}, f32[16,64]{1,0:T(8,128)}, u32[]{:S(2)}) copy-start(f32[16,64]{1,0:T(8,128)} %get-tuple-element.81) | copy-start | bytes 12292
  20.9 4.0 %copy-start.31 = (f32[16,64]{1,0:T(8,128)S(1)}, f32[16,64]{1,0:T(8,128)}, u32[]{:S(2)}) copy-start(f32[16,64]{1,0:T(8,128)} %get-tuple-element.82) | copy-start | bytes 12292
  20.9 4.0 %copy-start.32 = (f32[16,64]{1,0:T(8,128)S(1)}, f32[16,64]{1,0:T(8,128)}, u32[]{:S(2)}) copy-start(f32[16,64]{1,0:T(8,128)} %get-tuple-element.83) | copy-start | bytes 12292
  32.5 12.0 %collective-permute-start.3 = (f32[3,18,1,128]{3,2,1,0:T(1,128)}, f32[3,18,1,128]{3,2,1,0:T(1,128)S(1)}, u32[]{:S(2)}, u32[]{:S(2)}) collective-permute-start(f32[3,18,1,128]{3,2,1,0:T(1,128)} %get-tuple-element.29), channel_id=1, source_target_pairs={{1,0},{2,1},{3,2},{4,3},{5,4},{6,5},{7,6},{8,7},{9,8},{10,9},{11,1... | collective-permute-start | bytes 82952 | tf_op jit(solution)/shard_map/ppermute | solution.py:17
  33.5 11.0 %collective-permute-start.2 = (f32[3,18,1,128]{3,2,1,0:T(1,128)}, f32[3,18,1,128]{3,2,1,0:T(1,128)S(1)}, u32[]{:S(2)}, u32[]{:S(2)}) collective-permute-start(f32[3,18,1,128]{3,2,1,0:T(1,128)} %get-tuple-element.28), channel_id=1, source_target_pairs={{0,1},{1,2},{2,3},{3,4},{4,5},{5,6},{6,7},{7,8},{8,9},{9,10},{10,1... | collective-permute-start | bytes 82952 | tf_op jit(solution)/shard_map/ppermute | solution.py:16
  55.1 7.6 %collective-permute-start.5 = (f32[3,1,64,128]{3,2,1,0:T(8,128)S(1)}, f32[3,1,64,128]{3,2,1,0:T(8,128)S(1)}, u32[]{:S(2)}, u32[]{:S(2)}) collective-permute-start(f32[3,1,64,128]{3,2,1,0:T(8,128)S(1)} %get-tuple-element.47), channel_id=1, source_target_pairs={{16,0},{32,16},{48,32},{64,48},{80,64},{96,80},{112,96},{128,112},... | collective-permute-start | bytes 294920 | tf_op jit(solution)/shard_map/ppermute | solution.py:17
  60.7 7.1 %collective-permute-start.4 = (f32[3,1,64,128]{3,2,1,0:T(8,128)S(1)}, f32[3,1,64,128]{3,2,1,0:T(8,128)S(1)}, u32[]{:S(2)}, u32[]{:S(2)}) collective-permute-start(f32[3,1,64,128]{3,2,1,0:T(8,128)S(1)} %get-tuple-element.46), channel_id=1, source_target_pairs={{0,16},{16,32},{32,48},{48,64},{64,80},{80,96},{96,112},{112,128},... | collective-permute-start | bytes 294920 | tf_op jit(solution)/shard_map/ppermute | solution.py:16
  67.8 4.5 %collective-permute-start.7 = (f32[3,18,1,128]{3,2,1,0:T(1,128)S(1)}, f32[3,18,1,128]{3,2,1,0:T(1,128)S(1)}, u32[]{:S(2)}, u32[]{:S(2)}) collective-permute-start(f32[3,18,1,128]{3,2,1,0:T(1,128)S(1)} %get-tuple-element.25), channel_id=1, source_target_pairs={{1,0},{2,1},{3,2},{4,3},{5,4},{6,5},{7,6},{8,7},{9,8},{10,9},{11,1... | collective-permute-start | bytes 82952 | tf_op jit(solution)/shard_map/ppermute | solution.py:17
  70.7 2.5 %collective-permute-start.6 = (f32[3,18,1,128]{3,2,1,0:T(1,128)S(1)}, f32[3,18,1,128]{3,2,1,0:T(1,128)S(1)}, u32[]{:S(2)}, u32[]{:S(2)}) collective-permute-start(f32[3,18,1,128]{3,2,1,0:T(1,128)S(1)} %get-tuple-element.24), channel_id=1, source_target_pairs={{0,1},{1,2},{2,3},{3,4},{4,5},{5,6},{6,7},{7,8},{8,9},{9,10},{10,1... | collective-permute-start | bytes 82952 | tf_op jit(solution)/shard_map/ppermute | solution.py:16
  81.0 3.5 %collective-permute-start.9 = (f32[3,1,64,128]{3,2,1,0:T(8,128)S(1)}, f32[3,1,64,128]{3,2,1,0:T(8,128)S(1)}, u32[]{:S(2)}, u32[]{:S(2)}) collective-permute-start(f32[3,1,64,128]{3,2,1,0:T(8,128)S(1)} %get-tuple-element.45), channel_id=1, source_target_pairs={{16,0},{32,16},{48,32},{64,48},{80,64},{96,80},{112,96},{128,112},... | collective-permute-start | bytes 294920 | tf_op jit(solution)/shard_map/ppermute | solution.py:17
  81.7 7.1 %collective-permute-start.8 = (f32[3,1,64,128]{3,2,1,0:T(8,128)S(1)}, f32[3,1,64,128]{3,2,1,0:T(8,128)S(1)}, u32[]{:S(2)}, u32[]{:S(2)}) collective-permute-start(f32[3,1,64,128]{3,2,1,0:T(8,128)S(1)} %get-tuple-element.44), channel_id=1, source_target_pairs={{0,16},{16,32},{32,48},{48,64},{64,80},{80,96},{96,112},{112,128},... | collective-permute-start | bytes 294920 | tf_op jit(solution)/shard_map/ppermute | solution.py:16
  88.8 7.2 %collective-permute-start.11 = (f32[3,18,1,128]{3,2,1,0:T(1,128)S(1)}, f32[3,18,1,128]{3,2,1,0:T(1,128)S(1)}, u32[]{:S(2)}, u32[]{:S(2)}) collective-permute-start(f32[3,18,1,128]{3,2,1,0:T(1,128)S(1)} %get-tuple-element.21), channel_id=1, source_target_pairs={{1,0},{2,1},{3,2},{4,3},{5,4},{6,5},{7,6},{8,7},{9,8},{10,9},{11,1... | collective-permute-start | bytes 82952 | tf_op jit(solution)/shard_map/ppermute | solution.py:17
  95.0 1.2 collective-permute-start.10
  104.0 3.5 %collective-permute-start.13 = (f32[3,1,64,128]{3,2,1,0:T(8,128)S(1)}, f32[3,1,64,128]{3,2,1,0:T(8,128)S(1)}, u32[]{:S(2)}, u32[]{:S(2)}) collective-permute-start(f32[3,1,64,128]{3,2,1,0:T(8,128)S(1)} %get-tuple-element.43), channel_id=1, source_target_pairs={{16,0},{32,16},{48,32},{64,48},{80,64},{96,80},{112,96},{128,112},... | collective-permute-start | bytes 294920 | tf_op jit(solution)/shard_map/ppermute | solution.py:17
  104.1 7.2 %collective-permute-start.12 = (f32[3,1,64,128]{3,2,1,0:T(8,128)S(1)}, f32[3,1,64,128]{3,2,1,0:T(8,128)S(1)}, u32[]{:S(2)}, u32[]{:S(2)}) collective-permute-start(f32[3,1,64,128]{3,2,1,0:T(8,128)S(1)} %get-tuple-element.42), channel_id=1, source_target_pairs={{0,16},{16,32},{32,48},{48,64},{64,80},{80,96},{96,112},{112,128},... | collective-permute-start | bytes 294920 | tf_op jit(solution)/shard_map/ppermute | solution.py:16
  111.3 6.7 %collective-permute-start.15 = (f32[3,18,1,128]{3,2,1,0:T(1,128)S(1)}, f32[3,18,1,128]{3,2,1,0:T(1,128)S(1)}, u32[]{:S(2)}, u32[]{:S(2)}) collective-permute-start(f32[3,18,1,128]{3,2,1,0:T(1,128)S(1)} %get-tuple-element.17), channel_id=1, source_target_pairs={{1,0},{2,1},{3,2},{4,3},{5,4},{6,5},{7,6},{8,7},{9,8},{10,9},{11,1... | collective-permute-start | bytes 82952 | tf_op jit(solution)/shard_map/ppermute | solution.py:17
  117.1 1.2 collective-permute-start.14
  133.1 5.1 %copy-start.18 = (bf16[3072,1,64]{0,2,1:T(8,128)(2,1)S(1)}, bf16[3072,1,64]{0,2,1:T(8,128)(2,1)}, u32[]{:S(2)}) copy-start(bf16[3072,1,64]{0,2,1:T(8,128)(2,1)} %copy.13) | copy-start | bytes 1179652
  (35 other events, 96.3 us)

commit v2 on v0

--- a/solution.py
+++ b/solution.py
@@ -1,7 +1,12 @@
 import jax
 import jax.numpy as jnp
 from jax import lax
+from jax.experimental import pallas as pl
+from jax.experimental.pallas import tpu as pltpu
 from jax.sharding import PartitionSpec as P
+import functools
+
+MESH = pl.DeviceIdType.MESH
 
 STEPS = 4
 
@@ -66,6 +71,75 @@
     return result
 
 
+def gather_phase(src, slots, send_sem, recv_sem, mine, peer_of, count):
+    slots[mine] = src[...]
+    outgoing = []
+    for k in range(1, count):
+        target = lax.rem(mine + k, count)
+        copy = pltpu.make_async_remote_copy(
+            src_ref=src,
+            dst_ref=slots.at[mine],
+            send_sem=send_sem.at[k],
+            recv_sem=recv_sem.at[mine],
+            device_id=peer_of(target),
+            device_id_type=MESH,
+        )
+        copy.start()
+        outgoing.append(copy)
+    for k in range(1, count):
+        source = lax.rem(mine + count - k, count)
+        incoming = pltpu.make_async_remote_copy(
+            src_ref=src,
+            dst_ref=slots.at[source],
+            send_sem=send_sem.at[k],
+            recv_sem=recv_sem.at[source],
+            device_id=peer_of(source),
+            device_id_type=MESH,
+        )
+        incoming.wait_recv()
+    total = slots[0]
+    for j in range(1, count):
+        total = total + slots[j]
+    return total, outgoing
+
+
+def allsum_kernel(nx, nz, part_ref, out_ref, mid, slots_z, slots_x, send_z, recv_z, send_x, recv_x):
+    a = lax.axis_index("gx")
+    g = lax.axis_index("gz")
+    barrier = pltpu.get_barrier_semaphore()
+    for k in range(1, nz):
+        pl.semaphore_signal(barrier, inc=1, device_id=(a, lax.rem(g + k, nz)), device_id_type=MESH)
+    for k in range(1, nx):
+        pl.semaphore_signal(barrier, inc=1, device_id=(lax.rem(a + k, nx), g), device_id_type=MESH)
+    pl.semaphore_wait(barrier, (nz - 1) + (nx - 1))
+    spanned, sent_z = gather_phase(part_ref, slots_z, send_z, recv_z, g, lambda t: (a, t), nz)
+    mid[...] = spanned
+    total, sent_x = gather_phase(mid, slots_x, send_x, recv_x, a, lambda t: (t, g), nx)
+    out_ref[...] = total
+    for copy in sent_z + sent_x:
+        copy.wait_send()
+
+
+def allsum(part, nx, nz):
+    shape = part.shape
+    return pl.pallas_call(
+        functools.partial(allsum_kernel, nx, nz),
+        out_shape=jax.ShapeDtypeStruct(shape, jnp.float32),
+        in_specs=[pl.BlockSpec(memory_space=pltpu.VMEM)],
+        out_specs=pl.BlockSpec(memory_space=pltpu.VMEM),
+        scratch_shapes=[
+            pltpu.VMEM(shape, jnp.float32),
+            pltpu.VMEM((nz,) + shape, jnp.float32),
+            pltpu.VMEM((nx,) + shape, jnp.float32),
+            pltpu.SemaphoreType.DMA((nz,)),
+            pltpu.SemaphoreType.DMA((nz,)),
+            pltpu.SemaphoreType.DMA((nx,)),
+            pltpu.SemaphoreType.DMA((nx,)),
+        ],
+        compiler_params=pltpu.CompilerParams(collective_id=0, has_side_effects=True),
+    )(part)
+
+
 def body(direct_modes, adjoint_modes, stencil_taps, coupling):
     state = direct_modes.astype(jnp.float32)
     modes = state.shape[3] // 2
@@ -76,9 +150,12 @@
     adjoint_flat = adjoint_modes.reshape(-1, 2, modes)
     evolved_flat = evolved.reshape(-1, 2, modes)
     partial_sum = plane_product(adjoint_flat, evolved_flat)
-    spanned = lax.psum(partial_sum, "gz")
-    reduced = lax.psum_scatter(spanned, "gx", scatter_dimension=0, tiled=True)
-    return (evolved, reduced)
+    nx, nz = lax.axis_size("gx"), lax.axis_size("gz")
+    rows = partial_sum.shape[0] // nx
+    dense = partial_sum.reshape(nx, rows * partial_sum.shape[1])
+    total = allsum(dense, nx, nz)
+    reduced = lax.dynamic_slice_in_dim(total, lax.axis_index("gx"), 1, axis=0)
+    return (evolved, reduced.reshape(rows, partial_sum.shape[1]))
 
 
 def solution(mesh):

time: 268 us -> 163 us (0.61)
  blocking collectives: 125 us -> 0 us
  Pallas kernels: 0 us -> 20.9 us
    psum x1 -> x0, blocking collectives: 66.9 us -> none  [body(): spanned = lax.psum(partial_sum, 'gz')]
    unnamed x1 -> x0, blocking collectives: 58 us -> none
    pallas_call x0 -> x1, Pallas kernels: none -> 20.9 us  [allsum(): pl.pallas_call(functools.partial(allsum_kernel, nx, nz), out_shape=jax.Sh...]
    unnamed x111 -> x106, local copies, waits for them, and re-layouts: 17.3 us -> 16 us
  transfers between devices with their start and end apart: 16 -> 16, of which waited for: 7 -> 7; matrix products, arithmetic and copies ran while one was open for 15% -> 24% of each run, Pallas kernels for 0% -> 0%
where the time goes in v2:
time: 163 us; the launch traced here: 162 us
  other arithmetic  52.6 us (32%)
  local copies, waits for them, and re-layouts  36.6 us (22%)
  starting transfers between devices  34.7 us (21%)
  Pallas kernels  20.9 us (13%)
  waiting for transfers between devices  14.8 us (9%)
    ppermute x8, starting transfers between devices, with_halo(): after = lax.ppermute(leading, axis, down)  31 us
    pallas_call x1, Pallas kernels, allsum(): pl.pallas_call(functools.partial(allsum_kernel, nx, nz), out_shape=jax.Sh...  20.9 us
    add x3, other arithmetic, advance(): return own + total + jnp.stack(mixed, axis=0)  19.4 us
    unnamed x106, local copies, waits for them, and re-layouts  16 us
    ppermute x8, waiting for transfers between devices, with_halo(): before = lax.ppermute(last, axis, up)  14.3 us
    add x8, other arithmetic, advance(): term = term + weight * own[other_at]  13.3 us
    select_n x2, other arithmetic, lane_weight(): return jnp.where(lower, first[:, :, None], second[:, :, None])  8.01 us
    convert_element_type x1, other arithmetic, body(): evolved = state.astype(jnp.bfloat16)  7.25 us
  transfers between devices with their start and end apart: 16, of which 7 were waited for; matrix products, arithmetic and copies ran while one was open for 24% of the time, Pallas kernels for 0%

profile of v2, /device:TPU:1, one launch (start us, length us, event | category | flops | bytes accessed | tf_op | source)
XLA Modules:
  0.0 161.7 jit_solution(13474618587656231204)
XLA Ops:
  0.6 1.6 fusion.176
  2.2 8.9 %collective-permute-start.1 = (f32[3,1,64,128]{3,2,1,0:T(8,128)}, f32[3,1,64,128]{3,2,1,0:T(8,128)S(1)}, u32[]{:S(2)}, u32[]{:S(2)}) collective-permute-start(f32[3,1,64,128]{3,2,1,0:T(8,128)} %get-tuple-element.45), channel_id=1, source_target_pairs={{16,0},{32,16},{48,32},{64,48},{80,64},{96,80},{112,96},{128,112},... | collective-permute-start | bytes 294920 | tf_op jit(solution)/shard_map/ppermute | solution.py:22
  11.1 1.3 convert_element_type.6
  13.8 3.2 %reshape.125 = bf16[3072,2,64]{2,1,0:T(2,128)(2,1)S(1)} reshape(bf16[3,16,64,128]{3,2,1,0:T(8,128)(2,1)} %param.5) | data formatting | bytes 1572864 | tf_op jit(solution)/shard_map/reshape | solution.py:150
  17.2 3.5 %fusion.172 = (bf16[3072,1,64]{2,1,0:T(2,128)(2,1)}, bf16[3072,1,64]{2,1,0:T(2,128)(2,1)}) fusion(bf16[3072,2,64]{2,1,0:T(2,128)(2,1)S(1)} %reshape.125), kind=kLoop, calls=%fused_computation.399 | loop fusion | bytes 1572864 | tf_op jit(solution)/shard_map/slice | solution.py:66
  20.9 3.9 %broadcast_select_fusion.8 = (f32[16,64,128]{2,1,0:T(8,128)S(1)}, f32[16,64,128]{2,1,0:T(8,128)S(1)}, f32[16,64,128]{2,1,0:T(8,128)S(1)}, f32[16,64,128]{2,1,0:T...) fusion(f32[16,64]{1,0:T(8,128)S(1)} %copy-done.47, ...), kind=kLoop, calls=%fused_computation.316 | loop fusion | flops 1179648 | bytes 4792448 | tf_op jit(solution)/shard_map/jit(_where)/select_n | solution.py:28
  24.9 4.1 %broadcast_select_fusion.17 = (f32[16,64,128]{2,1,0:T(8,128)}, f32[16,64,128]{2,1,0:T(8,128)}, f32[16,64,128]{2,1,0:T(8,128)}, f32[16,64,128]{2,1,0:T(8,128)}, f...) fusion(f32[16,64]{1,0:T(8,128)S(1)} %get-tuple-element.65, ...), kind=kLoop, calls=%fused_computation.325 | loop fusion | flops 1179648 | bytes 4792448 | tf_op jit(solution)/shard_map/jit(_where)/select_n | solution.py:28
  29.0 2.9 %fusion.139 = (f32[1,16,64,128]{3,2,1,0:T(8,128)}, f32[1,16,64,128]{3,2,1,0:T(8,128)}) fusion(f32[3,16,64,128]{3,2,1,0:T(8,128)S(1)} %convert_element_type.6, f32[16,64]{1,0:T(8,128)S(1)} %get-tuple-element.93, f32[16,64]{1,0:T(8,128)S(1)} %get-tuple-element.94, f32[16,64]{1,0:T(8,128)S(1)} %get-tuple-element.95, f32[16,64]{1,0:T(8,128)S(1)} %get-tuple-element.96, ...), kind=kLoop, calls=%fused_computation.280 | loop fusion | flops 2097152 | bytes 2670720 | tf_op jit(solution)/shard_map/add | solution.py:57
  33.5 1.2 collective-permute-start.2
  34.7 1.7 %fusion.155 = f32[1,16,64,128]{3,2,1,0:T(8,128)} fusion(f32[3,16,64,128]{3,2,1,0:T(8,128)S(1)} %convert_element_type.6, f32[16,64]{1,0:T(8,128)S(1)} %get-tuple-element.98, f32[16,64]{1,0:T(8,128)S(1)} %get-tuple-element.99, f32[16,64]{1,0:T(8,128)S(1)} %get-tuple-element.83, f32[16,64]{1,0:T(8,128)S(1)} %get-tuple-element.84, ...), kind=kLoop, calls=%fused_computation.296 | loop fusion | flops 1048576 | bytes 2121856 | tf_op jit(solution)/shard_map/add | solution.py:57
  36.3 4.1 %copy.13 = bf16[3072,1,64]{0,2,1:T(8,128)(2,1)} copy(bf16[3072,1,64]{2,1,0:T(2,128)(2,1)} %get-tuple-element.37) | data formatting | bytes 786432
  40.4 4.1 %copy.15 = bf16[3072,1,64]{0,2,1:T(8,128)(2,1)} copy(bf16[3072,1,64]{2,1,0:T(2,128)(2,1)} %get-tuple-element.36) | data formatting | bytes 786432
  48.7 6.4 %fusion.106 = f32[3,16,64,128]{3,2,1,0:T(8,128)S(1)} fusion(f32[3,16,64,128]{3,2,1,0:T(8,128)S(1)} %convert_element_type.6, f32[3,18,66,64]{3,2,1,0:T(8,128)S(1)} %get-tuple-element.9, f32[3,18,66,64]{3,2,1,0:T(8,128)S(1)} %get-tuple-element.8, f32[3,18,65,128]{3,2,1,0:T(8,128)S(1)} %get-tuple-element.23, f32[3,1,64,128]{3,2,1,0:T(8,128)S(1)} %collective-permute-done.1, ...), kind=kLoop, calls=%fused_computation.188 | loop fusion | flops 19660800 | bytes 25614336 | tf_op jit(solution)/shard_map/add | solution.py:59
  55.1 5.6 %collective-permute-start.5 = (f32[3,1,64,128]{3,2,1,0:T(8,128)S(1)}, f32[3,1,64,128]{3,2,1,0:T(8,128)S(1)}, u32[]{:S(2)}, u32[]{:S(2)}) collective-permute-start(f32[3,1,64,128]{3,2,1,0:T(8,128)S(1)} %get-tuple-element.43), channel_id=1, source_target_pairs={{16,0},{32,16},{48,32},{64,48},{80,64},{96,80},{112,96},{128,112},... | collective-permute-start | bytes 294920 | tf_op jit(solution)/shard_map/ppermute | solution.py:22
  60.7 2.0 %fusion.141 = (f32[1,16,64,128]{3,2,1,0:T(8,128)S(1)}, f32[1,16,64,128]{3,2,1,0:T(8,128)S(1)}) fusion(f32[3,16,64,128]{3,2,1,0:T(8,128)S(1)} %fusion.106, f32[16,64]{1,0:T(8,128)S(1)} %get-tuple-element.93, f32[16,64]{1,0:T(8,128)S(1)} %get-tuple-element.94, f32[16,64]{1,0:T(8,128)S(1)} %get-tuple-element.95, f32[16,64]{1,0:T(8,128)S(1)} %get-tuple-element.96, ...), kind=kLoop, calls=%fused_computation.282 | loop fusion | flops 2097152 | bytes 2670720 | tf_op jit(solution)/shard_map/add | solution.py:57
  62.7 5.1 %collective-permute-done.4 = f32[3,1,64,128]{3,2,1,0:T(8,128)S(1)} collective-permute-done((f32[3,1,64,128]{3,2,1,0:T(8,128)S(1)}, f32[3,1,64,128]{3,2,1,0:T(8,128)S(1)}, u32[]{:S(2)}, u32[]{:S(2)}) %collective-permute-start.4) | collective-permute-done | bytes 98336 | tf_op jit(solution)/shard_map/ppermute | solution.py:21
  67.8 2.9 %collective-permute-start.7 = (f32[3,18,1,128]{3,2,1,0:T(1,128)S(1)}, f32[3,18,1,128]{3,2,1,0:T(1,128)S(1)}, u32[]{:S(2)}, u32[]{:S(2)}) collective-permute-start(f32[3,18,1,128]{3,2,1,0:T(1,128)S(1)} %get-tuple-element.21), channel_id=1, source_target_pairs={{1,0},{2,1},{3,2},{4,3},{5,4},{6,5},{7,6},{8,7},{9,8},{10,9},{11,1... | collective-permute-start | bytes 82952 | tf_op jit(solution)/shard_map/ppermute | solution.py:22
  74.5 6.5 %fusion.72 = f32[3,16,64,128]{3,2,1,0:T(8,128)S(1)} fusion(f32[3,16,64,128]{3,2,1,0:T(8,128)S(1)} %fusion.106, f32[3,18,66,64]{3,2,1,0:T(8,128)S(1)} %get-tuple-element.7, f32[3,18,66,64]{3,2,1,0:T(8,128)S(1)} %get-tuple-element.6, f32[3,18,65,128]{3,2,1,0:T(8,128)S(1)} %get-tuple-element.19, f32[3,1,64,128]{3,2,1,0:T(8,128)S(1)} %collective-permute-done.5, ...), kind=kLoop, calls=%fused_computation.131 | loop fusion | flops 19660800 | bytes 25614336 | tf_op jit(solution)/shard_map/add | solution.py:59
  82.6 2.0 %fusion.143 = (f32[1,16,64,128]{3,2,1,0:T(8,128)S(1)}, f32[1,16,64,128]{3,2,1,0:T(8,128)S(1)}) fusion(f32[3,16,64,128]{3,2,1,0:T(8,128)S(1)} %fusion.72, f32[16,64]{1,0:T(8,128)S(1)} %get-tuple-element.93, f32[16,64]{1,0:T(8,128)S(1)} %get-tuple-element.94, f32[16,64]{1,0:T(8,128)S(1)} %get-tuple-element.95, f32[16,64]{1,0:T(8,128)S(1)} %get-tuple-element.96, ...), kind=kLoop, calls=%fused_computation.284 | loop fusion | flops 2097152 | bytes 2670720 | tf_op jit(solution)/shard_map/add | solution.py:57
  84.6 4.2 %collective-permute-done.8 = f32[3,1,64,128]{3,2,1,0:T(8,128)S(1)} collective-permute-done((f32[3,1,64,128]{3,2,1,0:T(8,128)S(1)}, f32[3,1,64,128]{3,2,1,0:T(8,128)S(1)}, u32[]{:S(2)}, u32[]{:S(2)}) %collective-permute-start.8) | collective-permute-done | bytes 98336 | tf_op jit(solution)/shard_map/ppermute | solution.py:21
  88.8 6.2 %collective-permute-start.11 = (f32[3,18,1,128]{3,2,1,0:T(1,128)S(1)}, f32[3,18,1,128]{3,2,1,0:T(1,128)S(1)}, u32[]{:S(2)}, u32[]{:S(2)}) collective-permute-start(f32[3,18,1,128]{3,2,1,0:T(1,128)S(1)} %get-tuple-element.17), channel_id=1, source_target_pairs={{1,0},{2,1},{3,2},{4,3},{5,4},{6,5},{7,6},{8,7},{9,8},{10,9},{11,1... | collective-permute-start | bytes 82952 | tf_op jit(solution)/shard_map/ppermute | solution.py:22
  97.5 6.5 %fusion.38 = f32[3,16,64,128]{3,2,1,0:T(8,128)S(1)} fusion(f32[3,16,64,128]{3,2,1,0:T(8,128)S(1)} %fusion.72, f32[3,18,66,64]{3,2,1,0:T(8,128)S(1)} %get-tuple-element.5, f32[3,18,66,64]{3,2,1,0:T(8,128)S(1)} %get-tuple-element.4, f32[3,18,65,128]{3,2,1,0:T(8,128)S(1)} %get-tuple-element.15, f32[3,1,64,128]{3,2,1,0:T(8,128)S(1)} %collective-permute-done.9, ...), kind=kLoop, calls=%fused_computation.74 | loop fusion | flops 19660800 | bytes 25614336 | tf_op jit(solution)/shard_map/add | solution.py:59
  104.1 1.5 collective-permute-start.12
  105.6 2.0 %fusion.145 = (f32[1,16,64,128]{3,2,1,0:T(8,128)S(1)}, f32[1,16,64,128]{3,2,1,0:T(8,128)S(1)}) fusion(f32[3,16,64,128]{3,2,1,0:T(8,128)S(1)} %fusion.38, f32[16,64]{1,0:T(8,128)S(1)} %get-tuple-element.93, f32[16,64]{1,0:T(8,128)S(1)} %get-tuple-element.94, f32[16,64]{1,0:T(8,128)S(1)} %get-tuple-element.95, f32[16,64]{1,0:T(8,128)S(1)} %get-tuple-element.96, ...), kind=kLoop, calls=%fused_computation.286 | loop fusion | flops 2097152 | bytes 2670720 | tf_op jit(solution)/shard_map/add | solution.py:57
  107.6 3.7 %collective-permute-done.12 = f32[3,1,64,128]{3,2,1,0:T(8,128)S(1)} collective-permute-done((f32[3,1,64,128]{3,2,1,0:T(8,128)S(1)}, f32[3,1,64,128]{3,2,1,0:T(8,128)S(1)}, u32[]{:S(2)}, u32[]{:S(2)}) %collective-permute-start.12) | collective-permute-done | bytes 98336 | tf_op jit(solution)/shard_map/ppermute | solution.py:21
  111.3 5.7 %collective-permute-start.15 = (f32[3,18,1,128]{3,2,1,0:T(1,128)S(1)}, f32[3,18,1,128]{3,2,1,0:T(1,128)S(1)}, u32[]{:S(2)}, u32[]{:S(2)}) collective-permute-start(f32[3,18,1,128]{3,2,1,0:T(1,128)S(1)} %get-tuple-element.13), channel_id=1, source_target_pairs={{1,0},{2,1},{3,2},{4,3},{5,4},{6,5},{7,6},{8,7},{9,8},{10,9},{11,1... | collective-permute-start | bytes 82952 | tf_op jit(solution)/shard_map/ppermute | solution.py:22
  119.6 7.3 %fusion.4 = bf16[3,16,64,128]{3,2,1,0:T(8,128)(2,1)} fusion(f32[3,16,64,128]{3,2,1,0:T(8,128)S(1)} %fusion.38, f32[3,18,66,64]{3,2,1,0:T(8,128)S(1)} %get-tuple-element.3, f32[3,18,66,64]{3,2,1,0:T(8,128)S(1)} %get-tuple-element.2, f32[3,18,65,128]{3,2,1,0:T(8,128)S(1)} %get-tuple-element.11, f32[3,1,64,128]{3,2,1,0:T(8,128)S(1)} %collective-permute-done.13, ...), kind=kLoop, calls=%fused_computation.17 | loop fusion | flops 20054016 | bytes 24827904 | tf_op jit(solution)/shard_map/convert_element_type | solution.py:149
  126.8 3.2 %reshape.124 = bf16[3072,2,64]{2,1,0:T(2,128)(2,1)S(1)} reshape(bf16[3,16,64,128]{3,2,1,0:T(8,128)(2,1)} %fusion.4) | data formatting | bytes 1572864 | tf_op jit(solution)/shard_map/reshape | solution.py:151
  130.0 3.1 %fusion.171 = (bf16[3072,1,64]{2,1,0:T(2,128)(2,1)S(1)}, bf16[3072,1,64]{2,1,0:T(2,128)(2,1)}) fusion(bf16[3072,2,64]{2,1,0:T(2,128)(2,1)S(1)} %reshape.124), kind=kLoop, calls=%fused_computation.398 | loop fusion | bytes 1572864 | tf_op jit(solution)/shard_map/slice | solution.py:67
  133.1 3.5 %copy.12 = bf16[3072,1,64]{0,2,1:T(8,128)(2,1)S(1)} copy(bf16[3072,1,64]{2,1,0:T(2,128)(2,1)} %get-tuple-element.35) | data formatting | bytes 786432
  136.6 1.5 copy.14
  139.4 20.9 %shard_map.59 = f32[16,256]{1,0:T(8,128)} custom-call(f32[16,256]{1,0:T(8,128)} %reshape.122.part_ref), custom_call_target="tpu_custom_call" | custom-call | tf_op jit(solution)/shard_map/pallas_call | solution.py:125
  (156 shorter events, 20.3 us)
Async XLA Ops:
  0.6 11.7 %copy-start.20 = (f32[36,16,64]{2,1,0:T(8,128)S(1)}, f32[36,16,64]{2,1,0:T(8,128)}, u32[]{:S(2)}) copy-start(f32[36,16,64]{2,1,0:T(8,128)} %param.6) | copy-start | bytes 442372
  2.2 11.5 %copy-start.21 = (f32[18,16,64]{2,1,0:T(8,128)S(1)}, f32[18,16,64]{2,1,0:T(8,128)}, u32[]{:S(2)}) copy-start(f32[18,16,64]{2,1,0:T(8,128)} %param.7) | copy-start | bytes 221188
  2.2 29.7 %collective-permute-start.1 = (f32[3,1,64,128]{3,2,1,0:T(8,128)}, f32[3,1,64,128]{3,2,1,0:T(8,128)S(1)}, u32[]{:S(2)}, u32[]{:S(2)}) collective-permute-start(f32[3,1,64,128]{3,2,1,0:T(8,128)} %get-tuple-element.45), channel_id=1, source_target_pairs={{16,0},{32,16},{48,32},{64,48},{80,64},{96,80},{112,96},{128,112},... | collective-permute-start | bytes 294920 | tf_op jit(solution)/shard_map/ppermute | solution.py:22
  11.1 20.8 %collective-permute-start = (f32[3,1,64,128]{3,2,1,0:T(8,128)}, f32[3,1,64,128]{3,2,1,0:T(8,128)S(1)}, u32[]{:S(2)}, u32[]{:S(2)}) collective-permute-start(f32[3,1,64,128]{3,2,1,0:T(8,128)} %get-tuple-element.44), channel_id=1, source_target_pairs={{0,16},{16,32},{32,48},{48,64},{64,80},{80,96},{96,112},{112,128},... | collective-permute-start | bytes 294920 | tf_op jit(solution)/shard_map/ppermute | solution.py:21
  17.0 3.7 %copy-start.33 = (f32[16,64]{1,0:T(8,128)S(1)}, f32[16,64]{1,0:T(8,128)}, u32[]{:S(2)}) copy-start(f32[16,64]{1,0:T(8,128)} %get-tuple-element.47) | copy-start | bytes 12292
  17.0 3.6 %copy-start.34 = (f32[16,64]{1,0:T(8,128)S(1)}, f32[16,64]{1,0:T(8,128)}, u32[]{:S(2)}) copy-start(f32[16,64]{1,0:T(8,128)} %get-tuple-element.48) | copy-start | bytes 12292
  20.8 4.0 %copy-start.22 = (f32[16,64]{1,0:T(8,128)S(1)}, f32[16,64]{1,0:T(8,128)}, u32[]{:S(2)}) copy-start(f32[16,64]{1,0:T(8,128)} %get-tuple-element.69) | copy-start | bytes 12292
  20.8 4.0 %copy-start.23 = (f32[16,64]{1,0:T(8,128)S(1)}, f32[16,64]{1,0:T(8,128)}, u32[]{:S(2)}) copy-start(f32[16,64]{1,0:T(8,128)} %get-tuple-element.70) | copy-start | bytes 12292
  20.8 4.0 %copy-start.24 = (f32[16,64]{1,0:T(8,128)S(1)}, f32[16,64]{1,0:T(8,128)}, u32[]{:S(2)}) copy-start(f32[16,64]{1,0:T(8,128)} %get-tuple-element.71) | copy-start | bytes 12292
  20.8 4.0 %copy-start.25 = (f32[16,64]{1,0:T(8,128)S(1)}, f32[16,64]{1,0:T(8,128)}, u32[]{:S(2)}) copy-start(f32[16,64]{1,0:T(8,128)} %get-tuple-element.72) | copy-start | bytes 12292
  20.8 4.0 %copy-start.26 = (f32[16,64]{1,0:T(8,128)S(1)}, f32[16,64]{1,0:T(8,128)}, u32[]{:S(2)}) copy-start(f32[16,64]{1,0:T(8,128)} %get-tuple-element.73) | copy-start | bytes 12292
  20.8 4.0 %copy-start.27 = (f32[16,64]{1,0:T(8,128)S(1)}, f32[16,64]{1,0:T(8,128)}, u32[]{:S(2)}) copy-start(f32[16,64]{1,0:T(8,128)} %get-tuple-element.74) | copy-start | bytes 12292
  20.9 4.0 %copy-start.28 = (f32[16,64]{1,0:T(8,128)S(1)}, f32[16,64]{1,0:T(8,128)}, u32[]{:S(2)}) copy-start(f32[16,64]{1,0:T(8,128)} %get-tuple-element.75) | copy-start | bytes 12292
  20.9 4.0 %copy-start.29 = (f32[16,64]{1,0:T(8,128)S(1)}, f32[16,64]{1,0:T(8,128)}, u32[]{:S(2)}) copy-start(f32[16,64]{1,0:T(8,128)} %get-tuple-element.76) | copy-start | bytes 12292
  20.9 4.0 %copy-start.30 = (f32[16,64]{1,0:T(8,128)S(1)}, f32[16,64]{1,0:T(8,128)}, u32[]{:S(2)}) copy-start(f32[16,64]{1,0:T(8,128)} %get-tuple-element.77) | copy-start | bytes 12292
  20.9 4.0 %copy-start.31 = (f32[16,64]{1,0:T(8,128)S(1)}, f32[16,64]{1,0:T(8,128)}, u32[]{:S(2)}) copy-start(f32[16,64]{1,0:T(8,128)} %get-tuple-element.78) | copy-start | bytes 12292
  20.9 4.0 %copy-start.32 = (f32[16,64]{1,0:T(8,128)S(1)}, f32[16,64]{1,0:T(8,128)}, u32[]{:S(2)}) copy-start(f32[16,64]{1,0:T(8,128)} %get-tuple-element.79) | copy-start | bytes 12292
  32.5 12.0 %collective-permute-start.3 = (f32[3,18,1,128]{3,2,1,0:T(1,128)}, f32[3,18,1,128]{3,2,1,0:T(1,128)S(1)}, u32[]{:S(2)}, u32[]{:S(2)}) collective-permute-start(f32[3,18,1,128]{3,2,1,0:T(1,128)} %get-tuple-element.25), channel_id=1, source_target_pairs={{1,0},{2,1},{3,2},{4,3},{5,4},{6,5},{7,6},{8,7},{9,8},{10,9},{11,1... | collective-permute-start | bytes 82952 | tf_op jit(solution)/shard_map/ppermute | solution.py:22
  33.5 11.0 %collective-permute-start.2 = (f32[3,18,1,128]{3,2,1,0:T(1,128)}, f32[3,18,1,128]{3,2,1,0:T(1,128)S(1)}, u32[]{:S(2)}, u32[]{:S(2)}) collective-permute-start(f32[3,18,1,128]{3,2,1,0:T(1,128)} %get-tuple-element.24), channel_id=1, source_target_pairs={{0,1},{1,2},{2,3},{3,4},{4,5},{5,6},{6,7},{7,8},{8,9},{9,10},{10,1... | collective-permute-start | bytes 82952 | tf_op jit(solution)/shard_map/ppermute | solution.py:21
  55.1 7.6 %collective-permute-start.5 = (f32[3,1,64,128]{3,2,1,0:T(8,128)S(1)}, f32[3,1,64,128]{3,2,1,0:T(8,128)S(1)}, u32[]{:S(2)}, u32[]{:S(2)}) collective-permute-start(f32[3,1,64,128]{3,2,1,0:T(8,128)S(1)} %get-tuple-element.43), channel_id=1, source_target_pairs={{16,0},{32,16},{48,32},{64,48},{80,64},{96,80},{112,96},{128,112},... | collective-permute-start | bytes 294920 | tf_op jit(solution)/shard_map/ppermute | solution.py:22
  60.7 7.1 %collective-permute-start.4 = (f32[3,1,64,128]{3,2,1,0:T(8,128)S(1)}, f32[3,1,64,128]{3,2,1,0:T(8,128)S(1)}, u32[]{:S(2)}, u32[]{:S(2)}) collective-permute-start(f32[3,1,64,128]{3,2,1,0:T(8,128)S(1)} %get-tuple-element.42), channel_id=1, source_target_pairs={{0,16},{16,32},{32,48},{48,64},{64,80},{80,96},{96,112},{112,128},... | collective-permute-start | bytes 294920 | tf_op jit(solution)/shard_map/ppermute | solution.py:21
  67.8 4.5 %collective-permute-start.7 = (f32[3,18,1,128]{3,2,1,0:T(1,128)S(1)}, f32[3,18,1,128]{3,2,1,0:T(1,128)S(1)}, u32[]{:S(2)}, u32[]{:S(2)}) collective-permute-start(f32[3,18,1,128]{3,2,1,0:T(1,128)S(1)} %get-tuple-element.21), channel_id=1, source_target_pairs={{1,0},{2,1},{3,2},{4,3},{5,4},{6,5},{7,6},{8,7},{9,8},{10,9},{11,1... | collective-permute-start | bytes 82952 | tf_op jit(solution)/shard_map/ppermute | solution.py:22
  70.7 2.5 %collective-permute-start.6 = (f32[3,18,1,128]{3,2,1,0:T(1,128)S(1)}, f32[3,18,1,128]{3,2,1,0:T(1,128)S(1)}, u32[]{:S(2)}, u32[]{:S(2)}) collective-permute-start(f32[3,18,1,128]{3,2,1,0:T(1,128)S(1)} %get-tuple-element.20), channel_id=1, source_target_pairs={{0,1},{1,2},{2,3},{3,4},{4,5},{5,6},{6,7},{7,8},{8,9},{9,10},{10,1... | collective-permute-start | bytes 82952 | tf_op jit(solution)/shard_map/ppermute | solution.py:21
  81.0 3.5 %collective-permute-start.9 = (f32[3,1,64,128]{3,2,1,0:T(8,128)S(1)}, f32[3,1,64,128]{3,2,1,0:T(8,128)S(1)}, u32[]{:S(2)}, u32[]{:S(2)}) collective-permute-start(f32[3,1,64,128]{3,2,1,0:T(8,128)S(1)} %get-tuple-element.41), channel_id=1, source_target_pairs={{16,0},{32,16},{48,32},{64,48},{80,64},{96,80},{112,96},{128,112},... | collective-permute-start | bytes 294920 | tf_op jit(solution)/shard_map/ppermute | solution.py:22
  81.7 7.1 %collective-permute-start.8 = (f32[3,1,64,128]{3,2,1,0:T(8,128)S(1)}, f32[3,1,64,128]{3,2,1,0:T(8,128)S(1)}, u32[]{:S(2)}, u32[]{:S(2)}) collective-permute-start(f32[3,1,64,128]{3,2,1,0:T(8,128)S(1)} %get-tuple-element.40), channel_id=1, source_target_pairs={{0,16},{16,32},{32,48},{48,64},{64,80},{80,96},{96,112},{112,128},... | collective-permute-start | bytes 294920 | tf_op jit(solution)/shard_map/ppermute | solution.py:21
  88.8 7.2 %collective-permute-start.11 = (f32[3,18,1,128]{3,2,1,0:T(1,128)S(1)}, f32[3,18,1,128]{3,2,1,0:T(1,128)S(1)}, u32[]{:S(2)}, u32[]{:S(2)}) collective-permute-start(f32[3,18,1,128]{3,2,1,0:T(1,128)S(1)} %get-tuple-element.17), channel_id=1, source_target_pairs={{1,0},{2,1},{3,2},{4,3},{5,4},{6,5},{7,6},{8,7},{9,8},{10,9},{11,1... | collective-permute-start | bytes 82952 | tf_op jit(solution)/shard_map/ppermute | solution.py:22
  95.0 1.2 collective-permute-start.10
  104.0 3.5 %collective-permute-start.13 = (f32[3,1,64,128]{3,2,1,0:T(8,128)S(1)}, f32[3,1,64,128]{3,2,1,0:T(8,128)S(1)}, u32[]{:S(2)}, u32[]{:S(2)}) collective-permute-start(f32[3,1,64,128]{3,2,1,0:T(8,128)S(1)} %get-tuple-element.39), channel_id=1, source_target_pairs={{16,0},{32,16},{48,32},{64,48},{80,64},{96,80},{112,96},{128,112},... | collective-permute-start | bytes 294920 | tf_op jit(solution)/shard_map/ppermute | solution.py:22
  104.1 7.2 %collective-permute-start.12 = (f32[3,1,64,128]{3,2,1,0:T(8,128)S(1)}, f32[3,1,64,128]{3,2,1,0:T(8,128)S(1)}, u32[]{:S(2)}, u32[]{:S(2)}) collective-permute-start(f32[3,1,64,128]{3,2,1,0:T(8,128)S(1)} %get-tuple-element.38), channel_id=1, source_target_pairs={{0,16},{16,32},{32,48},{48,64},{64,80},{80,96},{96,112},{112,128},... | collective-permute-start | bytes 294920 | tf_op jit(solution)/shard_map/ppermute | solution.py:21
  111.3 6.7 %collective-permute-start.15 = (f32[3,18,1,128]{3,2,1,0:T(1,128)S(1)}, f32[3,18,1,128]{3,2,1,0:T(1,128)S(1)}, u32[]{:S(2)}, u32[]{:S(2)}) collective-permute-start(f32[3,18,1,128]{3,2,1,0:T(1,128)S(1)} %get-tuple-element.13), channel_id=1, source_target_pairs={{1,0},{2,1},{3,2},{4,3},{5,4},{6,5},{7,6},{8,7},{9,8},{10,9},{11,1... | collective-permute-start | bytes 82952 | tf_op jit(solution)/shard_map/ppermute | solution.py:22
  117.1 1.2 collective-permute-start.14
  133.1 5.1 %copy-start.18 = (bf16[3072,1,64]{0,2,1:T(8,128)(2,1)S(1)}, bf16[3072,1,64]{0,2,1:T(8,128)(2,1)}, u32[]{:S(2)}) copy-start(bf16[3072,1,64]{0,2,1:T(8,128)(2,1)} %copy.13) | copy-start | bytes 1179652
  (35 other events, 96.3 us)

commit v3 on v2

--- a/solution.py
+++ b/solution.py
@@ -147,9 +147,14 @@
         padded = with_halo(state, (("gx", 1), ("gz", 2)), 1)
         state = advance(padded, stencil_taps, coupling)
     evolved = state.astype(jnp.bfloat16)
-    adjoint_flat = adjoint_modes.reshape(-1, 2, modes)
-    evolved_flat = evolved.reshape(-1, 2, modes)
-    partial_sum = plane_product(adjoint_flat, evolved_flat)
+    lanes_all = 2 * modes
+    square = lax.dot_general(
+        adjoint_modes.reshape(-1, lanes_all),
+        evolved.reshape(-1, lanes_all),
+        (((0,), (0,)), ((), ())),
+        preferred_element_type=jnp.float32,
+    )
+    partial_sum = square[:modes, :modes] + square[modes:, modes:]
     nx, nz = lax.axis_size("gx"), lax.axis_size("gz")
     rows = partial_sum.shape[0] // nx
     dense = partial_sum.reshape(nx, rows * partial_sum.shape[1])

time: 163 us -> 137 us (0.84)
  local copies, waits for them, and re-layouts: 36.6 us -> 8.13 us
  starting transfers between devices: 34.7 us -> 37.3 us
  other arithmetic: 52.6 us -> 54.4 us
    unnamed x106, local copies, waits for them, and re-layouts: 16 us -> 2.43 us
    slice x2 -> x0, local copies, waits for them, and re-layouts: 6.55 us -> none  [the longest x1 3.47 us: plane_product(): adjoint_flat[:, plane_at, :]]
    reshape x2 -> x0, local copies, waits for them, and re-layouts: 6.43 us -> none  [the longest x1 3.22 us: body(): adjoint_flat = adjoint_modes.reshape(-1, 2, modes)]
    ppermute x8, starting transfers between devices: 31 us -> 33.2 us  [with_halo(): after = lax.ppermute(leading, axis, down)]
    concatenate x8, other arithmetic: 2.57 us -> 4.72 us  [with_halo(): x = jnp.concatenate([before, x, after], axis=dim)]
  transfers between devices with their start and end apart: 16 -> 16, of which waited for: 7 -> 8; matrix products, arithmetic and copies ran while one was open for 24% -> 17% of each run, Pallas kernels for 0% -> 0%
where the time goes in v3:
time: 137 us; the launch traced here: 136 us
  other arithmetic  54.4 us (40%)
  starting transfers between devices  37.3 us (27%)
  Pallas kernels  20.6 us (15%)
  waiting for transfers between devices  13.7 us (10%)
  local copies, waits for them, and re-layouts  8.13 us (6%)
  between operations  1.59 us (1%)
    ppermute x8, starting transfers between devices, with_halo(): after = lax.ppermute(leading, axis, down)  33.2 us
    pallas_call x1, Pallas kernels, allsum(): pl.pallas_call(functools.partial(allsum_kernel, nx, nz), out_shape=jax.Sh...  20.6 us
    add x3, other arithmetic, advance(): return own + total + jnp.stack(mixed, axis=0)  19.4 us
    ppermute x8, waiting for transfers between devices, with_halo(): before = lax.ppermute(last, axis, up)  13.4 us
    add x8, other arithmetic, advance(): term = term + weight * own[other_at]  13.4 us
    select_n x2, other arithmetic, lane_weight(): return jnp.where(lower, first[:, :, None], second[:, :, None])  8.11 us
    convert_element_type x1, other arithmetic, body(): evolved = state.astype(jnp.bfloat16)  6.64 us
    concatenate x8, other arithmetic, with_halo(): x = jnp.concatenate([before, x, after], axis=dim)  4.72 us
  transfers between devices with their start and end apart: 16, of which 8 were waited for; matrix products, arithmetic and copies ran while one was open for 17% of the time, Pallas kernels for 0%

profile of v3, /device:TPU:1, one launch (start us, length us, event | category | flops | bytes accessed | tf_op | source)
XLA Modules:
  0.0 136.2 jit_solution(5405011260671562346)
XLA Ops:
  0.7 0.9 fusion.168
  1.6 8.9 %collective-permute-start.1 = (f32[3,1,64,128]{3,2,1,0:T(8,128)S(1)}, f32[3,1,64,128]{3,2,1,0:T(8,128)S(1)}, u32[]{:S(2)}, u32[]{:S(2)}) collective-permute-start(f32[3,1,64,128]{3,2,1,0:T(8,128)S(1)} %get-tuple-element.41), channel_id=1, source_target_pairs={{16,0},{32,16},{48,32},{64,48},{80,64},{96,80},{112,96},{128,112},... | collective-permute-start | bytes 294920 | tf_op jit(solution)/shard_map/ppermute | solution.py:22
  10.5 1.3 convert_element_type.6
  12.1 4.0 %broadcast_select_fusion.8 = (f32[16,64,128]{2,1,0:T(8,128)S(1)}, f32[16,64,128]{2,1,0:T(8,128)S(1)}, f32[16,64,128]{2,1,0:T(8,128)}, f32[16,64,128]{2,1,0:T(8,1...) fusion(f32[16,64]{1,0:T(8,128)S(1)} %get-tuple-element.57, ...), kind=kLoop, calls=%fused_computation.310 | loop fusion | flops 1179648 | bytes 4792448 | tf_op jit(solution)/shard_map/jit(_where)/select_n | solution.py:28
  16.1 4.1 %broadcast_select_fusion.17 = (f32[16,64,128]{2,1,0:T(8,128)}, f32[16,64,128]{2,1,0:T(8,128)}, f32[16,64,128]{2,1,0:T(8,128)}, f32[16,64,128]{2,1,0:T(8,128)}, f...) fusion(f32[16,64]{1,0:T(8,128)S(1)} %get-tuple-element.61, ...), kind=kLoop, calls=%fused_computation.319 | loop fusion | flops 1179648 | bytes 4792448 | tf_op jit(solution)/shard_map/jit(_where)/select_n | solution.py:28
  20.3 2.9 %fusion.138 = (f32[1,16,64,128]{3,2,1,0:T(8,128)}, f32[1,16,64,128]{3,2,1,0:T(8,128)}) fusion(f32[3,16,64,128]{3,2,1,0:T(8,128)S(1)} %convert_element_type.6, f32[16,64]{1,0:T(8,128)S(1)} %get-tuple-element.89, f32[16,64]{1,0:T(8,128)S(1)} %get-tuple-element.90, f32[16,64]{1,0:T(8,128)S(1)} %get-tuple-element.91, f32[16,64]{1,0:T(8,128)S(1)} %get-tuple-element.92, ...), kind=kLoop, calls=%fused_computation.279 | loop fusion | flops 2097152 | bytes 2670720 | tf_op jit(solution)/shard_map/add | solution.py:57
  24.5 1.0 collective-permute-start.3
  25.5 1.2 collective-permute-start.2
  26.6 1.7 %fusion.154 = f32[1,16,64,128]{3,2,1,0:T(8,128)} fusion(f32[3,16,64,128]{3,2,1,0:T(8,128)S(1)} %convert_element_type.6, f32[16,64]{1,0:T(8,128)S(1)} %get-tuple-element.94, f32[16,64]{1,0:T(8,128)S(1)} %get-tuple-element.95, f32[16,64]{1,0:T(8,128)S(1)} %get-tuple-element.79, f32[16,64]{1,0:T(8,128)S(1)} %get-tuple-element.80, ...), kind=kLoop, calls=%fused_computation.295 | loop fusion | flops 1048576 | bytes 2121856 | tf_op jit(solution)/shard_map/add | solution.py:57
  28.7 1.2 pad_maximum_fusion.1
  30.9 1.6 %maximum_maximum_fusion = (f32[3,18,65,128]{3,2,1,0:T(8,128)S(1)}, f32[3,18,65,128]{3,2,1,0:T(8,128)S(1)}) fusion(f32[3,1,64,128]{3,2,1,0:T(8,128)S(1)} %collective-permute-done.1, f32[3,16,64,128]{3,2,1,0:T(8,128)S(1)} %convert_element_type.6, f32[3,1,64,128]{3,2,1,0:T(8,128)S(1)} %copy-done.21, f32[3,18,1,128]{3,2,1,0:T(1,128)} %collective-permute-done.2, ...), kind=kLoop, calls=%fused_computation | loop fusion | flops 2695680 | bytes 5419008 | tf_op jit(solution)/shard_map/concatenate | solution.py:23
  34.1 6.5 %fusion.106 = f32[3,16,64,128]{3,2,1,0:T(8,128)S(1)} fusion(f32[3,16,64,128]{3,2,1,0:T(8,128)S(1)} %convert_element_type.6, f32[3,18,66,64]{3,2,1,0:T(8,128)S(1)} %get-tuple-element.9, f32[3,18,66,64]{3,2,1,0:T(8,128)S(1)} %get-tuple-element.8, f32[3,18,65,128]{3,2,1,0:T(8,128)S(1)} %get-tuple-element.23, f32[3,1,64,128]{3,2,1,0:T(8,128)S(1)} %collective-permute-done.1, ...), kind=kLoop, calls=%fused_computation.188 | loop fusion | flops 19660800 | bytes 25614336 | tf_op jit(solution)/shard_map/add | solution.py:59
  40.6 5.8 %collective-permute-start.5 = (f32[3,1,64,128]{3,2,1,0:T(8,128)S(1)}, f32[3,1,64,128]{3,2,1,0:T(8,128)S(1)}, u32[]{:S(2)}, u32[]{:S(2)}) collective-permute-start(f32[3,1,64,128]{3,2,1,0:T(8,128)S(1)} %get-tuple-element.39), channel_id=1, source_target_pairs={{16,0},{32,16},{48,32},{64,48},{80,64},{96,80},{112,96},{128,112},... | collective-permute-start | bytes 294920 | tf_op jit(solution)/shard_map/ppermute | solution.py:22
  46.5 2.0 %fusion.140 = (f32[1,16,64,128]{3,2,1,0:T(8,128)S(1)}, f32[1,16,64,128]{3,2,1,0:T(8,128)S(1)}) fusion(f32[3,16,64,128]{3,2,1,0:T(8,128)S(1)} %fusion.106, f32[16,64]{1,0:T(8,128)S(1)} %copy-done.39, f32[16,64]{1,0:T(8,128)S(1)} %copy-done.41, f32[16,64]{1,0:T(8,128)S(1)} %copy-done.43, f32[16,64]{1,0:T(8,128)S(1)} %copy-done.45, ...), kind=kLoop, calls=%fused_computation.281 | loop fusion | flops 2097152 | bytes 2670720 | tf_op jit(solution)/shard_map/add | solution.py:57
  48.5 5.0 %collective-permute-done.4 = f32[3,1,64,128]{3,2,1,0:T(8,128)S(1)} collective-permute-done((f32[3,1,64,128]{3,2,1,0:T(8,128)S(1)}, f32[3,1,64,128]{3,2,1,0:T(8,128)S(1)}, u32[]{:S(2)}, u32[]{:S(2)}) %collective-permute-start.4) | collective-permute-done | bytes 98336 | tf_op jit(solution)/shard_map/ppermute | solution.py:21
  53.5 6.4 %collective-permute-start.7 = (f32[3,18,1,128]{3,2,1,0:T(1,128)S(1)}, f32[3,18,1,128]{3,2,1,0:T(1,128)S(1)}, u32[]{:S(2)}, u32[]{:S(2)}) collective-permute-start(f32[3,18,1,128]{3,2,1,0:T(1,128)S(1)} %get-tuple-element.21), channel_id=1, source_target_pairs={{1,0},{2,1},{3,2},{4,3},{5,4},{6,5},{7,6},{8,7},{9,8},{10,9},{11,1... | collective-permute-start | bytes 82952 | tf_op jit(solution)/shard_map/ppermute | solution.py:22
  59.8 1.0 fusion.156
  62.4 6.5 %fusion.72 = f32[3,16,64,128]{3,2,1,0:T(8,128)S(1)} fusion(f32[3,16,64,128]{3,2,1,0:T(8,128)S(1)} %fusion.106, f32[3,18,66,64]{3,2,1,0:T(8,128)S(1)} %get-tuple-element.7, f32[3,18,66,64]{3,2,1,0:T(8,128)S(1)} %get-tuple-element.6, f32[3,18,65,128]{3,2,1,0:T(8,128)S(1)} %get-tuple-element.19, f32[3,1,64,128]{3,2,1,0:T(8,128)S(1)} %collective-permute-done.5, ...), kind=kLoop, calls=%fused_computation.131 | loop fusion | flops 19660800 | bytes 25614336 | tf_op jit(solution)/shard_map/add | solution.py:59
  68.9 1.5 %collective-permute-start.8 = (f32[3,1,64,128]{3,2,1,0:T(8,128)S(1)}, f32[3,1,64,128]{3,2,1,0:T(8,128)S(1)}, u32[]{:S(2)}, u32[]{:S(2)}) collective-permute-start(f32[3,1,64,128]{3,2,1,0:T(8,128)S(1)} %get-tuple-element.36), channel_id=1, source_target_pairs={{0,16},{16,32},{32,48},{48,64},{64,80},{80,96},{96,112},{112,128},... | collective-permute-start | bytes 294920 | tf_op jit(solution)/shard_map/ppermute | solution.py:21
  70.4 2.0 %fusion.142 = (f32[1,16,64,128]{3,2,1,0:T(8,128)S(1)}, f32[1,16,64,128]{3,2,1,0:T(8,128)S(1)}) fusion(f32[3,16,64,128]{3,2,1,0:T(8,128)S(1)} %fusion.72, f32[16,64]{1,0:T(8,128)S(1)} %copy-done.39, f32[16,64]{1,0:T(8,128)S(1)} %copy-done.41, f32[16,64]{1,0:T(8,128)S(1)} %copy-done.43, f32[16,64]{1,0:T(8,128)S(1)} %copy-done.46, f32[16,64]{1,0:T(8,128)S(1)} %copy-done.49, ...), kind=kLoop, calls=%fused_computation.283 | loop fusion | flops 2097152 | bytes 2670720 | tf_op jit(solution)/shard_map/add | solution.py:57
  72.4 3.7 %collective-permute-done.8 = f32[3,1,64,128]{3,2,1,0:T(8,128)S(1)} collective-permute-done((f32[3,1,64,128]{3,2,1,0:T(8,128)S(1)}, f32[3,1,64,128]{3,2,1,0:T(8,128)S(1)}, u32[]{:S(2)}, u32[]{:S(2)}) %collective-permute-start.8) | collective-permute-done | bytes 98336 | tf_op jit(solution)/shard_map/ppermute | solution.py:21
  76.2 5.5 %collective-permute-start.11 = (f32[3,18,1,128]{3,2,1,0:T(1,128)S(1)}, f32[3,18,1,128]{3,2,1,0:T(1,128)S(1)}, u32[]{:S(2)}, u32[]{:S(2)}) collective-permute-start(f32[3,18,1,128]{3,2,1,0:T(1,128)S(1)} %get-tuple-element.17), channel_id=1, source_target_pairs={{1,0},{2,1},{3,2},{4,3},{5,4},{6,5},{7,6},{8,7},{9,8},{10,9},{11,1... | collective-permute-start | bytes 82952 | tf_op jit(solution)/shard_map/ppermute | solution.py:22
  81.7 1.0 fusion.158
  84.2 6.5 %fusion.38 = f32[3,16,64,128]{3,2,1,0:T(8,128)S(1)} fusion(f32[3,16,64,128]{3,2,1,0:T(8,128)S(1)} %fusion.72, f32[3,18,66,64]{3,2,1,0:T(8,128)S(1)} %get-tuple-element.5, f32[3,18,66,64]{3,2,1,0:T(8,128)S(1)} %get-tuple-element.4, f32[3,18,65,128]{3,2,1,0:T(8,128)S(1)} %get-tuple-element.15, f32[3,1,64,128]{3,2,1,0:T(8,128)S(1)} %collective-permute-done.9, ...), kind=kLoop, calls=%fused_computation.74 | loop fusion | flops 19660800 | bytes 25614336 | tf_op jit(solution)/shard_map/add | solution.py:59
  90.8 1.5 %collective-permute-start.12 = (f32[3,1,64,128]{3,2,1,0:T(8,128)S(1)}, f32[3,1,64,128]{3,2,1,0:T(8,128)S(1)}, u32[]{:S(2)}, u32[]{:S(2)}) collective-permute-start(f32[3,1,64,128]{3,2,1,0:T(8,128)S(1)} %get-tuple-element.34), channel_id=1, source_target_pairs={{0,16},{16,32},{32,48},{48,64},{64,80},{80,96},{96,112},{112,128},... | collective-permute-start | bytes 294920 | tf_op jit(solution)/shard_map/ppermute | solution.py:21
  92.2 1.9 %fusion.144 = (f32[1,16,64,128]{3,2,1,0:T(8,128)S(1)}, f32[1,16,64,128]{3,2,1,0:T(8,128)S(1)}) fusion(f32[3,16,64,128]{3,2,1,0:T(8,128)S(1)} %fusion.38, f32[16,64]{1,0:T(8,128)S(1)} %copy-done.39, f32[16,64]{1,0:T(8,128)S(1)} %copy-done.41, f32[16,64]{1,0:T(8,128)S(1)} %copy-done.43, f32[16,64]{1,0:T(8,128)S(1)} %copy-done.46, f32[16,64]{1,0:T(8,128)S(1)} %copy-done.49, ...), kind=kLoop, calls=%fused_computation.285 | loop fusion | flops 2097152 | bytes 2670720 | tf_op jit(solution)/shard_map/add | solution.py:57
  94.2 3.9 %collective-permute-done.12 = f32[3,1,64,128]{3,2,1,0:T(8,128)S(1)} collective-permute-done((f32[3,1,64,128]{3,2,1,0:T(8,128)S(1)}, f32[3,1,64,128]{3,2,1,0:T(8,128)S(1)}, u32[]{:S(2)}, u32[]{:S(2)}) %collective-permute-start.12) | collective-permute-done | bytes 98336 | tf_op jit(solution)/shard_map/ppermute | solution.py:21
  98.2 5.5 %collective-permute-start.15 = (f32[3,18,1,128]{3,2,1,0:T(1,128)S(1)}, f32[3,18,1,128]{3,2,1,0:T(1,128)S(1)}, u32[]{:S(2)}, u32[]{:S(2)}) collective-permute-start(f32[3,18,1,128]{3,2,1,0:T(1,128)S(1)} %get-tuple-element.13), channel_id=1, source_target_pairs={{1,0},{2,1},{3,2},{4,3},{5,4},{6,5},{7,6},{8,7},{9,8},{10,9},{11,1... | collective-permute-start | bytes 82952 | tf_op jit(solution)/shard_map/ppermute | solution.py:22
  103.7 1.0 fusion.160
  106.2 6.6 %fusion.4 = bf16[3,16,64,128]{3,2,1,0:T(8,128)(2,1)S(1)} fusion(f32[3,16,64,128]{3,2,1,0:T(8,128)S(1)} %fusion.38, f32[3,18,66,64]{3,2,1,0:T(8,128)S(1)} %get-tuple-element.3, f32[3,18,66,64]{3,2,1,0:T(8,128)S(1)} %get-tuple-element.2, f32[3,18,65,128]{3,2,1,0:T(8,128)S(1)} %get-tuple-element.11, f32[3,1,64,128]{3,2,1,0:T(8,128)S(1)} %collective-permute-done.13, ...), kind=kLoop, calls=%fused_computation.17 | loop fusion | flops 20054016 | bytes 24827904 | tf_op jit(solution)/shard_map/convert_element_type | solution.py:149
  114.1 20.6 %shard_map.59 = f32[16,256]{1,0:T(8,128)} custom-call(f32[16,256]{1,0:T(8,128)} %reshape.116.part_ref), custom_call_target="tpu_custom_call" | custom-call | tf_op jit(solution)/shard_map/pallas_call | solution.py:125
  134.8 0.7 dynamic-slice_reduce_fusion
  (152 shorter events, 11.0 us)
Async XLA Ops:
  0.6 112.2 %copy-start = (bf16[3,16,64,128]{3,2,1,0:T(8,128)(2,1)S(1)}, bf16[3,16,64,128]{3,2,1,0:T(8,128)(2,1)}, u32[]{:S(2)}) copy-start(bf16[3,16,64,128]{3,2,1,0:T(8,128)(2,1)} %param.5) | copy-start | bytes 2359300
  1.6 21.6 %collective-permute-start.1 = (f32[3,1,64,128]{3,2,1,0:T(8,128)S(1)}, f32[3,1,64,128]{3,2,1,0:T(8,128)S(1)}, u32[]{:S(2)}, u32[]{:S(2)}) collective-permute-start(f32[3,1,64,128]{3,2,1,0:T(8,128)S(1)} %get-tuple-element.41), channel_id=1, source_target_pairs={{16,0},{32,16},{48,32},{64,48},{80,64},{96,80},{112,96},{128,112},... | collective-permute-start | bytes 294920 | tf_op jit(solution)/shard_map/ppermute | solution.py:22
  10.5 12.7 %collective-permute-start = (f32[3,1,64,128]{3,2,1,0:T(8,128)S(1)}, f32[3,1,64,128]{3,2,1,0:T(8,128)S(1)}, u32[]{:S(2)}, u32[]{:S(2)}) collective-permute-start(f32[3,1,64,128]{3,2,1,0:T(8,128)S(1)} %get-tuple-element.40), channel_id=1, source_target_pairs={{0,16},{16,32},{32,48},{48,64},{64,80},{80,96},{96,112},{112,128},... | collective-permute-start | bytes 294920 | tf_op jit(solution)/shard_map/ppermute | solution.py:21
  11.9 14.8 %copy-start.51 = (pred[128]{0:T(512)(128)(4,1)}, pred[128]{0:T(512)(128)(4,1)S(1)}, u32[]{:S(2)}) copy-start(pred[128]{0:T(512)(128)(4,1)S(1)} %iota_compare_fusion) | copy-start | bytes 388
  24.5 4.0 %collective-permute-start.3 = (f32[3,18,1,128]{3,2,1,0:T(1,128)}, f32[3,18,1,128]{3,2,1,0:T(1,128)}, u32[]{:S(2)}, u32[]{:S(2)}) collective-permute-start(f32[3,18,1,128]{3,2,1,0:T(1,128)} %get-tuple-element.25), channel_id=1, source_target_pairs={{1,0},{2,1},{3,2},{4,3},{5,4},{6,5},{7,6},{8,7},{9,8},{10,9},{11,1... | collective-permute-start | bytes 82952 | tf_op jit(solution)/shard_map/ppermute | solution.py:22
  25.5 3.2 %collective-permute-start.2 = (f32[3,18,1,128]{3,2,1,0:T(1,128)}, f32[3,18,1,128]{3,2,1,0:T(1,128)}, u32[]{:S(2)}, u32[]{:S(2)}) collective-permute-start(f32[3,18,1,128]{3,2,1,0:T(1,128)} %get-tuple-element.24), channel_id=1, source_target_pairs={{0,1},{1,2},{2,3},{3,4},{4,5},{5,6},{6,7},{7,8},{8,9},{9,10},{10,1... | collective-permute-start | bytes 82952 | tf_op jit(solution)/shard_map/ppermute | solution.py:21
  34.0 12.4 %copy-start.25 = (f32[16,64]{1,0:T(8,128)S(1)}, f32[16,64]{1,0:T(8,128)}, u32[]{:S(2)}) copy-start(f32[16,64]{1,0:T(8,128)} %copy-done.24) | copy-start | bytes 12292
  34.0 12.4 %copy-start.27 = (f32[16,64]{1,0:T(8,128)S(1)}, f32[16,64]{1,0:T(8,128)}, u32[]{:S(2)}) copy-start(f32[16,64]{1,0:T(8,128)} %copy-done.26) | copy-start | bytes 12292
  34.0 12.4 %copy-start.29 = (f32[16,64]{1,0:T(8,128)S(1)}, f32[16,64]{1,0:T(8,128)}, u32[]{:S(2)}) copy-start(f32[16,64]{1,0:T(8,128)} %copy-done.28) | copy-start | bytes 12292
  34.0 12.4 %copy-start.31 = (f32[16,64]{1,0:T(8,128)S(1)}, f32[16,64]{1,0:T(8,128)}, u32[]{:S(2)}) copy-start(f32[16,64]{1,0:T(8,128)} %copy-done.30) | copy-start | bytes 12292
  34.0 12.4 %copy-start.33 = (f32[16,64]{1,0:T(8,128)S(1)}, f32[16,64]{1,0:T(8,128)}, u32[]{:S(2)}) copy-start(f32[16,64]{1,0:T(8,128)} %copy-done.32) | copy-start | bytes 12292
  34.0 12.4 %copy-start.35 = (f32[16,64]{1,0:T(8,128)S(1)}, f32[16,64]{1,0:T(8,128)}, u32[]{:S(2)}) copy-start(f32[16,64]{1,0:T(8,128)} %copy-done.34) | copy-start | bytes 12292
  34.0 12.4 %copy-start.37 = (f32[16,64]{1,0:T(8,128)S(1)}, f32[16,64]{1,0:T(8,128)}, u32[]{:S(2)}) copy-start(f32[16,64]{1,0:T(8,128)} %copy-done.36) | copy-start | bytes 12292
  34.0 12.4 %copy-start.39 = (f32[16,64]{1,0:T(8,128)S(1)}, f32[16,64]{1,0:T(8,128)}, u32[]{:S(2)}) copy-start(f32[16,64]{1,0:T(8,128)} %copy-done.38) | copy-start | bytes 12292
  34.0 12.4 %copy-start.41 = (f32[16,64]{1,0:T(8,128)S(1)}, f32[16,64]{1,0:T(8,128)}, u32[]{:S(2)}) copy-start(f32[16,64]{1,0:T(8,128)} %copy-done.40) | copy-start | bytes 12292
  34.1 12.4 %copy-start.43 = (f32[16,64]{1,0:T(8,128)S(1)}, f32[16,64]{1,0:T(8,128)}, u32[]{:S(2)}) copy-start(f32[16,64]{1,0:T(8,128)} %copy-done.42) | copy-start | bytes 12292
  34.1 12.4 %copy-start.45 = (f32[16,64]{1,0:T(8,128)S(1)}, f32[16,64]{1,0:T(8,128)}, u32[]{:S(2)}) copy-start(f32[16,64]{1,0:T(8,128)} %copy-done.44) | copy-start | bytes 12292
  34.1 12.4 %copy-start.48 = (f32[16,64]{1,0:T(8,128)S(1)}, f32[16,64]{1,0:T(8,128)}, u32[]{:S(2)}) copy-start(f32[16,64]{1,0:T(8,128)} %copy-done.47) | copy-start | bytes 12292
  34.1 12.4 %copy-start.52 = (pred[128]{0:T(512)(128)(4,1)S(1)}, pred[128]{0:T(512)(128)(4,1)}, u32[]{:S(2)}) copy-start(pred[128]{0:T(512)(128)(4,1)} %copy-done.51) | copy-start | bytes 388
  40.6 7.9 %collective-permute-start.5 = (f32[3,1,64,128]{3,2,1,0:T(8,128)S(1)}, f32[3,1,64,128]{3,2,1,0:T(8,128)S(1)}, u32[]{:S(2)}, u32[]{:S(2)}) collective-permute-start(f32[3,1,64,128]{3,2,1,0:T(8,128)S(1)} %get-tuple-element.39), channel_id=1, source_target_pairs={{16,0},{32,16},{48,32},{64,48},{80,64},{96,80},{112,96},{128,112},... | collective-permute-start | bytes 294920 | tf_op jit(solution)/shard_map/ppermute | solution.py:22
  46.3 7.1 %collective-permute-start.4 = (f32[3,1,64,128]{3,2,1,0:T(8,128)S(1)}, f32[3,1,64,128]{3,2,1,0:T(8,128)S(1)}, u32[]{:S(2)}, u32[]{:S(2)}) collective-permute-start(f32[3,1,64,128]{3,2,1,0:T(8,128)S(1)} %get-tuple-element.38), channel_id=1, source_target_pairs={{0,16},{16,32},{32,48},{48,64},{64,80},{80,96},{96,112},{112,128},... | collective-permute-start | bytes 294920 | tf_op jit(solution)/shard_map/ppermute | solution.py:21
  53.5 7.3 %collective-permute-start.7 = (f32[3,18,1,128]{3,2,1,0:T(1,128)S(1)}, f32[3,18,1,128]{3,2,1,0:T(1,128)S(1)}, u32[]{:S(2)}, u32[]{:S(2)}) collective-permute-start(f32[3,18,1,128]{3,2,1,0:T(1,128)S(1)} %get-tuple-element.21), channel_id=1, source_target_pairs={{1,0},{2,1},{3,2},{4,3},{5,4},{6,5},{7,6},{8,7},{9,8},{10,9},{11,1... | collective-permute-start | bytes 82952 | tf_op jit(solution)/shard_map/ppermute | solution.py:22
  59.8 1.2 collective-permute-start.6
  68.9 3.5 %collective-permute-start.9 = (f32[3,1,64,128]{3,2,1,0:T(8,128)S(1)}, f32[3,1,64,128]{3,2,1,0:T(8,128)S(1)}, u32[]{:S(2)}, u32[]{:S(2)}) collective-permute-start(f32[3,1,64,128]{3,2,1,0:T(8,128)S(1)} %get-tuple-element.37), channel_id=1, source_target_pairs={{16,0},{32,16},{48,32},{64,48},{80,64},{96,80},{112,96},{128,112},... | collective-permute-start | bytes 294920 | tf_op jit(solution)/shard_map/ppermute | solution.py:22
  68.9 7.2 %collective-permute-start.8 = (f32[3,1,64,128]{3,2,1,0:T(8,128)S(1)}, f32[3,1,64,128]{3,2,1,0:T(8,128)S(1)}, u32[]{:S(2)}, u32[]{:S(2)}) collective-permute-start(f32[3,1,64,128]{3,2,1,0:T(8,128)S(1)} %get-tuple-element.36), channel_id=1, source_target_pairs={{0,16},{16,32},{32,48},{48,64},{64,80},{80,96},{96,112},{112,128},... | collective-permute-start | bytes 294920 | tf_op jit(solution)/shard_map/ppermute | solution.py:21
  76.2 6.5 %collective-permute-start.11 = (f32[3,18,1,128]{3,2,1,0:T(1,128)S(1)}, f32[3,18,1,128]{3,2,1,0:T(1,128)S(1)}, u32[]{:S(2)}, u32[]{:S(2)}) collective-permute-start(f32[3,18,1,128]{3,2,1,0:T(1,128)S(1)} %get-tuple-element.17), channel_id=1, source_target_pairs={{1,0},{2,1},{3,2},{4,3},{5,4},{6,5},{7,6},{8,7},{9,8},{10,9},{11,1... | collective-permute-start | bytes 82952 | tf_op jit(solution)/shard_map/ppermute | solution.py:22
  81.7 1.2 collective-permute-start.10
  90.7 3.5 %collective-permute-start.13 = (f32[3,1,64,128]{3,2,1,0:T(8,128)S(1)}, f32[3,1,64,128]{3,2,1,0:T(8,128)S(1)}, u32[]{:S(2)}, u32[]{:S(2)}) collective-permute-start(f32[3,1,64,128]{3,2,1,0:T(8,128)S(1)} %get-tuple-element.35), channel_id=1, source_target_pairs={{16,0},{32,16},{48,32},{64,48},{80,64},{96,80},{112,96},{128,112},... | collective-permute-start | bytes 294920 | tf_op jit(solution)/shard_map/ppermute | solution.py:22
  90.8 7.4 %collective-permute-start.12 = (f32[3,1,64,128]{3,2,1,0:T(8,128)S(1)}, f32[3,1,64,128]{3,2,1,0:T(8,128)S(1)}, u32[]{:S(2)}, u32[]{:S(2)}) collective-permute-start(f32[3,1,64,128]{3,2,1,0:T(8,128)S(1)} %get-tuple-element.34), channel_id=1, source_target_pairs={{0,16},{16,32},{32,48},{48,64},{64,80},{80,96},{96,112},{112,128},... | collective-permute-start | bytes 294920 | tf_op jit(solution)/shard_map/ppermute | solution.py:21
  98.2 6.5 %collective-permute-start.15 = (f32[3,18,1,128]{3,2,1,0:T(1,128)S(1)}, f32[3,18,1,128]{3,2,1,0:T(1,128)S(1)}, u32[]{:S(2)}, u32[]{:S(2)}) collective-permute-start(f32[3,18,1,128]{3,2,1,0:T(1,128)S(1)} %get-tuple-element.13), channel_id=1, source_target_pairs={{1,0},{2,1},{3,2},{4,3},{5,4},{6,5},{7,6},{8,7},{9,8},{10,9},{11,1... | collective-permute-start | bytes 82952 | tf_op jit(solution)/shard_map/ppermute | solution.py:22
  103.7 1.2 collective-permute-start.14
  112.9 23.3 %copy-start.22 = (bf16[3,16,64,128]{3,2,1,0:T(8,128)(2,1)}, bf16[3,16,64,128]{3,2,1,0:T(8,128)(2,1)S(1)}, u32[]{:S(2)}) copy-start(bf16[3,16,64,128]{3,2,1,0:T(8,128)(2,1)S(1)} %fusion.4) | copy-start | bytes 2359300
  (37 other events, 185.3 us)

commit v4 on v3

--- a/solution.py
+++ b/solution.py
@@ -143,9 +143,14 @@
 def body(direct_modes, adjoint_modes, stencil_taps, coupling):
     state = direct_modes.astype(jnp.float32)
     modes = state.shape[3] // 2
+    width_x = state.shape[1]
+    state = with_halo(state, (("gx", 1),), STEPS)
+    fields = with_halo(jnp.concatenate([stencil_taps, coupling], axis=0), (("gx", 1),), STEPS - 1)
+    taps, mix = fields[: stencil_taps.shape[0]], fields[stencil_taps.shape[0] :]
     for step in range(STEPS):
-        padded = with_halo(state, (("gx", 1), ("gz", 2)), 1)
-        state = advance(padded, stencil_taps, coupling)
+        padded = with_halo(state, (("gz", 2),), 1)
+        rows = slice(step, step + width_x + 2 * (STEPS - 1 - step))
+        state = advance(padded, taps[:, rows], mix[:, rows])
     evolved = state.astype(jnp.bfloat16)
     lanes_all = 2 * modes
     square = lax.dot_general(

time: 137 us -> 197 us (1.44)
  other arithmetic: 54.4 us -> 124 us
  waiting for transfers between devices: 13.7 us -> 1.37 us
  starting transfers between devices: 37.3 us -> 25.1 us
  local copies, waits for them, and re-layouts: 8.13 us -> 19.7 us
  Pallas kernels: 20.6 us -> 22.8 us
    select_n x2 -> x8, other arithmetic: 8.11 us -> 43.8 us  [lane_weight(): return jnp.where(lower, first[:, :, None], second[:, :, None])]
    add x3, other arithmetic: 19.4 us -> 47.4 us  [advance(): return own + total + jnp.stack(mixed, axis=0)]
    ppermute x8 -> x6, waiting for transfers between devices: 13.4 us -> 1.35 us  [with_halo(): before = lax.ppermute(last, axis, up)]
    ppermute x8 -> x6, starting transfers between devices: 33.2 us -> 22.1 us  [with_halo(): after = lax.ppermute(leading, axis, down)]
    add x8, other arithmetic: 13.4 us -> 20.8 us  [advance(): term = term + weight * own[other_at]]
    unnamed x106 -> x171, local copies, waits for them, and re-layouts: 2.43 us -> 7.07 us
    slice x4, local copies, waits for them, and re-layouts: 2.52 us -> 5.27 us  [advance(): padded[:, :, :, half:]]
    broadcast_in_dim x3 -> x12, local copies, waits for them, and re-layouts: 0.05 us -> 2.32 us  [lane_weight(): return jnp.where(lower, first[:, :, None], second[:, :, None])]
  transfers between devices with their start and end apart: 16 -> 12, of which waited for: 8 -> 1; matrix products, arithmetic and copies ran while one was open for 17% -> 36% of each run, Pallas kernels for 0% -> 0%
where the time goes in v4:
time: 197 us; the launch traced here: 196 us
  other arithmetic  124 us (63%)
  starting transfers between devices  25.1 us (13%)
  Pallas kernels  22.8 us (12%)
  local copies, waits for them, and re-layouts  19.7 us (10%)
    add x3, other arithmetic, advance(): return own + total + jnp.stack(mixed, axis=0)  47.4 us
    select_n x8, other arithmetic, lane_weight(): return jnp.where(lower, first[:, :, None], second[:, :, None])  43.8 us
    pallas_call x1, Pallas kernels, allsum(): pl.pallas_call(functools.partial(allsum_kernel, nx, nz), out_shape=jax.Sh...  22.8 us
    ppermute x6, starting transfers between devices, with_halo(): after = lax.ppermute(leading, axis, down)  22.1 us
    add x8, other arithmetic, advance(): term = term + weight * own[other_at]  20.8 us
    unnamed x171, local copies, waits for them, and re-layouts  7.07 us
    convert_element_type x1, other arithmetic, body(): evolved = state.astype(jnp.bfloat16)  6.93 us
    slice x4, local copies, waits for them, and re-layouts, advance(): padded[:, :, :, half:]  5.27 us
  transfers between devices with their start and end apart: 12, of which 1 were waited for; matrix products, arithmetic and copies ran while one was open for 36% of the time, Pallas kernels for 0%

profile of v4, /device:TPU:1, one launch (start us, length us, event | category | flops | bytes accessed | tf_op | source)
XLA Modules:
  0.0 195.5 jit_solution(10494600153442767855)
XLA Ops:
  0.7 2.0 %fusion.166 = (f32[3,4,64,128]{3,2,1,0:T(8,128)S(1)}, f32[3,4,64,128]{3,2,1,0:T(8,128)}) fusion(bf16[3,16,64,128]{3,2,1,0:T(8,128)(2,1)} %param.4), kind=kLoop, calls=%fused_computation.586 | loop fusion | bytes 1572864 | tf_op jit(solution)/shard_map/slice | solution.py:19
  2.7 8.9 %collective-permute-start.1 = (f32[3,4,64,128]{3,2,1,0:T(8,128)}, f32[3,4,64,128]{3,2,1,0:T(8,128)S(1)}, u32[]{:S(2)}, u32[]{:S(2)}) collective-permute-start(f32[3,4,64,128]{3,2,1,0:T(8,128)} %get-tuple-element.29), channel_id=1, source_target_pairs={{16,0},{32,16},{48,32},{64,48},{80,64},{96,80},{112,96},{128,112},... | collective-permute-start | bytes 1179656 | tf_op jit(solution)/shard_map/ppermute | solution.py:22
  14.0 5.1 %collective-permute-start.3 = (f32[54,3,64]{2,1,0:T(4,128)}, f32[54,3,64]{2,1,0:T(4,128)}, u32[]{:S(2)}, u32[]{:S(2)}) collective-permute-start(f32[54,3,64]{2,1,0:T(4,128)} %get-tuple-element.192), channel_id=1, source_target_pairs={{16,0},{32,16},{48,32},{64,48},{80,64},{96,80},{112,96},{128,112},... | collective-permute-start | bytes 124424 | tf_op jit(solution)/shard_map/ppermute | solution.py:22
  19.2 4.1 %broadcast_select_fusion.62 = (f32[16,64,128]{2,1,0:T(8,128)}, f32[16,64,128]{2,1,0:T(8,128)}, f32[16,64,128]{2,1,0:T(8,128)}, f32[16,64,128]{2,1,0:T(8,128)}, f...) fusion(f32[16,64]{1,0:T(8,128)S(1)} %get-tuple-element.208, ...), kind=kLoop, calls=%fused_computation.346 | loop fusion | flops 1179648 | bytes 4792448 | tf_op jit(solution)/shard_map/jit(_where)/select_n | solution.py:28
  23.3 4.1 %broadcast_select_fusion.71 = (f32[16,64,128]{2,1,0:T(8,128)}, f32[16,64,128]{2,1,0:T(8,128)}, f32[16,64,128]{2,1,0:T(8,128)}, f32[16,64,128]{2,1,0:T(8,128)}, f...) fusion(f32[16,64]{1,0:T(8,128)S(1)} %get-tuple-element.212, ...), kind=kLoop, calls=%fused_computation.355 | loop fusion | flops 1179648 | bytes 4792448 | tf_op jit(solution)/shard_map/jit(_where)/select_n | solution.py:28
  28.3 1.2 pad_maximum_fusion.16
  31.1 6.2 %broadcast_select_fusion.8 = (f32[22,64,128]{2,1,0:T(8,128)S(1)}, f32[22,64,128]{2,1,0:T(8,128)}, f32[22,64,128]{2,1,0:T(8,128)}, f32[22,64,128]{2,1,0:T(8,128)}...) fusion(f32[22,64]{1,0:T(8,128)S(1)} %get-tuple-element.173, ...), kind=kLoop, calls=%fused_computation.292 | loop fusion | flops 1622016 | bytes 6589568 | tf_op jit(solution)/shard_map/jit(_where)/select_n | solution.py:28
  37.3 6.0 %broadcast_select_fusion.26 = (f32[20,64,128]{2,1,0:T(8,128)}, f32[20,64,128]{2,1,0:T(8,128)}, f32[20,64,128]{2,1,0:T(8,128)}, f32[20,64,128]{2,1,0:T(8,128)}, f...) fusion(f32[20,64]{1,0:T(8,128)S(1)} %get-tuple-element.119, ...), kind=kLoop, calls=%fused_computation.310 | loop fusion | flops 1474560 | bytes 5990528 | tf_op jit(solution)/shard_map/jit(_where)/select_n | solution.py:28
  43.3 6.0 %broadcast_select_fusion.35 = (f32[20,64,128]{2,1,0:T(8,128)}, f32[20,64,128]{2,1,0:T(8,128)}, f32[20,64,128]{2,1,0:T(8,128)}, f32[20,64,128]{2,1,0:T(8,128)}, f...) fusion(f32[20,64]{1,0:T(8,128)S(1)} %get-tuple-element.102, ...), kind=kLoop, calls=%fused_computation.319 | loop fusion | flops 1474560 | bytes 5990528 | tf_op jit(solution)/shard_map/jit(_where)/select_n | solution.py:28
  49.3 5.7 %broadcast_select_fusion.44 = (f32[18,64,128]{2,1,0:T(8,128)}, f32[18,64,128]{2,1,0:T(8,128)}, f32[18,64,128]{2,1,0:T(8,128)}, f32[18,64,128]{2,1,0:T(8,128)}, f...) fusion(f32[18,64]{1,0:T(8,128)S(1)} %get-tuple-element.31, ...), kind=kLoop, calls=%fused_computation.328 | loop fusion | flops 1327104 | bytes 5391488 | tf_op jit(solution)/shard_map/jit(_where)/select_n | solution.py:28
  55.0 5.6 %broadcast_select_fusion.53 = (f32[18,64,128]{2,1,0:T(8,128)}, f32[18,64,128]{2,1,0:T(8,128)}, f32[18,64,128]{2,1,0:T(8,128)}, f32[18,64,128]{2,1,0:T(8,128)}, f...) fusion(f32[18,64]{1,0:T(8,128)S(1)} %get-tuple-element.319, ...), kind=kLoop, calls=%fused_computation.337 | loop fusion | flops 1327104 | bytes 5391488 | tf_op jit(solution)/shard_map/jit(_where)/select_n | solution.py:28
  60.5 6.2 %broadcast_select_fusion.17 = (f32[22,64,128]{2,1,0:T(8,128)}, f32[22,64,128]{2,1,0:T(8,128)}, f32[22,64,128]{2,1,0:T(8,128)}, f32[22,64,128]{2,1,0:T(8,128)}, f...) fusion(f32[22,64]{1,0:T(8,128)S(1)} %get-tuple-element.156, ...), kind=kLoop, calls=%fused_computation.301 | loop fusion | flops 1622016 | bytes 6589568 | tf_op jit(solution)/shard_map/jit(_where)/select_n | solution.py:28
  66.8 1.6 collective-permute-start.5
  68.4 1.5 collective-permute-start.4
  70.2 3.5 %multiply_add_fusion.2 = (f32[1,22,64,128]{3,2,1,0:T(8,128)}, f32[1,22,64,128]{3,2,1,0:T(8,128)}) fusion(f32[3,24,64,128]{3,2,1,0:T(8,128)S(1)} %pad_maximum_fusion.3, f32[22,64]{1,0:T(8,128)S(1)} %get-tuple-element.150, f32[22,64]{1,0:T(8,128)S(1)} %get-tuple-element.151, f32[22,64]{1,0:T(8,128)S(1)} %get-tuple-element.152, ...), kind=kLoop, calls=%fused_computation.273 | loop fusion | flops 2883584 | bytes 3672192 | tf_op jit(solution)/shard_map/add | solution.py:57
  73.7 2.0 %multiply_add_fusion = f32[1,22,64,128]{3,2,1,0:T(8,128)} fusion(f32[3,24,64,128]{3,2,1,0:T(8,128)S(1)} %pad_maximum_fusion.3, f32[22,64]{1,0:T(8,128)S(1)} %get-tuple-element.138, f32[22,64]{1,0:T(8,128)S(1)} %get-tuple-element.139, f32[22,64]{1,0:T(8,128)S(1)} %get-tuple-element.140, f32[22,64]{1,0:T(8,128)S(1)} %get-tuple-element.141, ...), kind=kLoop, calls=%fused_computation.271 | loop fusion | flops 1441792 | bytes 2917504 | tf_op jit(solution)/shard_map/add | solution.py:57
  76.1 3.2 %fusion.159 = (f32[3,24,66,64]{3,2,1,0:T(8,128)}, f32[3,24,66,64]{3,2,1,0:T(8,128)}) fusion(f32[3,24,66,128]{3,2,1,0:T(8,128)S(1)} %pad_maximum_fusion.1), kind=kLoop, calls=%fused_computation.579 | loop fusion | bytes 4866048 | tf_op jit(solution)/shard_map/slice | solution.py:37
  79.3 2.1 %maximum_maximum_fusion = (f32[3,24,65,128]{3,2,1,0:T(8,128)S(1)}, f32[3,24,65,128]{3,2,1,0:T(8,128)}) fusion(f32[3,4,64,128]{3,2,1,0:T(8,128)S(1)} %collective-permute-done.1, f32[3,16,64,128]{3,2,1,0:T(8,128)S(1)} %convert_element_type.6, f32[3,4,64,128]{3,2,1,0:T(8,128)S(1)} %collective-permute-done, f32[3,24,1,128]{3,2,1,0:T(1,128)S(1)} %collective-permute-done.4, ...), kind=kLoop, calls=%fused_computation.12 | loop fusion | flops 3594240 | bytes 7225344 | tf_op jit(solution)/shard_map/concatenate | solution.py:23
  81.4 27.2 %fusion.3 = f32[3,22,64,128]{3,2,1,0:T(8,128)S(1)} fusion(f32[3,24,66,64]{3,2,1,0:T(8,128)} %get-tuple-element.3, f32[3,24,66,64]{3,2,1,0:T(8,128)} %get-tuple-element.2, f32[3,24,65,128]{3,2,1,0:T(8,128)} %get-tuple-element.9, f32[3,24,64,128]{3,2,1,0:T(8,128)S(1)} %pad_maximum_fusion.3, f32[3,24,65,128]{3,2,1,0:T(8,128)S(1)} %get-tuple-element.8, ...), kind=kLoop, calls=%fused_computation.30 | loop fusion | flops 25952256 | bytes 39198720 | tf_op jit(solution)/shard_map/add | solution.py:59
  109.0 1.6 collective-permute-start.6
  110.7 3.5 %multiply_add_fusion.5 = (f32[1,20,64,128]{3,2,1,0:T(8,128)}, f32[1,20,64,128]{3,2,1,0:T(8,128)}) fusion(f32[3,22,64,128]{3,2,1,0:T(8,128)S(1)} %fusion.3, f32[20,64]{1,0:T(8,128)S(1)} %copy-done.61, f32[20,64]{1,0:T(8,128)S(1)} %copy-done.62, f32[20,64]{1,0:T(8,128)S(1)} %copy-done.63, f32[20,64]{1,0:T(8,128)S(1)} %copy-done.64, ...), kind=kLoop, calls=%fused_computation.277 | loop fusion | flops 2621440 | bytes 3338368 | tf_op jit(solution)/shard_map/add | solution.py:57
  114.3 1.9 multiply_add_fusion.4
  119.9 10.2 %fusion.48 = f32[3,20,64,128]{3,2,1,0:T(8,128)S(1)} fusion(f32[3,22,64,128]{3,2,1,0:T(8,128)S(1)} %fusion.3, f32[3,22,1,128]{3,2,1,0:T(1,128)S(1)} %collective-permute-done.7, f32[3,22,1,128]{3,2,1,0:T(1,128)S(1)} %collective-permute-done.6, f32[3,22,66,64]{3,2,1,0:T(8,128)S(1)} %get-tuple-element.5, f32[3,22,66,64]{3,2,1,0:T(8,128)S(1)} %get-tuple-element.4, ...), kind=kLoop, calls=%fused_computation.102 | loop fusion | flops 26542080 | bytes 28723200 | tf_op jit(solution)/shard_map/add | solution.py:59
  130.2 2.4 %collective-permute-start.9 = (f32[3,20,1,128]{3,2,1,0:T(1,128)S(1)}, f32[3,20,1,128]{3,2,1,0:T(1,128)S(1)}, u32[]{:S(2)}, u32[]{:S(2)}) collective-permute-start(f32[3,20,1,128]{3,2,1,0:T(1,128)S(1)} %get-tuple-element.23), channel_id=1, source_target_pairs={{1,0},{2,1},{3,2},{4,3},{5,4},{6,5},{7,6},{8,7},{9,8},{10,9},{11,1... | collective-permute-start | bytes 92168 | tf_op jit(solution)/shard_map/ppermute | solution.py:22
  132.7 4.6 %multiply_add_fusion.8 = (f32[1,18,64,128]{3,2,1,0:T(8,128)}, f32[1,18,64,128]{3,2,1,0:T(8,128)}) fusion(f32[3,20,64,128]{3,2,1,0:T(8,128)S(1)} %fusion.48, f32[18,64]{1,0:T(8,128)S(1)} %copy-done.47, f32[18,64]{1,0:T(8,128)S(1)} %copy-done.48, f32[18,64]{1,0:T(8,128)} %get-tuple-element.64, f32[18,64]{1,0:T(8,128)} %get-tuple-element.65, ...), kind=kLoop, calls=%fused_computation.280 | loop fusion | flops 2359296 | bytes 3004544 | tf_op jit(solution)/shard_map/add | solution.py:57
  137.4 2.2 %multiply_add_fusion.7 = f32[1,18,64,128]{3,2,1,0:T(8,128)} fusion(f32[3,20,64,128]{3,2,1,0:T(8,128)S(1)} %fusion.48, f32[18,64]{1,0:T(8,128)S(1)} %get-tuple-element.56, f32[18,64]{1,0:T(8,128)S(1)} %copy-done.36, f32[18,64]{1,0:T(8,128)S(1)} %copy-done.37, f32[18,64]{1,0:T(8,128)S(1)} %copy-done.38, f32[18,64]{1,0:T(8,128)S(1)} %copy-done.39, ...), kind=kLoop, calls=%fused_computation.279 | loop fusion | flops 1179648 | bytes 2387072 | tf_op jit(solution)/shard_map/add | solution.py:57
  140.7 10.0 %fusion.90 = f32[3,18,64,128]{3,2,1,0:T(8,128)S(1)} fusion(f32[3,20,64,128]{3,2,1,0:T(8,128)S(1)} %fusion.48, f32[3,20,1,128]{3,2,1,0:T(1,128)S(1)} %collective-permute-done.9, f32[3,20,1,128]{3,2,1,0:T(1,128)S(1)} %collective-permute-done.8, f32[3,20,66,64]{3,2,1,0:T(8,128)S(1)} %get-tuple-element.13, f32[3,20,66,64]{3,2,1,0:T(8,128)S(1)} %get-tuple-element.12, ...), kind=kLoop, calls=%fused_computation.163 | loop fusion | flops 23887872 | bytes 25915392 | tf_op jit(solution)/shard_map/add | solution.py:59
  150.9 3.9 %collective-permute-start.11 = (f32[3,18,1,128]{3,2,1,0:T(1,128)S(1)}, f32[3,18,1,128]{3,2,1,0:T(1,128)S(1)}, u32[]{:S(2)}, u32[]{:S(2)}) collective-permute-start(f32[3,18,1,128]{3,2,1,0:T(1,128)S(1)} %get-tuple-element.27), channel_id=1, source_target_pairs={{1,0},{2,1},{3,2},{4,3},{5,4},{6,5},{7,6},{8,7},{9,8},{10,9},{11,1... | collective-permute-start | bytes 82952 | tf_op jit(solution)/shard_map/ppermute | solution.py:22
  154.9 2.0 %multiply_add_fusion.11 = (f32[1,16,64,128]{3,2,1,0:T(8,128)S(1)}, f32[1,16,64,128]{3,2,1,0:T(8,128)S(1)}) fusion(f32[3,18,64,128]{3,2,1,0:T(8,128)S(1)} %fusion.90, f32[16,64]{1,0:T(8,128)S(1)} %copy-done.78, f32[16,64]{1,0:T(8,128)S(1)} %copy-done.79, f32[16,64]{1,0:T(8,128)S(1)} %copy-done.80, f32[16,64]{1,0:T(8,128)S(1)} %copy-done.81, ...), kind=kLoop, calls=%fused_computation.283 | loop fusion | flops 2097152 | bytes 2670720 | tf_op jit(solution)/shard_map/add | solution.py:57
  158.0 1.3 collective-permute-done.10
  163.1 6.9 %fusion.158 = bf16[3,16,64,128]{3,2,1,0:T(8,128)(2,1)S(1)} fusion(f32[1,16,64,128]{3,2,1,0:T(8,128)S(1)} %get-tuple-element.25, f32[1,16,64,128]{3,2,1,0:T(8,128)S(1)} %multiply_add_fusion.10, f32[1,16,64,128]{3,2,1,0:T(8,128)S(1)} %get-tuple-element.24, f32[3,18,66,64]{3,2,1,0:T(8,128)S(1)} %get-tuple-element.19, ...), kind=kLoop, calls=%fused_computation.269 | loop fusion | flops 21626880 | bytes 22321152 | tf_op jit(solution)/shard_map/convert_element_type | solution.py:154
  171.3 22.8 %shard_map.59 = f32[16,256]{1,0:T(8,128)} custom-call(f32[16,256]{1,0:T(8,128)} %reshape.413.part_ref), custom_call_target="tpu_custom_call" | custom-call | tf_op jit(solution)/shard_map/pallas_call | solution.py:125
  (222 shorter events, 18.2 us)
Async XLA Ops:
  0.6 169.4 %copy-start = (bf16[3,16,64,128]{3,2,1,0:T(8,128)(2,1)S(1)}, bf16[3,16,64,128]{3,2,1,0:T(8,128)(2,1)}, u32[]{:S(2)}) copy-start(bf16[3,16,64,128]{3,2,1,0:T(8,128)(2,1)} %param.5) | copy-start | bytes 2359300
  0.6 18.5 %copy-start.33 = (f32[36,16,64]{2,1,0:T(8,128)S(1)}, f32[36,16,64]{2,1,0:T(8,128)}, u32[]{:S(2)}) copy-start(f32[36,16,64]{2,1,0:T(8,128)} %param.6) | copy-start | bytes 442372
  2.7 64.1 %collective-permute-start.1 = (f32[3,4,64,128]{3,2,1,0:T(8,128)}, f32[3,4,64,128]{3,2,1,0:T(8,128)S(1)}, u32[]{:S(2)}, u32[]{:S(2)}) collective-permute-start(f32[3,4,64,128]{3,2,1,0:T(8,128)} %get-tuple-element.29), channel_id=1, source_target_pairs={{16,0},{32,16},{48,32},{64,48},{80,64},{96,80},{112,96},{128,112},... | collective-permute-start | bytes 1179656 | tf_op jit(solution)/shard_map/ppermute | solution.py:22
  11.5 55.3 %collective-permute-start = (f32[3,4,64,128]{3,2,1,0:T(8,128)S(1)}, f32[3,4,64,128]{3,2,1,0:T(8,128)S(1)}, u32[]{:S(2)}, u32[]{:S(2)}) collective-permute-start(f32[3,4,64,128]{3,2,1,0:T(8,128)S(1)} %get-tuple-element.28), channel_id=1, source_target_pairs={{0,16},{16,32},{32,48},{48,64},{64,80},{80,96},{96,112},{112,128},... | collective-permute-start | bytes 1179656 | tf_op jit(solution)/shard_map/ppermute | solution.py:21
  14.0 14.2 %collective-permute-start.3 = (f32[54,3,64]{2,1,0:T(4,128)}, f32[54,3,64]{2,1,0:T(4,128)}, u32[]{:S(2)}, u32[]{:S(2)}) collective-permute-start(f32[54,3,64]{2,1,0:T(4,128)} %get-tuple-element.192), channel_id=1, source_target_pairs={{16,0},{32,16},{48,32},{64,48},{80,64},{96,80},{112,96},{128,112},... | collective-permute-start | bytes 124424 | tf_op jit(solution)/shard_map/ppermute | solution.py:22
  19.1 9.2 %collective-permute-start.2 = (f32[54,3,64]{2,1,0:T(4,128)}, f32[54,3,64]{2,1,0:T(4,128)}, u32[]{:S(2)}, u32[]{:S(2)}) collective-permute-start(f32[54,3,64]{2,1,0:T(4,128)} %get-tuple-element.191), channel_id=1, source_target_pairs={{0,16},{16,32},{32,48},{48,64},{64,80},{80,96},{96,112},{112,128},... | collective-permute-start | bytes 124424 | tf_op jit(solution)/shard_map/ppermute | solution.py:21
  66.8 8.8 %collective-permute-start.5 = (f32[3,24,1,128]{3,2,1,0:T(1,128)S(1)}, f32[3,24,1,128]{3,2,1,0:T(1,128)S(1)}, u32[]{:S(2)}, u32[]{:S(2)}) collective-permute-start(f32[3,24,1,128]{3,2,1,0:T(1,128)S(1)} %get-tuple-element.11), channel_id=1, source_target_pairs={{1,0},{2,1},{3,2},{4,3},{5,4},{6,5},{7,6},{8,7},{9,8},{10,9},{11,1... | collective-permute-start | bytes 110600 | tf_op jit(solution)/shard_map/ppermute | solution.py:22
  68.4 7.2 %collective-permute-start.4 = (f32[3,24,1,128]{3,2,1,0:T(1,128)S(1)}, f32[3,24,1,128]{3,2,1,0:T(1,128)S(1)}, u32[]{:S(2)}, u32[]{:S(2)}) collective-permute-start(f32[3,24,1,128]{3,2,1,0:T(1,128)S(1)} %get-tuple-element.10), channel_id=1, source_target_pairs={{0,1},{1,2},{2,3},{3,4},{4,5},{5,6},{6,7},{7,8},{8,9},{9,10},{10,1... | collective-permute-start | bytes 110600 | tf_op jit(solution)/shard_map/ppermute | solution.py:21
  81.3 29.2 %copy-start.55 = (f32[20,64]{1,0:T(8,128)S(1)}, f32[20,64]{1,0:T(8,128)}, u32[]{:S(2)}) copy-start(f32[20,64]{1,0:T(8,128)} %get-tuple-element.84) | copy-start | bytes 15364
  81.3 29.2 %copy-start.56 = (f32[20,64]{1,0:T(8,128)S(1)}, f32[20,64]{1,0:T(8,128)}, u32[]{:S(2)}) copy-start(f32[20,64]{1,0:T(8,128)} %get-tuple-element.85) | copy-start | bytes 15364
  81.3 29.2 %copy-start.57 = (f32[20,64]{1,0:T(8,128)S(1)}, f32[20,64]{1,0:T(8,128)}, u32[]{:S(2)}) copy-start(f32[20,64]{1,0:T(8,128)} %get-tuple-element.86) | copy-start | bytes 15364
  81.3 29.2 %copy-start.58 = (f32[20,64]{1,0:T(8,128)S(1)}, f32[20,64]{1,0:T(8,128)}, u32[]{:S(2)}) copy-start(f32[20,64]{1,0:T(8,128)} %get-tuple-element.87) | copy-start | bytes 15364
  81.3 29.2 %copy-start.59 = (f32[20,64]{1,0:T(8,128)S(1)}, f32[20,64]{1,0:T(8,128)}, u32[]{:S(2)}) copy-start(f32[20,64]{1,0:T(8,128)} %get-tuple-element.88) | copy-start | bytes 15364
  81.3 29.2 %copy-start.60 = (f32[20,64]{1,0:T(8,128)S(1)}, f32[20,64]{1,0:T(8,128)}, u32[]{:S(2)}) copy-start(f32[20,64]{1,0:T(8,128)} %get-tuple-element.89) | copy-start | bytes 15364
  81.4 29.2 %copy-start.61 = (f32[20,64]{1,0:T(8,128)S(1)}, f32[20,64]{1,0:T(8,128)}, u32[]{:S(2)}) copy-start(f32[20,64]{1,0:T(8,128)} %get-tuple-element.96) | copy-start | bytes 15364
  81.4 29.2 %copy-start.62 = (f32[20,64]{1,0:T(8,128)S(1)}, f32[20,64]{1,0:T(8,128)}, u32[]{:S(2)}) copy-start(f32[20,64]{1,0:T(8,128)} %get-tuple-element.97) | copy-start | bytes 15364
  81.4 29.2 %copy-start.63 = (f32[20,64]{1,0:T(8,128)S(1)}, f32[20,64]{1,0:T(8,128)}, u32[]{:S(2)}) copy-start(f32[20,64]{1,0:T(8,128)} %get-tuple-element.98) | copy-start | bytes 15364
  81.4 29.2 %copy-start.64 = (f32[20,64]{1,0:T(8,128)S(1)}, f32[20,64]{1,0:T(8,128)}, u32[]{:S(2)}) copy-start(f32[20,64]{1,0:T(8,128)} %get-tuple-element.99) | copy-start | bytes 15364
  81.4 29.2 %copy-start.65 = (f32[20,64]{1,0:T(8,128)S(1)}, f32[20,64]{1,0:T(8,128)}, u32[]{:S(2)}) copy-start(f32[20,64]{1,0:T(8,128)} %get-tuple-element.100) | copy-start | bytes 15364
  81.4 29.2 %copy-start.66 = (f32[20,64]{1,0:T(8,128)S(1)}, f32[20,64]{1,0:T(8,128)}, u32[]{:S(2)}) copy-start(f32[20,64]{1,0:T(8,128)} %get-tuple-element.101) | copy-start | bytes 15364
  108.7 7.5 %collective-permute-start.7 = (f32[3,22,1,128]{3,2,1,0:T(1,128)S(1)}, f32[3,22,1,128]{3,2,1,0:T(1,128)S(1)}, u32[]{:S(2)}, u32[]{:S(2)}) collective-permute-start(f32[3,22,1,128]{3,2,1,0:T(1,128)S(1)} %get-tuple-element.17), channel_id=1, source_target_pairs={{1,0},{2,1},{3,2},{4,3},{5,4},{6,5},{7,6},{8,7},{9,8},{10,9},{11,1... | collective-permute-start | bytes 101384 | tf_op jit(solution)/shard_map/ppermute | solution.py:22
  109.0 7.2 %collective-permute-start.6 = (f32[3,22,1,128]{3,2,1,0:T(1,128)S(1)}, f32[3,22,1,128]{3,2,1,0:T(1,128)S(1)}, u32[]{:S(2)}, u32[]{:S(2)}) collective-permute-start(f32[3,22,1,128]{3,2,1,0:T(1,128)S(1)} %get-tuple-element.16), channel_id=1, source_target_pairs={{0,1},{1,2},{2,3},{3,4},{4,5},{5,6},{6,7},{7,8},{8,9},{9,10},{10,1... | collective-permute-start | bytes 101384 | tf_op jit(solution)/shard_map/ppermute | solution.py:21
  130.2 9.3 %collective-permute-start.9 = (f32[3,20,1,128]{3,2,1,0:T(1,128)S(1)}, f32[3,20,1,128]{3,2,1,0:T(1,128)S(1)}, u32[]{:S(2)}, u32[]{:S(2)}) collective-permute-start(f32[3,20,1,128]{3,2,1,0:T(1,128)S(1)} %get-tuple-element.23), channel_id=1, source_target_pairs={{1,0},{2,1},{3,2},{4,3},{5,4},{6,5},{7,6},{8,7},{9,8},{10,9},{11,1... | collective-permute-start | bytes 92168 | tf_op jit(solution)/shard_map/ppermute | solution.py:22
  132.6 6.9 %collective-permute-start.8 = (f32[3,20,1,128]{3,2,1,0:T(1,128)S(1)}, f32[3,20,1,128]{3,2,1,0:T(1,128)S(1)}, u32[]{:S(2)}, u32[]{:S(2)}) collective-permute-start(f32[3,20,1,128]{3,2,1,0:T(1,128)S(1)} %get-tuple-element.22), channel_id=1, source_target_pairs={{0,1},{1,2},{2,3},{3,4},{4,5},{5,6},{6,7},{7,8},{8,9},{9,10},{10,1... | collective-permute-start | bytes 92168 | tf_op jit(solution)/shard_map/ppermute | solution.py:21
  140.6 14.2 %copy-start.73 = (f32[16,64]{1,0:T(8,128)S(1)}, f32[16,64]{1,0:T(8,128)}, u32[]{:S(2)}) copy-start(f32[16,64]{1,0:T(8,128)} %get-tuple-element.229) | copy-start | bytes 12292
  140.6 14.2 %copy-start.74 = (f32[16,64]{1,0:T(8,128)S(1)}, f32[16,64]{1,0:T(8,128)}, u32[]{:S(2)}) copy-start(f32[16,64]{1,0:T(8,128)} %get-tuple-element.230) | copy-start | bytes 12292
  140.6 14.2 %copy-start.75 = (f32[16,64]{1,0:T(8,128)S(1)}, f32[16,64]{1,0:T(8,128)}, u32[]{:S(2)}) copy-start(f32[16,64]{1,0:T(8,128)} %get-tuple-element.231) | copy-start | bytes 12292
  140.6 14.2 %copy-start.76 = (f32[16,64]{1,0:T(8,128)S(1)}, f32[16,64]{1,0:T(8,128)}, u32[]{:S(2)}) copy-start(f32[16,64]{1,0:T(8,128)} %get-tuple-element.232) | copy-start | bytes 12292
  140.6 14.2 %copy-start.77 = (f32[16,64]{1,0:T(8,128)S(1)}, f32[16,64]{1,0:T(8,128)}, u32[]{:S(2)}) copy-start(f32[16,64]{1,0:T(8,128)} %get-tuple-element.233) | copy-start | bytes 12292
  150.9 7.1 %collective-permute-start.11 = (f32[3,18,1,128]{3,2,1,0:T(1,128)S(1)}, f32[3,18,1,128]{3,2,1,0:T(1,128)S(1)}, u32[]{:S(2)}, u32[]{:S(2)}) collective-permute-start(f32[3,18,1,128]{3,2,1,0:T(1,128)S(1)} %get-tuple-element.27), channel_id=1, source_target_pairs={{1,0},{2,1},{3,2},{4,3},{5,4},{6,5},{7,6},{8,7},{9,8},{10,9},{11,1... | collective-permute-start | bytes 82952 | tf_op jit(solution)/shard_map/ppermute | solution.py:22
  154.8 4.5 %collective-permute-start.10 = (f32[3,18,1,128]{3,2,1,0:T(1,128)S(1)}, f32[3,18,1,128]{3,2,1,0:T(1,128)S(1)}, u32[]{:S(2)}, u32[]{:S(2)}) collective-permute-start(f32[3,18,1,128]{3,2,1,0:T(1,128)S(1)} %get-tuple-element.26), channel_id=1, source_target_pairs={{0,1},{1,2},{2,3},{3,4},{4,5},{5,6},{6,7},{7,8},{8,9},{9,10},{10,1... | collective-permute-start | bytes 82952 | tf_op jit(solution)/shard_map/ppermute | solution.py:21
  170.0 25.5 %copy-start.34 = (bf16[3,16,64,128]{3,2,1,0:T(8,128)(2,1)}, bf16[3,16,64,128]{3,2,1,0:T(8,128)(2,1)S(1)}, u32[]{:S(2)}) copy-start(bf16[3,16,64,128]{3,2,1,0:T(8,128)(2,1)S(1)} %fusion.158) | copy-start | bytes 2359300
  (65 other events, 389.5 us)

commit v5 on v3

--- a/solution.py
+++ b/solution.py
@@ -140,12 +140,58 @@
     )(part)
 
 
+def step_kernel(padded_ref, weights_ref, out_ref):
+    row = pl.program_id(0)
+    width_z = out_ref.shape[2]
+    half = out_ref.shape[3] // 2
+    for comp_at in range(3):
+        total = None
+        for side_at in range(2):
+            for tap_at in range(9):
+                shift_x = tap_at // 3
+                shift_z = tap_at % 3
+                shifted = padded_ref[comp_at, row + shift_x, pl.ds(shift_z, width_z), :]
+                if side_at == 1:
+                    shifted = pltpu.roll(shifted, half, 1)
+                term = weights_ref[side_at * 9 + tap_at, 0] * shifted
+                total = term if total is None else total + term
+        mixed = None
+        for other_at in range(3):
+            term = weights_ref[18 + comp_at * 3 + other_at, 0] * padded_ref[other_at, row + 1, pl.ds(1, width_z), :]
+            mixed = term if mixed is None else mixed + term
+        own = padded_ref[comp_at, row + 1, pl.ds(1, width_z), :]
+        out_ref[comp_at, 0] = own + total + mixed
+
+
+def advance_kernel(padded, weights):
+    comps, rows, cols, lanes_all = padded.shape
+    width_x, width_z = rows - 2, cols - 2
+    return pl.pallas_call(
+        step_kernel,
+        out_shape=jax.ShapeDtypeStruct((comps, width_x, width_z, lanes_all), jnp.float32),
+        grid=(width_x,),
+        in_specs=[
+            pl.BlockSpec((comps, rows, cols, lanes_all), lambda i: (0, 0, 0, 0)),
+            pl.BlockSpec((weights.shape[0], 1, width_z, lanes_all), lambda i: (0, i, 0, 0)),
+        ],
+        out_specs=pl.BlockSpec((comps, 1, width_z, lanes_all), lambda i: (0, i, 0, 0)),
+    )(padded, weights)
+
+
+def lane_weights(tap_block, mix_block, lanes_all):
+    lower = lax.broadcasted_iota(jnp.int32, (1, 1, lanes_all), 2) < lanes_all // 2
+    taps = [lane_weight(lower, tap_block[k], tap_block[18 + k]) for k in range(18)]
+    mixes = [lane_weight(lower, mix_block[k], mix_block[9 + k]) for k in range(9)]
+    return jnp.stack(taps + mixes, axis=0)
+
+
 def body(direct_modes, adjoint_modes, stencil_taps, coupling):
     state = direct_modes.astype(jnp.float32)
     modes = state.shape[3] // 2
+    weights = lane_weights(stencil_taps, coupling, state.shape[3])
     for step in range(STEPS):
         padded = with_halo(state, (("gx", 1), ("gz", 2)), 1)
-        state = advance(padded, stencil_taps, coupling)
+        state = advance_kernel(padded, weights)
     evolved = state.astype(jnp.bfloat16)
     lanes_all = 2 * modes
     square = lax.dot_general(

time: 137 us -> 194 us (1.42)
  Pallas kernels: 20.6 us -> 84.2 us
  other arithmetic: 54.4 us -> 46.1 us
    pallas_call x0 -> x4, Pallas kernels: none -> 59.9 us  [advance_kernel(): pl.pallas_call(step_kernel, out_shape=jax.ShapeDtypeStruct((comps, width_...]
    add x11 -> x0, other arithmetic: 32.8 us -> none  [the longest x3 19.4 us: advance(): return own + total + jnp.stack(mixed, axis=0)]
    unnamed x0 -> x26, other arithmetic: none -> 29.7 us
    select_n x2 -> x0, other arithmetic: 8.11 us -> none  [lane_weight(): return jnp.where(lower, first[:, :, None], second[:, :, None])]
    ppermute x8, waiting for transfers between devices: 13.4 us -> 7.65 us  [with_halo(): before = lax.ppermute(last, axis, up)]
    concatenate x8 -> x4, other arithmetic: 4.72 us -> 10.2 us  [with_halo(): x = jnp.concatenate([before, x, after], axis=dim)]
    convert_element_type x1, other arithmetic: 6.64 us -> 1.54 us  [body(): evolved = state.astype(jnp.bfloat16)]
    ppermute x8, waiting for transfers between devices: 0.27 us -> 4.94 us  [with_halo(): after = lax.ppermute(leading, axis, down)]
  transfers between devices with their start and end apart: 16 -> 16, of which waited for: 8 -> 10; matrix products, arithmetic and copies ran while one was open for 17% -> 18% of each run, Pallas kernels for 0% -> 0%
where the time goes in v5:
time: 194 us; the launch traced here: 191 us
  Pallas kernels  84.2 us (43%)
  other arithmetic  46.1 us (24%)
  starting transfers between devices  38.7 us (20%)
  waiting for transfers between devices  12.6 us (6%)
  local copies, waits for them, and re-layouts  8.66 us (4%)
    pallas_call x4, Pallas kernels, advance_kernel(): pl.pallas_call(step_kernel, out_shape=jax.ShapeDtypeStruct((comps, width_...  59.9 us
    ppermute x8, starting transfers between devices, with_halo(): after = lax.ppermute(leading, axis, down)  30.4 us
    unnamed x26, other arithmetic  29.7 us
    pallas_call x1, Pallas kernels, allsum(): pl.pallas_call(functools.partial(allsum_kernel, nx, nz), out_shape=jax.Sh...  24.3 us
    concatenate x4, other arithmetic, with_halo(): x = jnp.concatenate([before, x, after], axis=dim)  10.2 us
    ppermute x8, starting transfers between devices, with_halo(): before = lax.ppermute(last, axis, up)  8.25 us
    ppermute x8, waiting for transfers between devices, with_halo(): before = lax.ppermute(last, axis, up)  7.65 us
    ppermute x8, waiting for transfers between devices, with_halo(): after = lax.ppermute(leading, axis, down)  4.94 us
  transfers between devices with their start and end apart: 16, of which 10 were waited for; matrix products, arithmetic and copies ran while one was open for 18% of the time, Pallas kernels for 0%

profile of v5, /device:TPU:1, one launch (start us, length us, event | category | flops | bytes accessed | tf_op | source)
XLA Modules:
  0.0 191.4 jit_solution(11453420098537887094)
XLA Ops:
  1.6 2.5 %collective-permute-start = (f32[3,1,64,128]{3,2,1,0:T(8,128)S(1)}, f32[3,1,64,128]{3,2,1,0:T(8,128)S(1)}, u32[]{:S(2)}, u32[]{:S(2)}) collective-permute-start(f32[3,1,64,128]{3,2,1,0:T(8,128)S(1)} %get-tuple-element.16), channel_id=1, source_target_pairs={{0,16},{16,32},{32,48},{48,64},{64,80},{80,96},{96,112},{112,128},... | collective-permute-start | bytes 294920 | tf_op jit(solution)/shard_map/ppermute | solution.py:21
  4.1 6.5 %collective-permute-start.1 = (f32[3,1,64,128]{3,2,1,0:T(8,128)S(1)}, f32[3,1,64,128]{3,2,1,0:T(8,128)S(1)}, u32[]{:S(2)}, u32[]{:S(2)}) collective-permute-start(f32[3,1,64,128]{3,2,1,0:T(8,128)S(1)} %get-tuple-element.17), channel_id=1, source_target_pairs={{16,0},{32,16},{48,32},{64,48},{80,64},{96,80},{112,96},{128,112},... | collective-permute-start | bytes 294920 | tf_op jit(solution)/shard_map/ppermute | solution.py:22
  13.3 1.1 select_dynamic-update-slice_fusion.26
  14.5 1.1 select_dynamic-update-slice_fusion.25
  26.9 1.1 select_dynamic-update-slice_fusion.14
  30.3 1.2 select_dynamic-update-slice_fusion.11
  31.5 1.2 select_dynamic-update-slice_fusion.10
  35.0 1.2 select_dynamic-update-slice_fusion.7
  39.6 1.2 select_dynamic-update-slice_fusion.3
  40.7 1.2 select_dynamic-update-slice_fusion.2
  43.3 2.2 %collective-permute-start.2 = (f32[3,18,1,128]{3,2,1,0:T(1,128)S(1)}, f32[3,18,1,128]{3,2,1,0:T(1,128)S(1)}, u32[]{:S(2)}, u32[]{:S(2)}) collective-permute-start(f32[3,18,1,128]{3,2,1,0:T(1,128)S(1)} %get-tuple-element.8), channel_id=1, source_target_pairs={{0,1},{1,2},{2,3},{3,4},{4,5},{5,6},{6,7},{7,8},{8,9},{9,10},{10,1... | collective-permute-start | bytes 82952 | tf_op jit(solution)/shard_map/ppermute | solution.py:21
  46.6 2.4 %collective-permute-done.3 = f32[3,18,1,128]{3,2,1,0:T(1,128)S(1)} collective-permute-done((f32[3,18,1,128]{3,2,1,0:T(1,128)S(1)}, f32[3,18,1,128]{3,2,1,0:T(1,128)S(1)}, u32[]{:S(2)}, u32[]{:S(2)}) %collective-permute-start.3) | collective-permute-done | bytes 27680 | tf_op jit(solution)/shard_map/ppermute | solution.py:22
  49.1 1.6 pad_maximum_fusion.padded_ref
  50.6 15.0 %shard_map.59 = f32[3,16,64,128]{3,2,1,0:T(8,128)} custom-call(f32[3,18,66,128]{3,2,1,0:T(8,128)} %pad_maximum_fusion.padded_ref, f32[27,16,64,128]{3,2,1,0:T(8,128)} %select_dynamic-update-slice_fusion.weights_ref), custom_call_target="tpu_custom_call" | custom-call | tf_op jit(solution)/shard_map/pallas_call | solution.py:169
  66.7 5.1 %collective-permute-start.5 = (f32[3,1,64,128]{3,2,1,0:T(8,128)S(1)}, f32[3,1,64,128]{3,2,1,0:T(8,128)S(1)}, u32[]{:S(2)}, u32[]{:S(2)}) collective-permute-start(f32[3,1,64,128]{3,2,1,0:T(8,128)S(1)} %get-tuple-element.15), channel_id=1, source_target_pairs={{16,0},{32,16},{48,32},{64,48},{80,64},{96,80},{112,96},{128,112},... | collective-permute-start | bytes 294920 | tf_op jit(solution)/shard_map/ppermute | solution.py:22
  71.7 2.0 %collective-permute-done.4 = f32[3,1,64,128]{3,2,1,0:T(8,128)S(1)} collective-permute-done((f32[3,1,64,128]{3,2,1,0:T(8,128)S(1)}, f32[3,1,64,128]{3,2,1,0:T(8,128)S(1)}, u32[]{:S(2)}, u32[]{:S(2)}) %collective-permute-start.4) | collective-permute-done | bytes 98336 | tf_op jit(solution)/shard_map/ppermute | solution.py:21
  74.8 1.3 collective-permute-start.6
  77.4 2.0 %collective-permute-done.7 = f32[3,18,1,128]{3,2,1,0:T(1,128)S(1)} collective-permute-done((f32[3,18,1,128]{3,2,1,0:T(1,128)S(1)}, f32[3,18,1,128]{3,2,1,0:T(1,128)S(1)}, u32[]{:S(2)}, u32[]{:S(2)}) %collective-permute-start.7) | collective-permute-done | bytes 27680 | tf_op jit(solution)/shard_map/ppermute | solution.py:22
  79.4 2.9 %pad_maximum_fusion.1.padded_ref = f32[3,18,66,128]{3,2,1,0:T(8,128)} fusion(f32[3,18,1,128]{3,2,1,0:T(1,128)S(1)} %collective-permute-done.7, f32[3,1,64,128]{3,2,1,0:T(8,128)S(1)} %collective-permute-done.5, f32[3,16,64,128]{3,2,1,0:T(8,128)} %shard_map.59, f32[3,1,64,128]{3,2,1,0:T(8,128)S(1)} %collective-permute-done.4, ...), kind=kLoop, calls=%fused_computation.1 | loop fusion | flops 1824768 | bytes 3649536 | tf_op jit(solution)/shard_map/concatenate | solution.py:23
  82.3 15.0 %shard_map.60 = f32[3,16,64,128]{3,2,1,0:T(8,128)} custom-call(f32[3,18,66,128]{3,2,1,0:T(8,128)} %pad_maximum_fusion.1.padded_ref, f32[27,16,64,128]{3,2,1,0:T(8,128)} %select_dynamic-update-slice_fusion.weights_ref), custom_call_target="tpu_custom_call" | custom-call | tf_op jit(solution)/shard_map/pallas_call | solution.py:169
  98.3 5.7 %collective-permute-start.9 = (f32[3,1,64,128]{3,2,1,0:T(8,128)S(1)}, f32[3,1,64,128]{3,2,1,0:T(8,128)S(1)}, u32[]{:S(2)}, u32[]{:S(2)}) collective-permute-start(f32[3,1,64,128]{3,2,1,0:T(8,128)S(1)} %get-tuple-element.13), channel_id=1, source_target_pairs={{16,0},{32,16},{48,32},{64,48},{80,64},{96,80},{112,96},{128,112},... | collective-permute-start | bytes 294920 | tf_op jit(solution)/shard_map/ppermute | solution.py:22
  104.0 1.9 %collective-permute-done.8 = f32[3,1,64,128]{3,2,1,0:T(8,128)S(1)} collective-permute-done((f32[3,1,64,128]{3,2,1,0:T(8,128)S(1)}, f32[3,1,64,128]{3,2,1,0:T(8,128)S(1)}, u32[]{:S(2)}, u32[]{:S(2)}) %collective-permute-start.8) | collective-permute-done | bytes 98336 | tf_op jit(solution)/shard_map/ppermute | solution.py:21
  107.9 2.5 %collective-permute-start.11 = (f32[3,18,1,128]{3,2,1,0:T(1,128)S(1)}, f32[3,18,1,128]{3,2,1,0:T(1,128)S(1)}, u32[]{:S(2)}, u32[]{:S(2)}) collective-permute-start(f32[3,18,1,128]{3,2,1,0:T(1,128)S(1)} %get-tuple-element.5), channel_id=1, source_target_pairs={{1,0},{2,1},{3,2},{4,3},{5,4},{6,5},{7,6},{8,7},{9,8},{10,9},{11,1... | collective-permute-start | bytes 82952 | tf_op jit(solution)/shard_map/ppermute | solution.py:22
  111.3 2.9 %pad_maximum_fusion.2.padded_ref = f32[3,18,66,128]{3,2,1,0:T(8,128)} fusion(f32[3,18,1,128]{3,2,1,0:T(1,128)S(1)} %collective-permute-done.11, f32[3,1,64,128]{3,2,1,0:T(8,128)S(1)} %collective-permute-done.9, f32[3,16,64,128]{3,2,1,0:T(8,128)} %shard_map.60, f32[3,1,64,128]{3,2,1,0:T(8,128)S(1)} %collective-permute-done.8, ...), kind=kLoop, calls=%fused_computation.2 | loop fusion | flops 1824768 | bytes 3649536 | tf_op jit(solution)/shard_map/concatenate | solution.py:23
  114.2 15.0 %shard_map.61 = f32[3,16,64,128]{3,2,1,0:T(8,128)} custom-call(f32[3,18,66,128]{3,2,1,0:T(8,128)} %pad_maximum_fusion.2.padded_ref, f32[27,16,64,128]{3,2,1,0:T(8,128)} %select_dynamic-update-slice_fusion.weights_ref), custom_call_target="tpu_custom_call" | custom-call | tf_op jit(solution)/shard_map/pallas_call | solution.py:169
  130.2 5.5 %collective-permute-start.13 = (f32[3,1,64,128]{3,2,1,0:T(8,128)S(1)}, f32[3,1,64,128]{3,2,1,0:T(8,128)S(1)}, u32[]{:S(2)}, u32[]{:S(2)}) collective-permute-start(f32[3,1,64,128]{3,2,1,0:T(8,128)S(1)} %get-tuple-element.11), channel_id=1, source_target_pairs={{16,0},{32,16},{48,32},{64,48},{80,64},{96,80},{112,96},{128,112},... | collective-permute-start | bytes 294920 | tf_op jit(solution)/shard_map/ppermute | solution.py:22
  135.7 1.9 %collective-permute-done.12 = f32[3,1,64,128]{3,2,1,0:T(8,128)S(1)} collective-permute-done((f32[3,1,64,128]{3,2,1,0:T(8,128)S(1)}, f32[3,1,64,128]{3,2,1,0:T(8,128)S(1)}, u32[]{:S(2)}, u32[]{:S(2)}) %collective-permute-start.12) | collective-permute-done | bytes 98336 | tf_op jit(solution)/shard_map/ppermute | solution.py:21
  139.7 4.5 %collective-permute-start.15 = (f32[3,18,1,128]{3,2,1,0:T(1,128)S(1)}, f32[3,18,1,128]{3,2,1,0:T(1,128)S(1)}, u32[]{:S(2)}, u32[]{:S(2)}) collective-permute-start(f32[3,18,1,128]{3,2,1,0:T(1,128)S(1)} %get-tuple-element.3), channel_id=1, source_target_pairs={{1,0},{2,1},{3,2},{4,3},{5,4},{6,5},{7,6},{8,7},{9,8},{10,9},{11,1... | collective-permute-start | bytes 82952 | tf_op jit(solution)/shard_map/ppermute | solution.py:22
  145.1 2.9 %pad_maximum_fusion.3.padded_ref = f32[3,18,66,128]{3,2,1,0:T(8,128)} fusion(f32[3,18,1,128]{3,2,1,0:T(1,128)S(1)} %collective-permute-done.15, f32[3,1,64,128]{3,2,1,0:T(8,128)S(1)} %collective-permute-done.13, f32[3,16,64,128]{3,2,1,0:T(8,128)} %shard_map.61, f32[3,1,64,128]{3,2,1,0:T(8,128)S(1)} %collective-permute-done.12, ...), kind=kLoop, calls=%fused_computation.3 | loop fusion | flops 1824768 | bytes 3649536 | tf_op jit(solution)/shard_map/concatenate | solution.py:23
  147.9 15.0 %shard_map.62 = f32[3,16,64,128]{3,2,1,0:T(8,128)} custom-call(f32[3,18,66,128]{3,2,1,0:T(8,128)} %pad_maximum_fusion.3.padded_ref, f32[27,16,64,128]{3,2,1,0:T(8,128)} %select_dynamic-update-slice_fusion.weights_ref), custom_call_target="tpu_custom_call" | custom-call | tf_op jit(solution)/shard_map/pallas_call | solution.py:169
  162.9 1.5 convert_element_type.7
  165.7 24.3 %shard_map.63 = f32[16,256]{1,0:T(8,128)} custom-call(f32[16,256]{1,0:T(8,128)} %reshape.152.part_ref), custom_call_target="tpu_custom_call" | custom-call | tf_op jit(solution)/shard_map/pallas_call | solution.py:125
  (62 shorter events, 39.3 us)
Async XLA Ops:
  0.6 163.8 %copy-start = (bf16[3,16,64,128]{3,2,1,0:T(8,128)(2,1)S(1)}, bf16[3,16,64,128]{3,2,1,0:T(8,128)(2,1)}, u32[]{:S(2)}) copy-start(bf16[3,16,64,128]{3,2,1,0:T(8,128)(2,1)} %param.5) | copy-start | bytes 2359300
  0.6 42.4 %copy-start.1 = (bf16[3,16,64,128]{3,2,1,0:T(8,128)(2,1)S(1)}, bf16[3,16,64,128]{3,2,1,0:T(8,128)(2,1)}, u32[]{:S(2)}) copy-start(bf16[3,16,64,128]{3,2,1,0:T(8,128)(2,1)} %param.4) | copy-start | bytes 2359300
  1.6 41.6 %collective-permute-start = (f32[3,1,64,128]{3,2,1,0:T(8,128)S(1)}, f32[3,1,64,128]{3,2,1,0:T(8,128)S(1)}, u32[]{:S(2)}, u32[]{:S(2)}) collective-permute-start(f32[3,1,64,128]{3,2,1,0:T(8,128)S(1)} %get-tuple-element.16), channel_id=1, source_target_pairs={{0,16},{16,32},{32,48},{48,64},{64,80},{80,96},{96,112},{112,128},... | collective-permute-start | bytes 294920 | tf_op jit(solution)/shard_map/ppermute | solution.py:21
  4.1 39.1 %collective-permute-start.1 = (f32[3,1,64,128]{3,2,1,0:T(8,128)S(1)}, f32[3,1,64,128]{3,2,1,0:T(8,128)S(1)}, u32[]{:S(2)}, u32[]{:S(2)}) collective-permute-start(f32[3,1,64,128]{3,2,1,0:T(8,128)S(1)} %get-tuple-element.17), channel_id=1, source_target_pairs={{16,0},{32,16},{48,32},{64,48},{80,64},{96,80},{112,96},{128,112},... | collective-permute-start | bytes 294920 | tf_op jit(solution)/shard_map/ppermute | solution.py:22
  43.3 3.4 %collective-permute-start.2 = (f32[3,18,1,128]{3,2,1,0:T(1,128)S(1)}, f32[3,18,1,128]{3,2,1,0:T(1,128)S(1)}, u32[]{:S(2)}, u32[]{:S(2)}) collective-permute-start(f32[3,18,1,128]{3,2,1,0:T(1,128)S(1)} %get-tuple-element.8), channel_id=1, source_target_pairs={{0,1},{1,2},{2,3},{3,4},{4,5},{5,6},{6,7},{7,8},{8,9},{9,10},{10,1... | collective-permute-start | bytes 82952 | tf_op jit(solution)/shard_map/ppermute | solution.py:21
  45.5 3.6 %collective-permute-start.3 = (f32[3,18,1,128]{3,2,1,0:T(1,128)S(1)}, f32[3,18,1,128]{3,2,1,0:T(1,128)S(1)}, u32[]{:S(2)}, u32[]{:S(2)}) collective-permute-start(f32[3,18,1,128]{3,2,1,0:T(1,128)S(1)} %get-tuple-element.9), channel_id=1, source_target_pairs={{1,0},{2,1},{3,2},{4,3},{5,4},{6,5},{7,6},{8,7},{9,8},{10,9},{11,1... | collective-permute-start | bytes 82952 | tf_op jit(solution)/shard_map/ppermute | solution.py:22
  66.6 7.2 %collective-permute-start.4 = (f32[3,1,64,128]{3,2,1,0:T(8,128)S(1)}, f32[3,1,64,128]{3,2,1,0:T(8,128)S(1)}, u32[]{:S(2)}, u32[]{:S(2)}) collective-permute-start(f32[3,1,64,128]{3,2,1,0:T(8,128)S(1)} %get-tuple-element.14), channel_id=1, source_target_pairs={{0,16},{16,32},{32,48},{48,64},{64,80},{80,96},{96,112},{112,128},... | collective-permute-start | bytes 294920 | tf_op jit(solution)/shard_map/ppermute | solution.py:21
  66.7 7.1 %collective-permute-start.5 = (f32[3,1,64,128]{3,2,1,0:T(8,128)S(1)}, f32[3,1,64,128]{3,2,1,0:T(8,128)S(1)}, u32[]{:S(2)}, u32[]{:S(2)}) collective-permute-start(f32[3,1,64,128]{3,2,1,0:T(8,128)S(1)} %get-tuple-element.15), channel_id=1, source_target_pairs={{16,0},{32,16},{48,32},{64,48},{80,64},{96,80},{112,96},{128,112},... | collective-permute-start | bytes 294920 | tf_op jit(solution)/shard_map/ppermute | solution.py:22
  74.8 2.6 %collective-permute-start.6 = (f32[3,18,1,128]{3,2,1,0:T(1,128)S(1)}, f32[3,18,1,128]{3,2,1,0:T(1,128)S(1)}, u32[]{:S(2)}, u32[]{:S(2)}) collective-permute-start(f32[3,18,1,128]{3,2,1,0:T(1,128)S(1)} %get-tuple-element.6), channel_id=1, source_target_pairs={{0,1},{1,2},{2,3},{3,4},{4,5},{5,6},{6,7},{7,8},{8,9},{9,10},{10,1... | collective-permute-start | bytes 82952 | tf_op jit(solution)/shard_map/ppermute | solution.py:21
  76.1 3.3 %collective-permute-start.7 = (f32[3,18,1,128]{3,2,1,0:T(1,128)S(1)}, f32[3,18,1,128]{3,2,1,0:T(1,128)S(1)}, u32[]{:S(2)}, u32[]{:S(2)}) collective-permute-start(f32[3,18,1,128]{3,2,1,0:T(1,128)S(1)} %get-tuple-element.7), channel_id=1, source_target_pairs={{1,0},{2,1},{3,2},{4,3},{5,4},{6,5},{7,6},{8,7},{9,8},{10,9},{11,1... | collective-permute-start | bytes 82952 | tf_op jit(solution)/shard_map/ppermute | solution.py:22
  98.2 7.7 %collective-permute-start.8 = (f32[3,1,64,128]{3,2,1,0:T(8,128)S(1)}, f32[3,1,64,128]{3,2,1,0:T(8,128)S(1)}, u32[]{:S(2)}, u32[]{:S(2)}) collective-permute-start(f32[3,1,64,128]{3,2,1,0:T(8,128)S(1)} %get-tuple-element.12), channel_id=1, source_target_pairs={{0,16},{16,32},{32,48},{48,64},{64,80},{80,96},{96,112},{112,128},... | collective-permute-start | bytes 294920 | tf_op jit(solution)/shard_map/ppermute | solution.py:21
  98.3 7.6 %collective-permute-start.9 = (f32[3,1,64,128]{3,2,1,0:T(8,128)S(1)}, f32[3,1,64,128]{3,2,1,0:T(8,128)S(1)}, u32[]{:S(2)}, u32[]{:S(2)}) collective-permute-start(f32[3,1,64,128]{3,2,1,0:T(8,128)S(1)} %get-tuple-element.13), channel_id=1, source_target_pairs={{16,0},{32,16},{48,32},{64,48},{80,64},{96,80},{112,96},{128,112},... | collective-permute-start | bytes 294920 | tf_op jit(solution)/shard_map/ppermute | solution.py:22
  107.0 4.1 %collective-permute-start.10 = (f32[3,18,1,128]{3,2,1,0:T(1,128)S(1)}, f32[3,18,1,128]{3,2,1,0:T(1,128)S(1)}, u32[]{:S(2)}, u32[]{:S(2)}) collective-permute-start(f32[3,18,1,128]{3,2,1,0:T(1,128)S(1)} %get-tuple-element.4), channel_id=1, source_target_pairs={{0,1},{1,2},{2,3},{3,4},{4,5},{5,6},{6,7},{7,8},{8,9},{9,10},{10,1... | collective-permute-start | bytes 82952 | tf_op jit(solution)/shard_map/ppermute | solution.py:21
  107.9 3.4 %collective-permute-start.11 = (f32[3,18,1,128]{3,2,1,0:T(1,128)S(1)}, f32[3,18,1,128]{3,2,1,0:T(1,128)S(1)}, u32[]{:S(2)}, u32[]{:S(2)}) collective-permute-start(f32[3,18,1,128]{3,2,1,0:T(1,128)S(1)} %get-tuple-element.5), channel_id=1, source_target_pairs={{1,0},{2,1},{3,2},{4,3},{5,4},{6,5},{7,6},{8,7},{9,8},{10,9},{11,1... | collective-permute-start | bytes 82952 | tf_op jit(solution)/shard_map/ppermute | solution.py:22
  130.1 7.5 %collective-permute-start.12 = (f32[3,1,64,128]{3,2,1,0:T(8,128)S(1)}, f32[3,1,64,128]{3,2,1,0:T(8,128)S(1)}, u32[]{:S(2)}, u32[]{:S(2)}) collective-permute-start(f32[3,1,64,128]{3,2,1,0:T(8,128)S(1)} %get-tuple-element.10), channel_id=1, source_target_pairs={{0,16},{16,32},{32,48},{48,64},{64,80},{80,96},{96,112},{112,128},... | collective-permute-start | bytes 294920 | tf_op jit(solution)/shard_map/ppermute | solution.py:21
  130.2 7.4 %collective-permute-start.13 = (f32[3,1,64,128]{3,2,1,0:T(8,128)S(1)}, f32[3,1,64,128]{3,2,1,0:T(8,128)S(1)}, u32[]{:S(2)}, u32[]{:S(2)}) collective-permute-start(f32[3,1,64,128]{3,2,1,0:T(8,128)S(1)} %get-tuple-element.11), channel_id=1, source_target_pairs={{16,0},{32,16},{48,32},{64,48},{80,64},{96,80},{112,96},{128,112},... | collective-permute-start | bytes 294920 | tf_op jit(solution)/shard_map/ppermute | solution.py:22
  138.7 6.1 %collective-permute-start.14 = (f32[3,18,1,128]{3,2,1,0:T(1,128)S(1)}, f32[3,18,1,128]{3,2,1,0:T(1,128)S(1)}, u32[]{:S(2)}, u32[]{:S(2)}) collective-permute-start(f32[3,18,1,128]{3,2,1,0:T(1,128)S(1)} %get-tuple-element.2), channel_id=1, source_target_pairs={{0,1},{1,2},{2,3},{3,4},{4,5},{5,6},{6,7},{7,8},{8,9},{9,10},{10,1... | collective-permute-start | bytes 82952 | tf_op jit(solution)/shard_map/ppermute | solution.py:21
  139.7 5.3 %collective-permute-start.15 = (f32[3,18,1,128]{3,2,1,0:T(1,128)S(1)}, f32[3,18,1,128]{3,2,1,0:T(1,128)S(1)}, u32[]{:S(2)}, u32[]{:S(2)}) collective-permute-start(f32[3,18,1,128]{3,2,1,0:T(1,128)S(1)} %get-tuple-element.3), channel_id=1, source_target_pairs={{1,0},{2,1},{3,2},{4,3},{5,4},{6,5},{7,6},{8,7},{9,8},{10,9},{11,1... | collective-permute-start | bytes 82952 | tf_op jit(solution)/shard_map/ppermute | solution.py:22
  164.5 27.0 %copy-start.2 = (bf16[3,16,64,128]{3,2,1,0:T(8,128)(2,1)}, bf16[3,16,64,128]{3,2,1,0:T(8,128)(2,1)S(1)}, u32[]{:S(2)}) copy-start(bf16[3,16,64,128]{3,2,1,0:T(8,128)(2,1)S(1)} %convert_element_type.7) | copy-start | bytes 2359300

commit v6 on v3

--- a/solution.py
+++ b/solution.py
@@ -113,8 +113,36 @@
         pl.semaphore_signal(barrier, inc=1, device_id=(lax.rem(a + k, nx), g), device_id_type=MESH)
     pl.semaphore_wait(barrier, (nz - 1) + (nx - 1))
     spanned, sent_z = gather_phase(part_ref, slots_z, send_z, recv_z, g, lambda t: (a, t), nz)
-    mid[...] = spanned
-    total, sent_x = gather_phase(mid, slots_x, send_x, recv_x, a, lambda t: (t, g), nx)
+    for b in range(nx):
+        mid[b] = spanned[b : b + 1]
+    slots_x[a] = mid[a]
+    sent_x = []
+    for k in range(1, nx):
+        target = lax.rem(a + k, nx)
+        copy = pltpu.make_async_remote_copy(
+            src_ref=mid.at[target],
+            dst_ref=slots_x.at[a],
+            send_sem=send_x.at[k],
+            recv_sem=recv_x.at[a],
+            device_id=(target, g),
+            device_id_type=MESH,
+        )
+        copy.start()
+        sent_x.append(copy)
+    for k in range(1, nx):
+        source = lax.rem(a + nx - k, nx)
+        incoming = pltpu.make_async_remote_copy(
+            src_ref=mid.at[source],
+            dst_ref=slots_x.at[source],
+            send_sem=send_x.at[k],
+            recv_sem=recv_x.at[source],
+            device_id=(source, g),
+            device_id_type=MESH,
+        )
+        incoming.wait_recv()
+    total = slots_x[0]
+    for j in range(1, nx):
+        total = total + slots_x[j]
     out_ref[...] = total
     for copy in sent_z + sent_x:
         copy.wait_send()
@@ -122,15 +150,16 @@
 
 def allsum(part, nx, nz):
     shape = part.shape
+    row = (1, shape[1])
     return pl.pallas_call(
         functools.partial(allsum_kernel, nx, nz),
-        out_shape=jax.ShapeDtypeStruct(shape, jnp.float32),
+        out_shape=jax.ShapeDtypeStruct(row, jnp.float32),
         in_specs=[pl.BlockSpec(memory_space=pltpu.VMEM)],
         out_specs=pl.BlockSpec(memory_space=pltpu.VMEM),
         scratch_shapes=[
-            pltpu.VMEM(shape, jnp.float32),
+            pltpu.VMEM((nx,) + row, jnp.float32),
             pltpu.VMEM((nz,) + shape, jnp.float32),
-            pltpu.VMEM((nx,) + shape, jnp.float32),
+            pltpu.VMEM((nx,) + row, jnp.float32),
             pltpu.SemaphoreType.DMA((nz,)),
             pltpu.SemaphoreType.DMA((nz,)),
             pltpu.SemaphoreType.DMA((nx,)),
@@ -158,8 +187,7 @@
     nx, nz = lax.axis_size("gx"), lax.axis_size("gz")
     rows = partial_sum.shape[0] // nx
     dense = partial_sum.reshape(nx, rows * partial_sum.shape[1])
-    total = allsum(dense, nx, nz)
-    reduced = lax.dynamic_slice_in_dim(total, lax.axis_index("gx"), 1, axis=0)
+    reduced = allsum(dense, nx, nz)
     return (evolved, reduced.reshape(rows, partial_sum.shape[1]))
 
 

time: 137 us -> 126 us (0.920)
  other arithmetic: 54.4 us -> 48.6 us
  local copies, waits for them, and re-layouts: 8.13 us -> 5.52 us
  Pallas kernels: 20.6 us -> 18 us
    select_n x2, other arithmetic: 8.11 us -> 5.27 us  [lane_weight(): return jnp.where(lower, first[:, :, None], second[:, :, None])]
    pallas_call x1, Pallas kernels: 20.6 us -> 18 us  [allsum(): pl.pallas_call(functools.partial(allsum_kernel, nx, nz), out_shape=jax.Sh...]
    unnamed x106 -> x8, local copies, waits for them, and re-layouts: 2.43 us -> 0.03 us
    concatenate x8, other arithmetic: 4.72 us -> 2.62 us  [with_halo(): x = jnp.concatenate([before, x, after], axis=dim)]
    add x8, other arithmetic: 13.4 us -> 11.7 us  [advance(): term = term + weight * own[other_at]]
  transfers between devices with their start and end apart: 16 -> 16, of which waited for: 8 -> 8; matrix products, arithmetic and copies ran while one was open for 17% -> 15% of each run, Pallas kernels for 0% -> 0%
where the time goes in v6:
time: 126 us; the launch traced here: 125 us
  other arithmetic  48.6 us (39%)
  starting transfers between devices  37.5 us (30%)
  Pallas kernels  18 us (14%)
  waiting for transfers between devices  14.1 us (11%)
  local copies, waits for them, and re-layouts  5.52 us (4%)
    ppermute x8, starting transfers between devices, with_halo(): after = lax.ppermute(leading, axis, down)  33.3 us
    add x3, other arithmetic, advance(): return own + total + jnp.stack(mixed, axis=0)  19.5 us
    pallas_call x1, Pallas kernels, allsum(): pl.pallas_call(functools.partial(allsum_kernel, nx, nz), out_shape=jax.Sh...  18 us
    ppermute x8, waiting for transfers between devices, with_halo(): before = lax.ppermute(last, axis, up)  13.5 us
    add x8, other arithmetic, advance(): term = term + weight * own[other_at]  11.7 us
    convert_element_type x1, other arithmetic, body(): evolved = state.astype(jnp.bfloat16)  6.65 us
    select_n x2, other arithmetic, lane_weight(): return jnp.where(lower, first[:, :, None], second[:, :, None])  5.27 us
    ppermute x8, starting transfers between devices, with_halo(): before = lax.ppermute(last, axis, up)  4.19 us
  transfers between devices with their start and end apart: 16, of which 8 were waited for; matrix products, arithmetic and copies ran while one was open for 15% of the time, Pallas kernels for 0%

profile of v6, /device:TPU:1, one launch (start us, length us, event | category | flops | bytes accessed | tf_op | source)
XLA Modules:
  0.0 125.3 jit_solution(15868546510685544301)
XLA Ops:
  0.7 0.9 fusion.168
  1.6 8.9 %collective-permute-start.1 = (f32[3,1,64,128]{3,2,1,0:T(8,128)S(1)}, f32[3,1,64,128]{3,2,1,0:T(8,128)S(1)}, u32[]{:S(2)}, u32[]{:S(2)}) collective-permute-start(f32[3,1,64,128]{3,2,1,0:T(8,128)S(1)} %get-tuple-element.41), channel_id=1, source_target_pairs={{16,0},{32,16},{48,32},{64,48},{80,64},{96,80},{112,96},{128,112},... | collective-permute-start | bytes 294920 | tf_op jit(solution)/shard_map/ppermute | solution.py:22
  10.5 1.3 %convert_element_type.6 = f32[3,16,64,128]{3,2,1,0:T(8,128)S(1)} convert(bf16[3,16,64,128]{3,2,1,0:T(8,128)(2,1)} %param.4) | non-fusion elementwise | flops 393216 | bytes 2359296 | tf_op jit(solution)/shard_map/convert_element_type | solution.py:173
  12.0 2.6 %broadcast_select_fusion.8 = (f32[16,64,128]{2,1,0:T(8,128)S(1)}, f32[16,64,128]{2,1,0:T(8,128)S(1)}, f32[16,64,128]{2,1,0:T(8,128)S(1)}, f32[16,64,128]{2,1,0:T...) fusion(f32[16,64]{1,0:T(8,128)S(1)} %get-tuple-element.57, ...), kind=kLoop, calls=%fused_computation.310 | loop fusion | flops 1179648 | bytes 4792448 | tf_op jit(solution)/shard_map/jit(_where)/select_n | solution.py:28
  14.6 2.6 %broadcast_select_fusion.17 = (f32[16,64,128]{2,1,0:T(8,128)S(1)}, f32[16,64,128]{2,1,0:T(8,128)S(1)}, f32[16,64,128]{2,1,0:T(8,128)S(1)}, f32[16,64,128]{2,1,0:...) fusion(f32[16,64]{1,0:T(8,128)S(1)} %get-tuple-element.61, ...), kind=kLoop, calls=%fused_computation.319 | loop fusion | flops 1179648 | bytes 4792448 | tf_op jit(solution)/shard_map/jit(_where)/select_n | solution.py:28
  17.2 2.0 %fusion.138 = (f32[1,16,64,128]{3,2,1,0:T(8,128)S(1)}, f32[1,16,64,128]{3,2,1,0:T(8,128)S(1)}) fusion(f32[3,16,64,128]{3,2,1,0:T(8,128)S(1)} %convert_element_type.6, f32[16,64]{1,0:T(8,128)S(1)} %get-tuple-element.89, f32[16,64]{1,0:T(8,128)S(1)} %get-tuple-element.90, f32[16,64]{1,0:T(8,128)S(1)} %get-tuple-element.91, ...), kind=kLoop, calls=%fused_computation.279 | loop fusion | flops 2097152 | bytes 2670720 | tf_op jit(solution)/shard_map/add | solution.py:57
  19.3 1.0 collective-permute-start.3
  20.3 1.3 %collective-permute-start.2 = (f32[3,18,1,128]{3,2,1,0:T(1,128)S(1)}, f32[3,18,1,128]{3,2,1,0:T(1,128)S(1)}, u32[]{:S(2)}, u32[]{:S(2)}) collective-permute-start(f32[3,18,1,128]{3,2,1,0:T(1,128)S(1)} %get-tuple-element.24), channel_id=1, source_target_pairs={{0,1},{1,2},{2,3},{3,4},{4,5},{5,6},{6,7},{7,8},{8,9},{9,10},{10,1... | collective-permute-start | bytes 82952 | tf_op jit(solution)/shard_map/ppermute | solution.py:21
  21.6 1.0 fusion.154
  24.5 6.5 %fusion.106 = f32[3,16,64,128]{3,2,1,0:T(8,128)S(1)} fusion(f32[3,16,64,128]{3,2,1,0:T(8,128)S(1)} %convert_element_type.6, f32[3,18,66,64]{3,2,1,0:T(8,128)S(1)} %get-tuple-element.9, f32[3,18,66,64]{3,2,1,0:T(8,128)S(1)} %get-tuple-element.8, f32[3,18,65,128]{3,2,1,0:T(8,128)S(1)} %get-tuple-element.23, f32[3,1,64,128]{3,2,1,0:T(8,128)S(1)} %collective-permute-done.1, ...), kind=kLoop, calls=%fused_computation.188 | loop fusion | flops 19660800 | bytes 25614336 | tf_op jit(solution)/shard_map/add | solution.py:59
  31.1 5.8 %collective-permute-start.5 = (f32[3,1,64,128]{3,2,1,0:T(8,128)S(1)}, f32[3,1,64,128]{3,2,1,0:T(8,128)S(1)}, u32[]{:S(2)}, u32[]{:S(2)}) collective-permute-start(f32[3,1,64,128]{3,2,1,0:T(8,128)S(1)} %get-tuple-element.39), channel_id=1, source_target_pairs={{16,0},{32,16},{48,32},{64,48},{80,64},{96,80},{112,96},{128,112},... | collective-permute-start | bytes 294920 | tf_op jit(solution)/shard_map/ppermute | solution.py:22
  36.8 2.0 %fusion.140 = (f32[1,16,64,128]{3,2,1,0:T(8,128)S(1)}, f32[1,16,64,128]{3,2,1,0:T(8,128)S(1)}) fusion(f32[3,16,64,128]{3,2,1,0:T(8,128)S(1)} %fusion.106, f32[16,64]{1,0:T(8,128)S(1)} %get-tuple-element.89, f32[16,64]{1,0:T(8,128)S(1)} %get-tuple-element.90, f32[16,64]{1,0:T(8,128)S(1)} %get-tuple-element.91, f32[16,64]{1,0:T(8,128)S(1)} %get-tuple-element.92, ...), kind=kLoop, calls=%fused_computation.281 | loop fusion | flops 2097152 | bytes 2670720 | tf_op jit(solution)/shard_map/add | solution.py:57
  38.8 5.1 %collective-permute-done.4 = f32[3,1,64,128]{3,2,1,0:T(8,128)S(1)} collective-permute-done((f32[3,1,64,128]{3,2,1,0:T(8,128)S(1)}, f32[3,1,64,128]{3,2,1,0:T(8,128)S(1)}, u32[]{:S(2)}, u32[]{:S(2)}) %collective-permute-start.4) | collective-permute-done | bytes 98336 | tf_op jit(solution)/shard_map/ppermute | solution.py:21
  44.0 6.4 %collective-permute-start.7 = (f32[3,18,1,128]{3,2,1,0:T(1,128)S(1)}, f32[3,18,1,128]{3,2,1,0:T(1,128)S(1)}, u32[]{:S(2)}, u32[]{:S(2)}) collective-permute-start(f32[3,18,1,128]{3,2,1,0:T(1,128)S(1)} %get-tuple-element.21), channel_id=1, source_target_pairs={{1,0},{2,1},{3,2},{4,3},{5,4},{6,5},{7,6},{8,7},{9,8},{10,9},{11,1... | collective-permute-start | bytes 82952 | tf_op jit(solution)/shard_map/ppermute | solution.py:22
  50.4 1.0 fusion.156
  52.9 6.5 %fusion.72 = f32[3,16,64,128]{3,2,1,0:T(8,128)S(1)} fusion(f32[3,16,64,128]{3,2,1,0:T(8,128)S(1)} %fusion.106, f32[3,18,66,64]{3,2,1,0:T(8,128)S(1)} %get-tuple-element.7, f32[3,18,66,64]{3,2,1,0:T(8,128)S(1)} %get-tuple-element.6, f32[3,18,65,128]{3,2,1,0:T(8,128)S(1)} %get-tuple-element.19, f32[3,1,64,128]{3,2,1,0:T(8,128)S(1)} %collective-permute-done.5, ...), kind=kLoop, calls=%fused_computation.131 | loop fusion | flops 19660800 | bytes 25614336 | tf_op jit(solution)/shard_map/add | solution.py:59
  59.5 1.5 %collective-permute-start.8 = (f32[3,1,64,128]{3,2,1,0:T(8,128)S(1)}, f32[3,1,64,128]{3,2,1,0:T(8,128)S(1)}, u32[]{:S(2)}, u32[]{:S(2)}) collective-permute-start(f32[3,1,64,128]{3,2,1,0:T(8,128)S(1)} %get-tuple-element.36), channel_id=1, source_target_pairs={{0,16},{16,32},{32,48},{48,64},{64,80},{80,96},{96,112},{112,128},... | collective-permute-start | bytes 294920 | tf_op jit(solution)/shard_map/ppermute | solution.py:21
  60.9 2.0 %fusion.142 = (f32[1,16,64,128]{3,2,1,0:T(8,128)S(1)}, f32[1,16,64,128]{3,2,1,0:T(8,128)S(1)}) fusion(f32[3,16,64,128]{3,2,1,0:T(8,128)S(1)} %fusion.72, f32[16,64]{1,0:T(8,128)S(1)} %get-tuple-element.89, f32[16,64]{1,0:T(8,128)S(1)} %get-tuple-element.90, f32[16,64]{1,0:T(8,128)S(1)} %get-tuple-element.91, f32[16,64]{1,0:T(8,128)S(1)} %get-tuple-element.92, ...), kind=kLoop, calls=%fused_computation.283 | loop fusion | flops 2097152 | bytes 2670720 | tf_op jit(solution)/shard_map/add | solution.py:57
  62.9 3.7 %collective-permute-done.8 = f32[3,1,64,128]{3,2,1,0:T(8,128)S(1)} collective-permute-done((f32[3,1,64,128]{3,2,1,0:T(8,128)S(1)}, f32[3,1,64,128]{3,2,1,0:T(8,128)S(1)}, u32[]{:S(2)}, u32[]{:S(2)}) %collective-permute-start.8) | collective-permute-done | bytes 98336 | tf_op jit(solution)/shard_map/ppermute | solution.py:21
  66.7 5.5 %collective-permute-start.11 = (f32[3,18,1,128]{3,2,1,0:T(1,128)S(1)}, f32[3,18,1,128]{3,2,1,0:T(1,128)S(1)}, u32[]{:S(2)}, u32[]{:S(2)}) collective-permute-start(f32[3,18,1,128]{3,2,1,0:T(1,128)S(1)} %get-tuple-element.17), channel_id=1, source_target_pairs={{1,0},{2,1},{3,2},{4,3},{5,4},{6,5},{7,6},{8,7},{9,8},{10,9},{11,1... | collective-permute-start | bytes 82952 | tf_op jit(solution)/shard_map/ppermute | solution.py:22
  72.2 1.0 fusion.158
  74.7 6.5 %fusion.38 = f32[3,16,64,128]{3,2,1,0:T(8,128)S(1)} fusion(f32[3,16,64,128]{3,2,1,0:T(8,128)S(1)} %fusion.72, f32[3,18,66,64]{3,2,1,0:T(8,128)S(1)} %get-tuple-element.5, f32[3,18,66,64]{3,2,1,0:T(8,128)S(1)} %get-tuple-element.4, f32[3,18,65,128]{3,2,1,0:T(8,128)S(1)} %get-tuple-element.15, f32[3,1,64,128]{3,2,1,0:T(8,128)S(1)} %collective-permute-done.9, ...), kind=kLoop, calls=%fused_computation.74 | loop fusion | flops 19660800 | bytes 25614336 | tf_op jit(solution)/shard_map/add | solution.py:59
  81.3 1.5 %collective-permute-start.12 = (f32[3,1,64,128]{3,2,1,0:T(8,128)S(1)}, f32[3,1,64,128]{3,2,1,0:T(8,128)S(1)}, u32[]{:S(2)}, u32[]{:S(2)}) collective-permute-start(f32[3,1,64,128]{3,2,1,0:T(8,128)S(1)} %get-tuple-element.34), channel_id=1, source_target_pairs={{0,16},{16,32},{32,48},{48,64},{64,80},{80,96},{96,112},{112,128},... | collective-permute-start | bytes 294920 | tf_op jit(solution)/shard_map/ppermute | solution.py:21
  82.8 2.0 %fusion.144 = (f32[1,16,64,128]{3,2,1,0:T(8,128)S(1)}, f32[1,16,64,128]{3,2,1,0:T(8,128)S(1)}) fusion(f32[3,16,64,128]{3,2,1,0:T(8,128)S(1)} %fusion.38, f32[16,64]{1,0:T(8,128)S(1)} %get-tuple-element.89, f32[16,64]{1,0:T(8,128)S(1)} %get-tuple-element.90, f32[16,64]{1,0:T(8,128)S(1)} %get-tuple-element.91, f32[16,64]{1,0:T(8,128)S(1)} %get-tuple-element.92, ...), kind=kLoop, calls=%fused_computation.285 | loop fusion | flops 2097152 | bytes 2670720 | tf_op jit(solution)/shard_map/add | solution.py:57
  84.8 3.9 %collective-permute-done.12 = f32[3,1,64,128]{3,2,1,0:T(8,128)S(1)} collective-permute-done((f32[3,1,64,128]{3,2,1,0:T(8,128)S(1)}, f32[3,1,64,128]{3,2,1,0:T(8,128)S(1)}, u32[]{:S(2)}, u32[]{:S(2)}) %collective-permute-start.12) | collective-permute-done | bytes 98336 | tf_op jit(solution)/shard_map/ppermute | solution.py:21
  88.7 5.5 %collective-permute-start.15 = (f32[3,18,1,128]{3,2,1,0:T(1,128)S(1)}, f32[3,18,1,128]{3,2,1,0:T(1,128)S(1)}, u32[]{:S(2)}, u32[]{:S(2)}) collective-permute-start(f32[3,18,1,128]{3,2,1,0:T(1,128)S(1)} %get-tuple-element.13), channel_id=1, source_target_pairs={{1,0},{2,1},{3,2},{4,3},{5,4},{6,5},{7,6},{8,7},{9,8},{10,9},{11,1... | collective-permute-start | bytes 82952 | tf_op jit(solution)/shard_map/ppermute | solution.py:22
  94.3 1.0 fusion.160
  96.8 6.7 %fusion.4 = bf16[3,16,64,128]{3,2,1,0:T(8,128)(2,1)S(1)} fusion(f32[3,16,64,128]{3,2,1,0:T(8,128)S(1)} %fusion.38, f32[3,18,66,64]{3,2,1,0:T(8,128)S(1)} %get-tuple-element.3, f32[3,18,66,64]{3,2,1,0:T(8,128)S(1)} %get-tuple-element.2, f32[3,18,65,128]{3,2,1,0:T(8,128)S(1)} %get-tuple-element.11, f32[3,1,64,128]{3,2,1,0:T(8,128)S(1)} %collective-permute-done.13, ...), kind=kLoop, calls=%fused_computation.17 | loop fusion | flops 20054016 | bytes 24827904 | tf_op jit(solution)/shard_map/convert_element_type | solution.py:178
  104.0 0.7 reshape.116.part_ref
  104.7 18.0 %shard_map.59 = f32[1,256]{1,0:T(1,128)} custom-call(f32[16,256]{1,0:T(8,128)} %reshape.116.part_ref), custom_call_target="tpu_custom_call" | custom-call | tf_op jit(solution)/shard_map/pallas_call | solution.py:154
  123.3 1.3 %reduce.3 = f32[256]{0:T(256)S(1)} reduce(f32[1,256]{1,0:T(1,128)} %shard_map.59, f32[]{:T(128)} %broadcast.499), dimensions={0}, to_apply=%pallas_call.3.reduce_sub_computation.3 | reduce | bytes 2052 | tf_op jit(solution)/shard_map/pallas_call | solution.py:154
  124.6 0.7 reshape.117
  (55 shorter events, 8.0 us)
Async XLA Ops:
  0.6 102.8 %copy-start = (bf16[3,16,64,128]{3,2,1,0:T(8,128)(2,1)S(1)}, bf16[3,16,64,128]{3,2,1,0:T(8,128)(2,1)}, u32[]{:S(2)}) copy-start(bf16[3,16,64,128]{3,2,1,0:T(8,128)(2,1)} %param.5) | copy-start | bytes 2359300
  0.6 11.2 %copy-start.2 = (f32[36,16,64]{2,1,0:T(8,128)S(1)}, f32[36,16,64]{2,1,0:T(8,128)}, u32[]{:S(2)}) copy-start(f32[36,16,64]{2,1,0:T(8,128)} %param.6) | copy-start | bytes 442372
  1.6 10.3 %copy-start.3 = (f32[18,16,64]{2,1,0:T(8,128)S(1)}, f32[18,16,64]{2,1,0:T(8,128)}, u32[]{:S(2)}) copy-start(f32[18,16,64]{2,1,0:T(8,128)} %param.7) | copy-start | bytes 221188
  1.6 17.6 %collective-permute-start.1 = (f32[3,1,64,128]{3,2,1,0:T(8,128)S(1)}, f32[3,1,64,128]{3,2,1,0:T(8,128)S(1)}, u32[]{:S(2)}, u32[]{:S(2)}) collective-permute-start(f32[3,1,64,128]{3,2,1,0:T(8,128)S(1)} %get-tuple-element.41), channel_id=1, source_target_pairs={{16,0},{32,16},{48,32},{64,48},{80,64},{96,80},{112,96},{128,112},... | collective-permute-start | bytes 294920 | tf_op jit(solution)/shard_map/ppermute | solution.py:22
  10.5 8.7 %collective-permute-start = (f32[3,1,64,128]{3,2,1,0:T(8,128)S(1)}, f32[3,1,64,128]{3,2,1,0:T(8,128)S(1)}, u32[]{:S(2)}, u32[]{:S(2)}) collective-permute-start(f32[3,1,64,128]{3,2,1,0:T(8,128)S(1)} %get-tuple-element.40), channel_id=1, source_target_pairs={{0,16},{16,32},{32,48},{48,64},{64,80},{80,96},{96,112},{112,128},... | collective-permute-start | bytes 294920 | tf_op jit(solution)/shard_map/ppermute | solution.py:21
  19.3 3.8 %collective-permute-start.3 = (f32[3,18,1,128]{3,2,1,0:T(1,128)S(1)}, f32[3,18,1,128]{3,2,1,0:T(1,128)S(1)}, u32[]{:S(2)}, u32[]{:S(2)}) collective-permute-start(f32[3,18,1,128]{3,2,1,0:T(1,128)S(1)} %get-tuple-element.25), channel_id=1, source_target_pairs={{1,0},{2,1},{3,2},{4,3},{5,4},{6,5},{7,6},{8,7},{9,8},{10,9},{11,1... | collective-permute-start | bytes 82952 | tf_op jit(solution)/shard_map/ppermute | solution.py:22
  20.3 2.9 %collective-permute-start.2 = (f32[3,18,1,128]{3,2,1,0:T(1,128)S(1)}, f32[3,18,1,128]{3,2,1,0:T(1,128)S(1)}, u32[]{:S(2)}, u32[]{:S(2)}) collective-permute-start(f32[3,18,1,128]{3,2,1,0:T(1,128)S(1)} %get-tuple-element.24), channel_id=1, source_target_pairs={{0,1},{1,2},{2,3},{3,4},{4,5},{5,6},{6,7},{7,8},{8,9},{9,10},{10,1... | collective-permute-start | bytes 82952 | tf_op jit(solution)/shard_map/ppermute | solution.py:21
  31.1 7.7 %collective-permute-start.5 = (f32[3,1,64,128]{3,2,1,0:T(8,128)S(1)}, f32[3,1,64,128]{3,2,1,0:T(8,128)S(1)}, u32[]{:S(2)}, u32[]{:S(2)}) collective-permute-start(f32[3,1,64,128]{3,2,1,0:T(8,128)S(1)} %get-tuple-element.39), channel_id=1, source_target_pairs={{16,0},{32,16},{48,32},{64,48},{80,64},{96,80},{112,96},{128,112},... | collective-permute-start | bytes 294920 | tf_op jit(solution)/shard_map/ppermute | solution.py:22
  36.8 7.1 %collective-permute-start.4 = (f32[3,1,64,128]{3,2,1,0:T(8,128)S(1)}, f32[3,1,64,128]{3,2,1,0:T(8,128)S(1)}, u32[]{:S(2)}, u32[]{:S(2)}) collective-permute-start(f32[3,1,64,128]{3,2,1,0:T(8,128)S(1)} %get-tuple-element.38), channel_id=1, source_target_pairs={{0,16},{16,32},{32,48},{48,64},{64,80},{80,96},{96,112},{112,128},... | collective-permute-start | bytes 294920 | tf_op jit(solution)/shard_map/ppermute | solution.py:21
  44.0 7.4 %collective-permute-start.7 = (f32[3,18,1,128]{3,2,1,0:T(1,128)S(1)}, f32[3,18,1,128]{3,2,1,0:T(1,128)S(1)}, u32[]{:S(2)}, u32[]{:S(2)}) collective-permute-start(f32[3,18,1,128]{3,2,1,0:T(1,128)S(1)} %get-tuple-element.21), channel_id=1, source_target_pairs={{1,0},{2,1},{3,2},{4,3},{5,4},{6,5},{7,6},{8,7},{9,8},{10,9},{11,1... | collective-permute-start | bytes 82952 | tf_op jit(solution)/shard_map/ppermute | solution.py:22
  50.3 1.2 collective-permute-start.6
  59.4 3.5 %collective-permute-start.9 = (f32[3,1,64,128]{3,2,1,0:T(8,128)S(1)}, f32[3,1,64,128]{3,2,1,0:T(8,128)S(1)}, u32[]{:S(2)}, u32[]{:S(2)}) collective-permute-start(f32[3,1,64,128]{3,2,1,0:T(8,128)S(1)} %get-tuple-element.37), channel_id=1, source_target_pairs={{16,0},{32,16},{48,32},{64,48},{80,64},{96,80},{112,96},{128,112},... | collective-permute-start | bytes 294920 | tf_op jit(solution)/shard_map/ppermute | solution.py:22
  59.5 7.2 %collective-permute-start.8 = (f32[3,1,64,128]{3,2,1,0:T(8,128)S(1)}, f32[3,1,64,128]{3,2,1,0:T(8,128)S(1)}, u32[]{:S(2)}, u32[]{:S(2)}) collective-permute-start(f32[3,1,64,128]{3,2,1,0:T(8,128)S(1)} %get-tuple-element.36), channel_id=1, source_target_pairs={{0,16},{16,32},{32,48},{48,64},{64,80},{80,96},{96,112},{112,128},... | collective-permute-start | bytes 294920 | tf_op jit(solution)/shard_map/ppermute | solution.py:21
  66.7 6.5 %collective-permute-start.11 = (f32[3,18,1,128]{3,2,1,0:T(1,128)S(1)}, f32[3,18,1,128]{3,2,1,0:T(1,128)S(1)}, u32[]{:S(2)}, u32[]{:S(2)}) collective-permute-start(f32[3,18,1,128]{3,2,1,0:T(1,128)S(1)} %get-tuple-element.17), channel_id=1, source_target_pairs={{1,0},{2,1},{3,2},{4,3},{5,4},{6,5},{7,6},{8,7},{9,8},{10,9},{11,1... | collective-permute-start | bytes 82952 | tf_op jit(solution)/shard_map/ppermute | solution.py:22
  72.2 1.2 collective-permute-start.10
  81.2 3.5 %collective-permute-start.13 = (f32[3,1,64,128]{3,2,1,0:T(8,128)S(1)}, f32[3,1,64,128]{3,2,1,0:T(8,128)S(1)}, u32[]{:S(2)}, u32[]{:S(2)}) collective-permute-start(f32[3,1,64,128]{3,2,1,0:T(8,128)S(1)} %get-tuple-element.35), channel_id=1, source_target_pairs={{16,0},{32,16},{48,32},{64,48},{80,64},{96,80},{112,96},{128,112},... | collective-permute-start | bytes 294920 | tf_op jit(solution)/shard_map/ppermute | solution.py:22
  81.3 7.4 %collective-permute-start.12 = (f32[3,1,64,128]{3,2,1,0:T(8,128)S(1)}, f32[3,1,64,128]{3,2,1,0:T(8,128)S(1)}, u32[]{:S(2)}, u32[]{:S(2)}) collective-permute-start(f32[3,1,64,128]{3,2,1,0:T(8,128)S(1)} %get-tuple-element.34), channel_id=1, source_target_pairs={{0,16},{16,32},{32,48},{48,64},{64,80},{80,96},{96,112},{112,128},... | collective-permute-start | bytes 294920 | tf_op jit(solution)/shard_map/ppermute | solution.py:21
  88.7 6.5 %collective-permute-start.15 = (f32[3,18,1,128]{3,2,1,0:T(1,128)S(1)}, f32[3,18,1,128]{3,2,1,0:T(1,128)S(1)}, u32[]{:S(2)}, u32[]{:S(2)}) collective-permute-start(f32[3,18,1,128]{3,2,1,0:T(1,128)S(1)} %get-tuple-element.13), channel_id=1, source_target_pairs={{1,0},{2,1},{3,2},{4,3},{5,4},{6,5},{7,6},{8,7},{9,8},{10,9},{11,1... | collective-permute-start | bytes 82952 | tf_op jit(solution)/shard_map/ppermute | solution.py:22
  94.3 1.2 collective-permute-start.14
  103.4 21.8 %copy-start.1 = (bf16[3,16,64,128]{3,2,1,0:T(8,128)(2,1)}, bf16[3,16,64,128]{3,2,1,0:T(8,128)(2,1)S(1)}, u32[]{:S(2)}) copy-start(bf16[3,16,64,128]{3,2,1,0:T(8,128)(2,1)S(1)} %fusion.4) | copy-start | bytes 2359300

commit v7 on v6

--- a/solution.py
+++ b/solution.py
@@ -103,7 +103,7 @@
     return total, outgoing
 
 
-def allsum_kernel(nx, nz, part_ref, out_ref, mid, slots_z, slots_x, send_z, recv_z, send_x, recv_x):
+def allsum_kernel(nx, nz, part_ref, out_ref, mid, slots_x, slots_z, send_x, recv_x, send_z, recv_z):
     a = lax.axis_index("gx")
     g = lax.axis_index("gz")
     barrier = pltpu.get_barrier_semaphore()
@@ -112,15 +112,12 @@
     for k in range(1, nx):
         pl.semaphore_signal(barrier, inc=1, device_id=(lax.rem(a + k, nx), g), device_id_type=MESH)
     pl.semaphore_wait(barrier, (nz - 1) + (nx - 1))
-    spanned, sent_z = gather_phase(part_ref, slots_z, send_z, recv_z, g, lambda t: (a, t), nz)
-    for b in range(nx):
-        mid[b] = spanned[b : b + 1]
-    slots_x[a] = mid[a]
+    slots_x[a] = part_ref[a]
     sent_x = []
     for k in range(1, nx):
         target = lax.rem(a + k, nx)
         copy = pltpu.make_async_remote_copy(
-            src_ref=mid.at[target],
+            src_ref=part_ref.at[target],
             dst_ref=slots_x.at[a],
             send_sem=send_x.at[k],
             recv_sem=recv_x.at[a],
@@ -132,7 +129,7 @@
     for k in range(1, nx):
         source = lax.rem(a + nx - k, nx)
         incoming = pltpu.make_async_remote_copy(
-            src_ref=mid.at[source],
+            src_ref=part_ref.at[source],
             dst_ref=slots_x.at[source],
             send_sem=send_x.at[k],
             recv_sem=recv_x.at[source],
@@ -140,30 +137,31 @@
             device_id_type=MESH,
         )
         incoming.wait_recv()
-    total = slots_x[0]
+    spanned = slots_x[0]
     for j in range(1, nx):
-        total = total + slots_x[j]
+        spanned = spanned + slots_x[j]
+    mid[...] = spanned
+    total, sent_z = gather_phase(mid, slots_z, send_z, recv_z, g, lambda t: (a, t), nz)
     out_ref[...] = total
-    for copy in sent_z + sent_x:
+    for copy in sent_x + sent_z:
         copy.wait_send()
 
 
 def allsum(part, nx, nz):
-    shape = part.shape
-    row = (1, shape[1])
+    row = part.shape[1:]
     return pl.pallas_call(
         functools.partial(allsum_kernel, nx, nz),
         out_shape=jax.ShapeDtypeStruct(row, jnp.float32),
         in_specs=[pl.BlockSpec(memory_space=pltpu.VMEM)],
         out_specs=pl.BlockSpec(memory_space=pltpu.VMEM),
         scratch_shapes=[
+            pltpu.VMEM(row, jnp.float32),
             pltpu.VMEM((nx,) + row, jnp.float32),
-            pltpu.VMEM((nz,) + shape, jnp.float32),
-            pltpu.VMEM((nx,) + row, jnp.float32),
+            pltpu.VMEM((nz,) + row, jnp.float32),
+            pltpu.SemaphoreType.DMA((nx,)),
+            pltpu.SemaphoreType.DMA((nx,)),
             pltpu.SemaphoreType.DMA((nz,)),
             pltpu.SemaphoreType.DMA((nz,)),
-            pltpu.SemaphoreType.DMA((nx,)),
-            pltpu.SemaphoreType.DMA((nx,)),
         ],
         compiler_params=pltpu.CompilerParams(collective_id=0, has_side_effects=True),
     )(part)
@@ -186,7 +184,7 @@
     partial_sum = square[:modes, :modes] + square[modes:, modes:]
     nx, nz = lax.axis_size("gx"), lax.axis_size("gz")
     rows = partial_sum.shape[0] // nx
-    dense = partial_sum.reshape(nx, rows * partial_sum.shape[1])
+    dense = partial_sum.reshape(nx, 1, rows * partial_sum.shape[1])
     reduced = allsum(dense, nx, nz)
     return (evolved, reduced.reshape(rows, partial_sum.shape[1]))
 

time: 126 us -> 125 us (level)
  no operation moved by 1% of the time
where the time goes in v7:
time: 125 us
  other arithmetic  48.6 us (39%)
  starting transfers between devices  37.5 us (30%)
  Pallas kernels  18 us (14%)
  waiting for transfers between devices  14.1 us (11%)
  local copies, waits for them, and re-layouts  5.53 us (4%)
    ppermute x8, starting transfers between devices, with_halo(): after = lax.ppermute(leading, axis, down)  33.3 us
    add x3, other arithmetic, advance(): return own + total + jnp.stack(mixed, axis=0)  19.5 us
    pallas_call x1, Pallas kernels, allsum(): pl.pallas_call(functools.partial(allsum_kernel, nx, nz), out_shape=jax.Sh...  18 us
    ppermute x8, waiting for transfers between devices, with_halo(): before = lax.ppermute(last, axis, up)  13.5 us
    add x8, other arithmetic, advance(): term = term + weight * own[other_at]  11.7 us
    convert_element_type x1, other arithmetic, body(): evolved = state.astype(jnp.bfloat16)  6.65 us
    select_n x2, other arithmetic, lane_weight(): return jnp.where(lower, first[:, :, None], second[:, :, None])  5.27 us
    ppermute x8, starting transfers between devices, with_halo(): before = lax.ppermute(last, axis, up)  4.19 us
  transfers between devices with their start and end apart: 16, of which 8 were waited for; matrix products, arithmetic and copies ran while one was open for 15% of the time, Pallas kernels for 0%

profile of v7, /device:TPU:1, one launch (start us, length us, event | category | flops | bytes accessed | tf_op | source)
XLA Modules:
  0.0 125.2 jit_solution(6663368874711705187)
XLA Ops:
  0.7 0.9 fusion.168
  1.6 8.9 %collective-permute-start.1 = (f32[3,1,64,128]{3,2,1,0:T(8,128)S(1)}, f32[3,1,64,128]{3,2,1,0:T(8,128)S(1)}, u32[]{:S(2)}, u32[]{:S(2)}) collective-permute-start(f32[3,1,64,128]{3,2,1,0:T(8,128)S(1)} %get-tuple-element.41), channel_id=1, source_target_pairs={{16,0},{32,16},{48,32},{64,48},{80,64},{96,80},{112,96},{128,112},... | collective-permute-start | bytes 294920 | tf_op jit(solution)/shard_map/ppermute | solution.py:22
  10.5 1.3 %convert_element_type.6 = f32[3,16,64,128]{3,2,1,0:T(8,128)S(1)} convert(bf16[3,16,64,128]{3,2,1,0:T(8,128)(2,1)} %param.4) | non-fusion elementwise | flops 393216 | bytes 2359296 | tf_op jit(solution)/shard_map/convert_element_type | solution.py:171
  12.0 2.6 %broadcast_select_fusion.8 = (f32[16,64,128]{2,1,0:T(8,128)S(1)}, f32[16,64,128]{2,1,0:T(8,128)S(1)}, f32[16,64,128]{2,1,0:T(8,128)S(1)}, f32[16,64,128]{2,1,0:T...) fusion(f32[16,64]{1,0:T(8,128)S(1)} %get-tuple-element.57, ...), kind=kLoop, calls=%fused_computation.310 | loop fusion | flops 1179648 | bytes 4792448 | tf_op jit(solution)/shard_map/jit(_where)/select_n | solution.py:28
  14.6 2.6 %broadcast_select_fusion.17 = (f32[16,64,128]{2,1,0:T(8,128)S(1)}, f32[16,64,128]{2,1,0:T(8,128)S(1)}, f32[16,64,128]{2,1,0:T(8,128)S(1)}, f32[16,64,128]{2,1,0:...) fusion(f32[16,64]{1,0:T(8,128)S(1)} %get-tuple-element.61, ...), kind=kLoop, calls=%fused_computation.319 | loop fusion | flops 1179648 | bytes 4792448 | tf_op jit(solution)/shard_map/jit(_where)/select_n | solution.py:28
  17.2 2.0 %fusion.138 = (f32[1,16,64,128]{3,2,1,0:T(8,128)S(1)}, f32[1,16,64,128]{3,2,1,0:T(8,128)S(1)}) fusion(f32[3,16,64,128]{3,2,1,0:T(8,128)S(1)} %convert_element_type.6, f32[16,64]{1,0:T(8,128)S(1)} %get-tuple-element.89, f32[16,64]{1,0:T(8,128)S(1)} %get-tuple-element.90, f32[16,64]{1,0:T(8,128)S(1)} %get-tuple-element.91, ...), kind=kLoop, calls=%fused_computation.279 | loop fusion | flops 2097152 | bytes 2670720 | tf_op jit(solution)/shard_map/add | solution.py:57
  19.3 1.0 collective-permute-start.3
  20.3 1.3 %collective-permute-start.2 = (f32[3,18,1,128]{3,2,1,0:T(1,128)S(1)}, f32[3,18,1,128]{3,2,1,0:T(1,128)S(1)}, u32[]{:S(2)}, u32[]{:S(2)}) collective-permute-start(f32[3,18,1,128]{3,2,1,0:T(1,128)S(1)} %get-tuple-element.24), channel_id=1, source_target_pairs={{0,1},{1,2},{2,3},{3,4},{4,5},{5,6},{6,7},{7,8},{8,9},{9,10},{10,1... | collective-permute-start | bytes 82952 | tf_op jit(solution)/shard_map/ppermute | solution.py:21
  21.6 1.0 fusion.154
  24.5 6.5 %fusion.106 = f32[3,16,64,128]{3,2,1,0:T(8,128)S(1)} fusion(f32[3,16,64,128]{3,2,1,0:T(8,128)S(1)} %convert_element_type.6, f32[3,18,66,64]{3,2,1,0:T(8,128)S(1)} %get-tuple-element.9, f32[3,18,66,64]{3,2,1,0:T(8,128)S(1)} %get-tuple-element.8, f32[3,18,65,128]{3,2,1,0:T(8,128)S(1)} %get-tuple-element.23, f32[3,1,64,128]{3,2,1,0:T(8,128)S(1)} %collective-permute-done.1, ...), kind=kLoop, calls=%fused_computation.188 | loop fusion | flops 19660800 | bytes 25614336 | tf_op jit(solution)/shard_map/add | solution.py:59
  31.1 5.8 %collective-permute-start.5 = (f32[3,1,64,128]{3,2,1,0:T(8,128)S(1)}, f32[3,1,64,128]{3,2,1,0:T(8,128)S(1)}, u32[]{:S(2)}, u32[]{:S(2)}) collective-permute-start(f32[3,1,64,128]{3,2,1,0:T(8,128)S(1)} %get-tuple-element.39), channel_id=1, source_target_pairs={{16,0},{32,16},{48,32},{64,48},{80,64},{96,80},{112,96},{128,112},... | collective-permute-start | bytes 294920 | tf_op jit(solution)/shard_map/ppermute | solution.py:22
  36.8 2.0 %fusion.140 = (f32[1,16,64,128]{3,2,1,0:T(8,128)S(1)}, f32[1,16,64,128]{3,2,1,0:T(8,128)S(1)}) fusion(f32[3,16,64,128]{3,2,1,0:T(8,128)S(1)} %fusion.106, f32[16,64]{1,0:T(8,128)S(1)} %get-tuple-element.89, f32[16,64]{1,0:T(8,128)S(1)} %get-tuple-element.90, f32[16,64]{1,0:T(8,128)S(1)} %get-tuple-element.91, f32[16,64]{1,0:T(8,128)S(1)} %get-tuple-element.92, ...), kind=kLoop, calls=%fused_computation.281 | loop fusion | flops 2097152 | bytes 2670720 | tf_op jit(solution)/shard_map/add | solution.py:57
  38.8 5.1 %collective-permute-done.4 = f32[3,1,64,128]{3,2,1,0:T(8,128)S(1)} collective-permute-done((f32[3,1,64,128]{3,2,1,0:T(8,128)S(1)}, f32[3,1,64,128]{3,2,1,0:T(8,128)S(1)}, u32[]{:S(2)}, u32[]{:S(2)}) %collective-permute-start.4) | collective-permute-done | bytes 98336 | tf_op jit(solution)/shard_map/ppermute | solution.py:21
  44.0 6.4 %collective-permute-start.7 = (f32[3,18,1,128]{3,2,1,0:T(1,128)S(1)}, f32[3,18,1,128]{3,2,1,0:T(1,128)S(1)}, u32[]{:S(2)}, u32[]{:S(2)}) collective-permute-start(f32[3,18,1,128]{3,2,1,0:T(1,128)S(1)} %get-tuple-element.21), channel_id=1, source_target_pairs={{1,0},{2,1},{3,2},{4,3},{5,4},{6,5},{7,6},{8,7},{9,8},{10,9},{11,1... | collective-permute-start | bytes 82952 | tf_op jit(solution)/shard_map/ppermute | solution.py:22
  50.4 1.0 fusion.156
  52.9 6.5 %fusion.72 = f32[3,16,64,128]{3,2,1,0:T(8,128)S(1)} fusion(f32[3,16,64,128]{3,2,1,0:T(8,128)S(1)} %fusion.106, f32[3,18,66,64]{3,2,1,0:T(8,128)S(1)} %get-tuple-element.7, f32[3,18,66,64]{3,2,1,0:T(8,128)S(1)} %get-tuple-element.6, f32[3,18,65,128]{3,2,1,0:T(8,128)S(1)} %get-tuple-element.19, f32[3,1,64,128]{3,2,1,0:T(8,128)S(1)} %collective-permute-done.5, ...), kind=kLoop, calls=%fused_computation.131 | loop fusion | flops 19660800 | bytes 25614336 | tf_op jit(solution)/shard_map/add | solution.py:59
  59.5 1.5 %collective-permute-start.8 = (f32[3,1,64,128]{3,2,1,0:T(8,128)S(1)}, f32[3,1,64,128]{3,2,1,0:T(8,128)S(1)}, u32[]{:S(2)}, u32[]{:S(2)}) collective-permute-start(f32[3,1,64,128]{3,2,1,0:T(8,128)S(1)} %get-tuple-element.36), channel_id=1, source_target_pairs={{0,16},{16,32},{32,48},{48,64},{64,80},{80,96},{96,112},{112,128},... | collective-permute-start | bytes 294920 | tf_op jit(solution)/shard_map/ppermute | solution.py:21
  60.9 2.0 %fusion.142 = (f32[1,16,64,128]{3,2,1,0:T(8,128)S(1)}, f32[1,16,64,128]{3,2,1,0:T(8,128)S(1)}) fusion(f32[3,16,64,128]{3,2,1,0:T(8,128)S(1)} %fusion.72, f32[16,64]{1,0:T(8,128)S(1)} %get-tuple-element.89, f32[16,64]{1,0:T(8,128)S(1)} %get-tuple-element.90, f32[16,64]{1,0:T(8,128)S(1)} %get-tuple-element.91, f32[16,64]{1,0:T(8,128)S(1)} %get-tuple-element.92, ...), kind=kLoop, calls=%fused_computation.283 | loop fusion | flops 2097152 | bytes 2670720 | tf_op jit(solution)/shard_map/add | solution.py:57
  62.9 3.7 %collective-permute-done.8 = f32[3,1,64,128]{3,2,1,0:T(8,128)S(1)} collective-permute-done((f32[3,1,64,128]{3,2,1,0:T(8,128)S(1)}, f32[3,1,64,128]{3,2,1,0:T(8,128)S(1)}, u32[]{:S(2)}, u32[]{:S(2)}) %collective-permute-start.8) | collective-permute-done | bytes 98336 | tf_op jit(solution)/shard_map/ppermute | solution.py:21
  66.7 5.5 %collective-permute-start.11 = (f32[3,18,1,128]{3,2,1,0:T(1,128)S(1)}, f32[3,18,1,128]{3,2,1,0:T(1,128)S(1)}, u32[]{:S(2)}, u32[]{:S(2)}) collective-permute-start(f32[3,18,1,128]{3,2,1,0:T(1,128)S(1)} %get-tuple-element.17), channel_id=1, source_target_pairs={{1,0},{2,1},{3,2},{4,3},{5,4},{6,5},{7,6},{8,7},{9,8},{10,9},{11,1... | collective-permute-start | bytes 82952 | tf_op jit(solution)/shard_map/ppermute | solution.py:22
  72.2 1.0 fusion.158
  74.7 6.5 %fusion.38 = f32[3,16,64,128]{3,2,1,0:T(8,128)S(1)} fusion(f32[3,16,64,128]{3,2,1,0:T(8,128)S(1)} %fusion.72, f32[3,18,66,64]{3,2,1,0:T(8,128)S(1)} %get-tuple-element.5, f32[3,18,66,64]{3,2,1,0:T(8,128)S(1)} %get-tuple-element.4, f32[3,18,65,128]{3,2,1,0:T(8,128)S(1)} %get-tuple-element.15, f32[3,1,64,128]{3,2,1,0:T(8,128)S(1)} %collective-permute-done.9, ...), kind=kLoop, calls=%fused_computation.74 | loop fusion | flops 19660800 | bytes 25614336 | tf_op jit(solution)/shard_map/add | solution.py:59
  81.3 1.5 %collective-permute-start.12 = (f32[3,1,64,128]{3,2,1,0:T(8,128)S(1)}, f32[3,1,64,128]{3,2,1,0:T(8,128)S(1)}, u32[]{:S(2)}, u32[]{:S(2)}) collective-permute-start(f32[3,1,64,128]{3,2,1,0:T(8,128)S(1)} %get-tuple-element.34), channel_id=1, source_target_pairs={{0,16},{16,32},{32,48},{48,64},{64,80},{80,96},{96,112},{112,128},... | collective-permute-start | bytes 294920 | tf_op jit(solution)/shard_map/ppermute | solution.py:21
  82.8 2.0 %fusion.144 = (f32[1,16,64,128]{3,2,1,0:T(8,128)S(1)}, f32[1,16,64,128]{3,2,1,0:T(8,128)S(1)}) fusion(f32[3,16,64,128]{3,2,1,0:T(8,128)S(1)} %fusion.38, f32[16,64]{1,0:T(8,128)S(1)} %get-tuple-element.89, f32[16,64]{1,0:T(8,128)S(1)} %get-tuple-element.90, f32[16,64]{1,0:T(8,128)S(1)} %get-tuple-element.91, f32[16,64]{1,0:T(8,128)S(1)} %get-tuple-element.92, ...), kind=kLoop, calls=%fused_computation.285 | loop fusion | flops 2097152 | bytes 2670720 | tf_op jit(solution)/shard_map/add | solution.py:57
  84.8 3.9 %collective-permute-done.12 = f32[3,1,64,128]{3,2,1,0:T(8,128)S(1)} collective-permute-done((f32[3,1,64,128]{3,2,1,0:T(8,128)S(1)}, f32[3,1,64,128]{3,2,1,0:T(8,128)S(1)}, u32[]{:S(2)}, u32[]{:S(2)}) %collective-permute-start.12) | collective-permute-done | bytes 98336 | tf_op jit(solution)/shard_map/ppermute | solution.py:21
  88.7 5.5 %collective-permute-start.15 = (f32[3,18,1,128]{3,2,1,0:T(1,128)S(1)}, f32[3,18,1,128]{3,2,1,0:T(1,128)S(1)}, u32[]{:S(2)}, u32[]{:S(2)}) collective-permute-start(f32[3,18,1,128]{3,2,1,0:T(1,128)S(1)} %get-tuple-element.13), channel_id=1, source_target_pairs={{1,0},{2,1},{3,2},{4,3},{5,4},{6,5},{7,6},{8,7},{9,8},{10,9},{11,1... | collective-permute-start | bytes 82952 | tf_op jit(solution)/shard_map/ppermute | solution.py:22
  94.3 1.0 fusion.160
  96.8 6.7 %fusion.4 = bf16[3,16,64,128]{3,2,1,0:T(8,128)(2,1)S(1)} fusion(f32[3,16,64,128]{3,2,1,0:T(8,128)S(1)} %fusion.38, f32[3,18,66,64]{3,2,1,0:T(8,128)S(1)} %get-tuple-element.3, f32[3,18,66,64]{3,2,1,0:T(8,128)S(1)} %get-tuple-element.2, f32[3,18,65,128]{3,2,1,0:T(8,128)S(1)} %get-tuple-element.11, f32[3,1,64,128]{3,2,1,0:T(8,128)S(1)} %collective-permute-done.13, ...), kind=kLoop, calls=%fused_computation.17 | loop fusion | flops 20054016 | bytes 24827904 | tf_op jit(solution)/shard_map/convert_element_type | solution.py:176
  104.0 0.7 reshape.116.part_ref
  104.7 18.0 %shard_map.59 = f32[1,256]{1,0:T(1,128)} custom-call(f32[16,1,256]{2,1,0:T(1,128)} %reshape.116.part_ref), custom_call_target="tpu_custom_call" | custom-call | tf_op jit(solution)/shard_map/pallas_call | solution.py:152
  123.3 1.3 %reduce.3 = f32[256]{0:T(256)S(1)} reduce(f32[1,256]{1,0:T(1,128)} %shard_map.59, f32[]{:T(128)} %broadcast.499), dimensions={0}, to_apply=%pallas_call.3.reduce_sub_computation.3 | reduce | bytes 2052 | tf_op jit(solution)/shard_map/pallas_call | solution.py:152
  124.6 0.7 reshape.117
  (55 shorter events, 8.0 us)
Async XLA Ops:
  0.6 102.8 %copy-start = (bf16[3,16,64,128]{3,2,1,0:T(8,128)(2,1)S(1)}, bf16[3,16,64,128]{3,2,1,0:T(8,128)(2,1)}, u32[]{:S(2)}) copy-start(bf16[3,16,64,128]{3,2,1,0:T(8,128)(2,1)} %param.5) | copy-start | bytes 2359300
  0.6 11.2 %copy-start.2 = (f32[36,16,64]{2,1,0:T(8,128)S(1)}, f32[36,16,64]{2,1,0:T(8,128)}, u32[]{:S(2)}) copy-start(f32[36,16,64]{2,1,0:T(8,128)} %param.6) | copy-start | bytes 442372
  1.6 10.3 %copy-start.3 = (f32[18,16,64]{2,1,0:T(8,128)S(1)}, f32[18,16,64]{2,1,0:T(8,128)}, u32[]{:S(2)}) copy-start(f32[18,16,64]{2,1,0:T(8,128)} %param.7) | copy-start | bytes 221188
  1.6 17.6 %collective-permute-start.1 = (f32[3,1,64,128]{3,2,1,0:T(8,128)S(1)}, f32[3,1,64,128]{3,2,1,0:T(8,128)S(1)}, u32[]{:S(2)}, u32[]{:S(2)}) collective-permute-start(f32[3,1,64,128]{3,2,1,0:T(8,128)S(1)} %get-tuple-element.41), channel_id=1, source_target_pairs={{16,0},{32,16},{48,32},{64,48},{80,64},{96,80},{112,96},{128,112},... | collective-permute-start | bytes 294920 | tf_op jit(solution)/shard_map/ppermute | solution.py:22
  10.5 8.7 %collective-permute-start = (f32[3,1,64,128]{3,2,1,0:T(8,128)S(1)}, f32[3,1,64,128]{3,2,1,0:T(8,128)S(1)}, u32[]{:S(2)}, u32[]{:S(2)}) collective-permute-start(f32[3,1,64,128]{3,2,1,0:T(8,128)S(1)} %get-tuple-element.40), channel_id=1, source_target_pairs={{0,16},{16,32},{32,48},{48,64},{64,80},{80,96},{96,112},{112,128},... | collective-permute-start | bytes 294920 | tf_op jit(solution)/shard_map/ppermute | solution.py:21
  19.3 3.8 %collective-permute-start.3 = (f32[3,18,1,128]{3,2,1,0:T(1,128)S(1)}, f32[3,18,1,128]{3,2,1,0:T(1,128)S(1)}, u32[]{:S(2)}, u32[]{:S(2)}) collective-permute-start(f32[3,18,1,128]{3,2,1,0:T(1,128)S(1)} %get-tuple-element.25), channel_id=1, source_target_pairs={{1,0},{2,1},{3,2},{4,3},{5,4},{6,5},{7,6},{8,7},{9,8},{10,9},{11,1... | collective-permute-start | bytes 82952 | tf_op jit(solution)/shard_map/ppermute | solution.py:22
  20.3 2.9 %collective-permute-start.2 = (f32[3,18,1,128]{3,2,1,0:T(1,128)S(1)}, f32[3,18,1,128]{3,2,1,0:T(1,128)S(1)}, u32[]{:S(2)}, u32[]{:S(2)}) collective-permute-start(f32[3,18,1,128]{3,2,1,0:T(1,128)S(1)} %get-tuple-element.24), channel_id=1, source_target_pairs={{0,1},{1,2},{2,3},{3,4},{4,5},{5,6},{6,7},{7,8},{8,9},{9,10},{10,1... | collective-permute-start | bytes 82952 | tf_op jit(solution)/shard_map/ppermute | solution.py:21
  31.1 7.7 %collective-permute-start.5 = (f32[3,1,64,128]{3,2,1,0:T(8,128)S(1)}, f32[3,1,64,128]{3,2,1,0:T(8,128)S(1)}, u32[]{:S(2)}, u32[]{:S(2)}) collective-permute-start(f32[3,1,64,128]{3,2,1,0:T(8,128)S(1)} %get-tuple-element.39), channel_id=1, source_target_pairs={{16,0},{32,16},{48,32},{64,48},{80,64},{96,80},{112,96},{128,112},... | collective-permute-start | bytes 294920 | tf_op jit(solution)/shard_map/ppermute | solution.py:22
  36.8 7.1 %collective-permute-start.4 = (f32[3,1,64,128]{3,2,1,0:T(8,128)S(1)}, f32[3,1,64,128]{3,2,1,0:T(8,128)S(1)}, u32[]{:S(2)}, u32[]{:S(2)}) collective-permute-start(f32[3,1,64,128]{3,2,1,0:T(8,128)S(1)} %get-tuple-element.38), channel_id=1, source_target_pairs={{0,16},{16,32},{32,48},{48,64},{64,80},{80,96},{96,112},{112,128},... | collective-permute-start | bytes 294920 | tf_op jit(solution)/shard_map/ppermute | solution.py:21
  44.0 7.4 %collective-permute-start.7 = (f32[3,18,1,128]{3,2,1,0:T(1,128)S(1)}, f32[3,18,1,128]{3,2,1,0:T(1,128)S(1)}, u32[]{:S(2)}, u32[]{:S(2)}) collective-permute-start(f32[3,18,1,128]{3,2,1,0:T(1,128)S(1)} %get-tuple-element.21), channel_id=1, source_target_pairs={{1,0},{2,1},{3,2},{4,3},{5,4},{6,5},{7,6},{8,7},{9,8},{10,9},{11,1... | collective-permute-start | bytes 82952 | tf_op jit(solution)/shard_map/ppermute | solution.py:22
  50.3 1.2 collective-permute-start.6
  59.4 3.5 %collective-permute-start.9 = (f32[3,1,64,128]{3,2,1,0:T(8,128)S(1)}, f32[3,1,64,128]{3,2,1,0:T(8,128)S(1)}, u32[]{:S(2)}, u32[]{:S(2)}) collective-permute-start(f32[3,1,64,128]{3,2,1,0:T(8,128)S(1)} %get-tuple-element.37), channel_id=1, source_target_pairs={{16,0},{32,16},{48,32},{64,48},{80,64},{96,80},{112,96},{128,112},... | collective-permute-start | bytes 294920 | tf_op jit(solution)/shard_map/ppermute | solution.py:22
  59.5 7.2 %collective-permute-start.8 = (f32[3,1,64,128]{3,2,1,0:T(8,128)S(1)}, f32[3,1,64,128]{3,2,1,0:T(8,128)S(1)}, u32[]{:S(2)}, u32[]{:S(2)}) collective-permute-start(f32[3,1,64,128]{3,2,1,0:T(8,128)S(1)} %get-tuple-element.36), channel_id=1, source_target_pairs={{0,16},{16,32},{32,48},{48,64},{64,80},{80,96},{96,112},{112,128},... | collective-permute-start | bytes 294920 | tf_op jit(solution)/shard_map/ppermute | solution.py:21
  66.7 6.5 %collective-permute-start.11 = (f32[3,18,1,128]{3,2,1,0:T(1,128)S(1)}, f32[3,18,1,128]{3,2,1,0:T(1,128)S(1)}, u32[]{:S(2)}, u32[]{:S(2)}) collective-permute-start(f32[3,18,1,128]{3,2,1,0:T(1,128)S(1)} %get-tuple-element.17), channel_id=1, source_target_pairs={{1,0},{2,1},{3,2},{4,3},{5,4},{6,5},{7,6},{8,7},{9,8},{10,9},{11,1... | collective-permute-start | bytes 82952 | tf_op jit(solution)/shard_map/ppermute | solution.py:22
  72.2 1.2 collective-permute-start.10
  81.2 3.5 %collective-permute-start.13 = (f32[3,1,64,128]{3,2,1,0:T(8,128)S(1)}, f32[3,1,64,128]{3,2,1,0:T(8,128)S(1)}, u32[]{:S(2)}, u32[]{:S(2)}) collective-permute-start(f32[3,1,64,128]{3,2,1,0:T(8,128)S(1)} %get-tuple-element.35), channel_id=1, source_target_pairs={{16,0},{32,16},{48,32},{64,48},{80,64},{96,80},{112,96},{128,112},... | collective-permute-start | bytes 294920 | tf_op jit(solution)/shard_map/ppermute | solution.py:22
  81.3 7.4 %collective-permute-start.12 = (f32[3,1,64,128]{3,2,1,0:T(8,128)S(1)}, f32[3,1,64,128]{3,2,1,0:T(8,128)S(1)}, u32[]{:S(2)}, u32[]{:S(2)}) collective-permute-start(f32[3,1,64,128]{3,2,1,0:T(8,128)S(1)} %get-tuple-element.34), channel_id=1, source_target_pairs={{0,16},{16,32},{32,48},{48,64},{64,80},{80,96},{96,112},{112,128},... | collective-permute-start | bytes 294920 | tf_op jit(solution)/shard_map/ppermute | solution.py:21
  88.7 6.5 %collective-permute-start.15 = (f32[3,18,1,128]{3,2,1,0:T(1,128)S(1)}, f32[3,18,1,128]{3,2,1,0:T(1,128)S(1)}, u32[]{:S(2)}, u32[]{:S(2)}) collective-permute-start(f32[3,18,1,128]{3,2,1,0:T(1,128)S(1)} %get-tuple-element.13), channel_id=1, source_target_pairs={{1,0},{2,1},{3,2},{4,3},{5,4},{6,5},{7,6},{8,7},{9,8},{10,9},{11,1... | collective-permute-start | bytes 82952 | tf_op jit(solution)/shard_map/ppermute | solution.py:22
  94.3 1.2 collective-permute-start.14
  103.4 21.8 %copy-start.1 = (bf16[3,16,64,128]{3,2,1,0:T(8,128)(2,1)}, bf16[3,16,64,128]{3,2,1,0:T(8,128)(2,1)S(1)}, u32[]{:S(2)}) copy-start(bf16[3,16,64,128]{3,2,1,0:T(8,128)(2,1)S(1)} %fusion.4) | copy-start | bytes 2359300
